TPU v7x, 256 devices: a whole 4x4x8 slice. The times are simulated.
256 devices in a mesh: gx: 16 (over y_lo, z), gy: 16 (over x, y_hi, core).
Axes of the slice: x: 4, y: 4 (y_hi: 2, y_lo: 2; y = y_hi * 2 + y_lo), z: 8, core: 2. Of those that a mesh axis runs over, the one named last changes fastest.
Arguments:
- adjoint: float32 [4, 256, 512, 128], P(None, 'gx', 'gy'), may hold values from -6 to 6
- velocity: bfloat16 [3, 256, 512, 128], P(None, 'gx', 'gy'), may hold values from -3 to 3
- diffusivity: bfloat16 [256, 512, 128], P('gx', 'gy'), may hold values from 0.049804688 to 0.796875
- concentration: bfloat16 [256, 512, 128], P('gx', 'gy'), may hold values from -4 to 4
- heights: int32 [256, 512], P('gx', 'gy'), may hold values from 0 to 32
- receptors: int32 [16, 16, 64], P('gx', 'gy'), may hold values from 0 to 65535
- face_src: int32 [16, 16, 16, 16], P('gx', 'gy'), may hold values from -1 to 511, as said below
- face_dst: int32 [16, 16, 16, 16], P('gx', 'gy'), may hold values from 0 to 511
- face_coef: float32 [16, 16, 16, 16, 128], P('gx', 'gy'), may hold values from 0.2 to 1
Outputs:
- adjoint_out: float32 [4, 256, 512, 128], P(None, 'gx', 'gy')
Inputs may be any that keep to these rules, and one draw needn't show every extreme that they name: `face_src`: -1 marks an empty slot; the slots of one source tile and owner are filled from the front; at most 16 live slots for one source and owner, reached for some owner of every source tile and for one owner from every source.
All inputs are finite; a program needn't handle non-finite values.
Results may differ from a plain program's by a relative error of at most 0.0003.
Values may be sent and summed in bfloat16 or wider, within the bound.
No kernel may reach another device: no remote copies, remote signals or barrier semaphores. Data moves between devices by JAX's collectives and lax.ppermute only.
A program may use at most 64 MiB of HBM per device.

v0:
```python
import jax
import jax.numpy as jnp
from jax import lax
from jax.sharding import PartitionSpec as P

STEPS = 2


TIME_STEP = 0.1


def with_halo(x, sides, width):
    for axis, dim in sides:
        count, length = (lax.axis_size(axis), x.shape[dim])
        up = [(i, (i + 1) % count) for i in range(count - 1)]
        down = [(j, i) for i, j in up]
        last = lax.slice_in_dim(x, length - width, length, axis=dim)
        leading = lax.slice_in_dim(x, 0, width, axis=dim)
        before = lax.ppermute(last, axis, up)
        after = lax.ppermute(leading, axis, down)
        x = jnp.concatenate([before, x, after], axis=dim)
    return x


def shift_up(field):
    return jnp.concatenate([field[..., 1:], jnp.zeros_like(field[..., :1])], axis=-1)


def shift_down(field):
    return jnp.concatenate([jnp.zeros_like(field[..., :1]), field[..., :-1]], axis=-1)


def field_operator(padded, vel_pad, diff_pad):
    center = padded[..., 1:-1, 1:-1, :]
    k_center = diff_pad[1:-1, 1:-1]
    flux = vel_pad[0] * padded
    transport = flux[..., 2:, 1:-1, :] - flux[..., :-2, 1:-1, :]
    flux = vel_pad[1] * padded
    transport = transport + flux[..., 1:-1, 2:, :] - flux[..., 1:-1, :-2, :]
    flux = vel_pad[2, 1:-1, 1:-1] * center
    transport = transport + shift_up(flux) - shift_down(flux)
    spread = (k_center + diff_pad[2:, 1:-1]) * (padded[..., 2:, 1:-1, :] - center) - (
        k_center + diff_pad[:-2, 1:-1]
    ) * (center - padded[..., :-2, 1:-1, :])
    spread = (
        spread
        + (k_center + diff_pad[1:-1, 2:]) * (padded[..., 1:-1, 2:, :] - center)
        - (k_center + diff_pad[1:-1, :-2]) * (center - padded[..., 1:-1, :-2, :])
    )
    spread = (
        spread
        + (k_center + shift_up(k_center)) * (shift_up(center) - center)
        - (k_center + shift_down(k_center)) * (center - shift_down(center))
    )
    return 0.5 * (transport + spread)


def shards(
    adjoint, velocity, diffusivity, concentration, heights, receptors, face_src, face_dst, face_coef
):
    rows_x, rows_y, levels = (adjoint.shape[1], adjoint.shape[2], adjoint.shape[3])
    stacked = jnp.concatenate([velocity, diffusivity[None], concentration[None]], axis=0)
    coef_pad = with_halo(stacked, (("gx", 1), ("gy", 2)), 1).astype(jnp.float32)
    vel_pad = coef_pad[:3]
    diff_pad = coef_pad[3]
    conc_pad = coef_pad[4]
    conc_center = conc_pad[1:-1, 1:-1]
    gradients = jnp.stack(
        [
            0.5 * (conc_pad[2:, 1:-1] - conc_pad[:-2, 1:-1]),
            0.5 * (conc_pad[1:-1, 2:] - conc_pad[1:-1, :-2]),
            0.5 * (shift_up(conc_center) - shift_down(conc_center)),
        ]
    )
    level_ids = jnp.arange(levels, dtype=jnp.int32)
    fluid = (level_ids[None, None, :] >= heights[:, :, None]).astype(jnp.float32)
    live_slots = face_src[0, 0] >= 0
    src_cols = jnp.maximum(face_src[0, 0], 0)
    dst_cols = face_dst[0, 0].reshape(-1)
    face_weight = face_coef[0, 0]
    receptor_cells = receptors.reshape(-1)
    for step in range(STEPS):
        conc_adj = (
            adjoint[3].reshape(-1).at[receptor_cells].add(1.0).reshape(rows_x, rows_y, levels)
        )
        columns = conc_adj.reshape(rows_x * rows_y, levels)
        blocks = jnp.where(live_slots[..., None], face_weight * columns[src_cols], 0.0)
        arrived = lax.all_to_all(blocks, "gx", split_axis=0, concat_axis=0, tiled=True)
        wall_sum = (
            jnp.zeros((rows_x * rows_y, levels), jnp.float32)
            .at[dst_cols]
            .add(arrived.reshape(-1, levels))
        )
        wall_sum = wall_sum.reshape(rows_x, rows_y, levels)
        state = adjoint.at[3].set(conc_adj)
        padded = with_halo(state, (("gx", 1), ("gy", 2)), 1)
        change = field_operator(padded, vel_pad, diff_pad)
        change = jnp.concatenate([change[:3] - conc_adj[None] * gradients, change[3:]], axis=0)
        updated = fluid[None] * (state + TIME_STEP * change)
        adjoint = updated.at[2].add(wall_sum)
    return adjoint


def solution(mesh):
    placed = (
        P(None, "gx", "gy", None),
        P(None, "gx", "gy", None),
        P("gx", "gy", None),
        P("gx", "gy", None),
        P("gx", "gy"),
        P("gx", "gy", None),
        P("gx", "gy", None, None),
        P("gx", "gy", None, None),
        P("gx", "gy", None, None, None),
    )
    return jax.shard_map(
        shards, mesh=mesh, in_specs=placed, out_specs=P(None, "gx", "gy", None), check_vma=False
    )
```

profile of v0, /device:TPU:10, one launch (start us, length us, event | category | flops | bytes accessed | tf_op | source)
XLA Modules:
  0.0 97.6 jit_solution(12228454834160688312)
XLA Ops:
  0.0 1.3 %copy.17 = f32[4,16,32,128]{3,2,1,0:T(8,128)S(1)} copy(f32[4,16,32,128]{3,2,1,0:T(8,128)} %param.17) | data formatting | bytes 2097152
  1.3 0.0 copy-done.26
  1.3 0.1 copy-done.25
  1.4 3.8 %collective-permute-start = (bf16[5,1,32,128]{3,2,1,0:T(8,128)(2,1)S(1)}, bf16[5,1,32,128]{3,2,1,0:T(8,128)(2,1)S(1)}, u32[]{:S(2)}, u32[]{:S(2)}) collective-permute-start(bf16[5,1,32,128]{3,2,1,0:T(8,128)(2,1)S(1)} %get-tuple-element.79), channel_id=1, source_target_pairs={{0,16},{16,32},{32,48},{48,64},{64,80},{80,96},{96,112},{112,128},... | collective-permute-start | bytes 122888 | tf_op jit(solution)/shard_map/ppermute | solution.py:19
  5.3 5.7 %collective-permute-start.1 = (bf16[5,1,32,128]{3,2,1,0:T(8,128)(2,1)S(1)}, bf16[5,1,32,128]{3,2,1,0:T(8,128)(2,1)S(1)}, u32[]{:S(2)}, u32[]{:S(2)}) collective-permute-start(bf16[5,1,32,128]{3,2,1,0:T(8,128)(2,1)S(1)} %get-tuple-element.80), channel_id=1, source_target_pairs={{16,0},{32,16},{48,32},{64,48},{80,64},{96,80},{112,96},{128,112},... | collective-permute-start | bytes 122888 | tf_op jit(solution)/shard_map/ppermute | solution.py:20
  11.1 0.0 copy-start.27
  11.1 1.0 %scatter_fusion = f32[65536]{0:T(1024)S(1)} fusion(f32[65536]{0:T(1024)S(1)} %bitcast.50, s32[64]{0:T(128)S(1)} %fusion.55, f32[64]{0:T(128)S(1)} %broadcast.173), kind=kCustom, calls=%fused_computation.2 | custom fusion | flops 64 | bytes 1024 | tf_op jit(solution)/shard_map/scatter-add | solution.py:84
  12.2 1.9 %collective-permute-start.4 = (f32[4,1,32,128]{3,2,1,0:T(8,128)S(1)}, f32[4,1,32,128]{3,2,1,0:T(8,128)S(1)}, u32[]{:S(2)}, u32[]{:S(2)}) collective-permute-start(f32[4,1,32,128]{3,2,1,0:T(8,128)S(1)} %get-tuple-element.75), channel_id=1, source_target_pairs={{0,16},{16,32},{32,48},{48,64},{64,80},{80,96},{96,112},{112,128},... | collective-permute-start | bytes 196616 | tf_op jit(solution)/shard_map/ppermute | solution.py:19
  14.1 6.0 %collective-permute-start.5 = (f32[4,1,32,128]{3,2,1,0:T(8,128)S(1)}, f32[4,1,32,128]{3,2,1,0:T(8,128)S(1)}, u32[]{:S(2)}, u32[]{:S(2)}) collective-permute-start(f32[4,1,32,128]{3,2,1,0:T(8,128)S(1)} %get-tuple-element.76), channel_id=1, source_target_pairs={{16,0},{32,16},{48,32},{64,48},{80,64},{96,80},{112,96},{128,112},... | collective-permute-start | bytes 196616 | tf_op jit(solution)/shard_map/ppermute | solution.py:20
  20.2 0.1 reshape.249
  20.3 0.7 gather_fusion
  21.0 0.8 fusion.49
  21.8 6.5 %all-to-all-start = ((f32[16,16,128]{2,1,0:T(8,128)}), f32[16,16,128]{2,1,0:T(8,128)S(1)}, u32[]{:S(2)}, u32[]{:S(2)}) async-start(f32[16,16,128]{2,1,0:T(8,128)} %fusion.49), calls=%async_computation | async-start | bytes 262144 | tf_op jit(solution)/shard_map/all_to_all | solution.py:88
  28.3 0.1 fusion.48
  28.5 0.1 reshape_squeeze.10
  28.6 0.1 pad_maximum_fusion.23
  28.7 1.9 %collective-permute-start.2 = (bf16[5,18,1,128]{3,2,1,0:T(2,128)(2,1)S(1)}, bf16[5,18,1,128]{3,2,1,0:T(2,128)(2,1)S(1)}, u32[]{:S(2)}, u32[]{:S(2)}) collective-permute-start(bf16[5,18,1,128]{3,2,1,0:T(2,128)(2,1)S(1)} %get-tuple-element.77), channel_id=1, source_target_pairs={{0,1},{1,2},{2,3},{3,4},{4,5},{5,6},{6,7},{7,8},{8,9},{9,10},{10,1... | collective-permute-start | bytes 69128 | tf_op jit(solution)/shard_map/ppermute | solution.py:19
  30.6 6.0 %collective-permute-start.3 = (bf16[5,18,1,128]{3,2,1,0:T(2,128)(2,1)S(1)}, bf16[5,18,1,128]{3,2,1,0:T(2,128)(2,1)S(1)}, u32[]{:S(2)}, u32[]{:S(2)}) collective-permute-start(bf16[5,18,1,128]{3,2,1,0:T(2,128)(2,1)S(1)} %get-tuple-element.78), channel_id=1, source_target_pairs={{1,0},{2,1},{3,2},{4,3},{5,4},{6,5},{7,6},{8,7},{9,8},{10,9},{11,1... | collective-permute-start | bytes 69128 | tf_op jit(solution)/shard_map/ppermute | solution.py:20
  36.7 1.7 %collective-permute-done.3 = bf16[5,18,1,128]{3,2,1,0:T(2,128)(2,1)S(1)} collective-permute-done((bf16[5,18,1,128]{3,2,1,0:T(2,128)(2,1)S(1)}, bf16[5,18,1,128]{3,2,1,0:T(2,128)(2,1)S(1)}, u32[]{:S(2)}, u32[]{:S(2)}) %collective-permute-start.3) | collective-permute-done | bytes 23072 | tf_op jit(solution)/shard_map/ppermute | solution.py:20
  38.3 0.4 maximum_convert_fusion
  38.7 0.1 slice_bitcast_fusion
  38.9 0.1 broadcast_multiply_fusion.1
  39.0 0.7 fusion.59
  39.7 0.2 fusion.62
  40.0 0.2 slice_add_fusion.7
  40.3 0.1 fusion.47
  40.4 0.1 pad_maximum_fusion.30
  40.5 3.4 %collective-permute-start.6 = (f32[4,18,1,128]{3,2,1,0:T(1,128)S(1)}, f32[4,18,1,128]{3,2,1,0:T(1,128)S(1)}, u32[]{:S(2)}, u32[]{:S(2)}) collective-permute-start(f32[4,18,1,128]{3,2,1,0:T(1,128)S(1)} %get-tuple-element.64), channel_id=1, source_target_pairs={{0,1},{1,2},{2,3},{3,4},{4,5},{5,6},{6,7},{7,8},{8,9},{9,10},{10,1... | collective-permute-start | bytes 110600 | tf_op jit(solution)/shard_map/ppermute | solution.py:19
  43.9 4.6 %collective-permute-start.7 = (f32[4,18,1,128]{3,2,1,0:T(1,128)S(1)}, f32[4,18,1,128]{3,2,1,0:T(1,128)S(1)}, u32[]{:S(2)}, u32[]{:S(2)}) collective-permute-start(f32[4,18,1,128]{3,2,1,0:T(1,128)S(1)} %get-tuple-element.63), channel_id=1, source_target_pairs={{1,0},{2,1},{3,2},{4,3},{5,4},{6,5},{7,6},{8,7},{9,8},{10,9},{11,1... | collective-permute-start | bytes 110600 | tf_op jit(solution)/shard_map/ppermute | solution.py:20
  48.5 0.1 multiply_bitcast_fusion
  48.6 1.5 %collective-permute-done.7 = f32[4,18,1,128]{3,2,1,0:T(1,128)S(1)} collective-permute-done((f32[4,18,1,128]{3,2,1,0:T(1,128)S(1)}, f32[4,18,1,128]{3,2,1,0:T(1,128)S(1)}, u32[]{:S(2)}, u32[]{:S(2)}) %collective-permute-start.7) | collective-permute-done | bytes 36896 | tf_op jit(solution)/shard_map/ppermute | solution.py:20
  50.1 0.3 fusion.41
  50.5 2.7 %fusion.23 = f32[4,16,32,128]{3,2,1,0:T(8,128)S(1)} fusion(f32[4,16,32,128]{3,2,1,0:T(8,128)S(1)} %constant_dynamic-update-slice_fusion.1, f32[4,18,1,128]{3,2,1,0:T(1,128)S(1)} %collective-permute-done.6, f32[4,1,32,128]{3,2,1,0:T(8,128)S(1)} %collective-permute-done.5, f32[4,1,32,128]{3,2,1,0:T(8,128)S(1)} %collective-permute-done.4, ...), kind=kLoop, calls=%fused_computation.43 | loop fusion | flops 8388608 | bytes 12230656 | tf_op jit(solution)/shard_map/mul | solution.py:55
  53.2 0.2 slice_subtract_fusion.5
  53.4 0.3 fusion.35
  53.7 1.5 %scatter_custom_fusion.1 = f32[512,128]{1,0:T(8,128)S(1)} fusion(s32[256]{0:T(256)S(1)} %bitcast.69, f32[256,128]{1,0:T(8,128)S(1)} %bitcast.68, f32[]{:T(128)} %constant.113.clone.1), kind=kCustom, calls=%fused_computation.110 | custom fusion | flops 32768 | bytes 262148 | tf_op jit(solution)/shard_map/scatter-add | solution.py:92
  55.2 0.1 fusion.43
  55.3 1.0 %scatter_fusion.1 = f32[65536]{0:T(1024)S(1)} fusion(f32[65536]{0:T(1024)S(1)} %bitcast.54, s32[64]{0:T(128)S(1)} %fusion.55, f32[64]{0:T(128)S(1)} %broadcast.173), kind=kCustom, calls=%fused_computation.4 | custom fusion | flops 64 | bytes 1024 | tf_op jit(solution)/shard_map/scatter-add | solution.py:84
  56.4 0.1 broadcast_multiply_fusion
  56.5 0.6 fusion.58
  57.1 0.4 fusion.57
  57.5 3.4 %collective-permute-start.8 = (f32[4,1,32,128]{3,2,1,0:T(8,128)}, f32[4,1,32,128]{3,2,1,0:T(8,128)S(1)}, u32[]{:S(2)}, u32[]{:S(2)}) collective-permute-start(f32[4,1,32,128]{3,2,1,0:T(8,128)} %get-tuple-element.69), channel_id=1, source_target_pairs={{0,16},{16,32},{32,48},{48,64},{64,80},{80,96},{96,112},{112,128},... | collective-permute-start | bytes 196616 | tf_op jit(solution)/shard_map/ppermute | solution.py:19
  60.9 4.6 %collective-permute-start.9 = (f32[4,1,32,128]{3,2,1,0:T(8,128)}, f32[4,1,32,128]{3,2,1,0:T(8,128)S(1)}, u32[]{:S(2)}, u32[]{:S(2)}) collective-permute-start(f32[4,1,32,128]{3,2,1,0:T(8,128)} %get-tuple-element.70), channel_id=1, source_target_pairs={{16,0},{32,16},{48,32},{64,48},{80,64},{96,80},{112,96},{128,112},... | collective-permute-start | bytes 196616 | tf_op jit(solution)/shard_map/ppermute | solution.py:20
  65.5 1.7 %fusion.56 = (f32[4,16,32,127]{3,2,1,0:T(8,128)}, f32[4,16,32,127]{3,2,1,0:T(8,128)}) fusion(f32[4,16,32,128]{3,2,1,0:T(8,128)S(1)} %broadcast_multiply_fusion), kind=kLoop, calls=%fused_computation.134 | loop fusion | bytes 4161536 | tf_op jit(solution)/shard_map/slice | solution.py:26
  67.2 1.3 %gather_fusion.1 = f32[256,128]{1,0:T(8,128)} fusion(f32[512,128]{1,0:T(8,128)S(1)} %bitcast.56, s32[1024]{0:T(1024)S(1)} %pad_clamp_fusion), kind=kCustom, calls=%fused_computation.1 | custom fusion | bytes 263168 | tf_op jit(solution)/shard_map/gather | solution.py:87
  68.5 0.7 pad_maximum_fusion.27
  69.2 2.0 %collective-permute-start.10 = (f32[4,18,1,128]{3,2,1,0:T(1,128)}, f32[4,18,1,128]{3,2,1,0:T(1,128)}, u32[]{:S(2)}, u32[]{:S(2)}) collective-permute-start(f32[4,18,1,128]{3,2,1,0:T(1,128)} %get-tuple-element.62), channel_id=1, source_target_pairs={{0,1},{1,2},{2,3},{3,4},{4,5},{5,6},{6,7},{7,8},{8,9},{9,10},{10,1... | collective-permute-start | bytes 110600 | tf_op jit(solution)/shard_map/ppermute | solution.py:19
  71.2 6.0 %collective-permute-start.11 = (f32[4,18,1,128]{3,2,1,0:T(1,128)}, f32[4,18,1,128]{3,2,1,0:T(1,128)}, u32[]{:S(2)}, u32[]{:S(2)}) collective-permute-start(f32[4,18,1,128]{3,2,1,0:T(1,128)} %get-tuple-element.61), channel_id=1, source_target_pairs={{1,0},{2,1},{3,2},{4,3},{5,4},{6,5},{7,6},{8,7},{9,8},{10,9},{11,1... | collective-permute-start | bytes 110600 | tf_op jit(solution)/shard_map/ppermute | solution.py:20
  77.2 1.7 %fusion.50 = f32[16,16,128]{2,1,0:T(8,128)} fusion(f32[16,16,128]{2,1,0:T(8,128)} %bitcast.66, f32[1,1,16,16,128]{4,3,2,1,0:T(8,128)} %param.25, pred[16,16]{1,0:T(8,128)(4,1)S(1)} %compare_bitcast_fusion), kind=kLoop, calls=%fused_computation.107 | loop fusion | flops 65536 | bytes 393472 | tf_op jit(solution)/shard_map/jit(_where)/select_n | solution.py:87
  78.9 7.3 %all-to-all-start.1 = ((f32[16,16,128]{2,1,0:T(8,128)}), f32[16,16,128]{2,1,0:T(8,128)}, u32[]{:S(2)}, u32[]{:S(2)}) async-start(f32[16,16,128]{2,1,0:T(8,128)} %fusion.50), calls=%async_computation.1 | async-start | bytes 262144 | tf_op jit(solution)/shard_map/all_to_all | solution.py:88
  86.2 1.6 %fusion.39 = (f32[4,18,34,128]{3,2,1,0:T(8,128)S(1)}, f32[4,18,34,128]{3,2,1,0:T(8,128)S(1)}) fusion(f32[4,18,1,128]{3,2,1,0:T(1,128)} %collective-permute-done.11, f32[4,1,32,128]{3,2,1,0:T(8,128)S(1)} %collective-permute-done.9, f32[4,16,32,128]{3,2,1,0:T(8,128)S(1)} %constant_dynamic-update-slice_fusion, f32[4,1,32,128]{3,2,1,0:T(8,128)S(1)} %collective-permute-done.8, ...), kind=kLoop, calls=%fused_computation.72 | loop fusion | flops 1880064 | bytes 4386816 | tf_op jit(solution)/shard_map/mul | solution.py:36
  87.8 0.1 copy-done.1
  87.9 0.0 copy-done.14
  88.0 0.1 copy-done.16
  88.1 0.1 copy-done.18
  88.1 0.1 copy-done.20
  88.2 0.1 copy-done.22
  88.3 0.1 copy-done.24
  88.4 3.4 %fusion.6 = f32[4,16,32,128]{3,2,1,0:T(8,128)S(1)} fusion(f32[4,16,32,128]{3,2,1,0:T(8,128)S(1)} %constant_dynamic-update-slice_fusion, f32[4,18,1,128]{3,2,1,0:T(1,128)} %collective-permute-done.10, f32[4,1,32,128]{3,2,1,0:T(8,128)S(1)} %collective-permute-done.9, f32[4,1,32,128]{3,2,1,0:T(8,128)S(1)} %collective-permute-done.8, ...), kind=kLoop, calls=%fused_computation.15 | loop fusion | flops 8388608 | bytes 12230656 | tf_op jit(solution)/shard_map/mul | solution.py:55
  91.9 0.2 slice_subtract_fusion.4
  92.1 0.7 copy-done.12
  92.8 1.2 %fusion.37 = f32[4,16,32,128]{3,2,1,0:T(8,128)} fusion(f32[4,16,32,128]{3,2,1,0:T(8,128)S(1)} %constant_dynamic-update-slice_fusion, f32[1,16,32,128]{3,2,1,0:T(8,128)S(1)} %slice.420, f32[3,16,32,128]{3,2,1,0:T(8,128)S(1)} %slice_subtract_fusion.4, f32[16,32,128]{2,1,0:T(8,128)S(1)} %copy-done.12), kind=kLoop, calls=%fused_computation.69 | loop fusion | flops 1048576 | bytes 3407872 | tf_op jit(solution)/shard_map/mul | solution.py:99
  94.0 1.9 %scatter_custom_fusion.3 = f32[512,128]{1,0:T(8,128)S(1)} fusion(s32[256]{0:T(256)S(1)} %bitcast.70, f32[256,128]{1,0:T(8,128)} %bitcast.27, f32[]{:T(128)} %constant.113.clone.1), kind=kCustom, calls=%fused_computation.108 | custom fusion | flops 32768 | bytes 262656 | tf_op jit(solution)/shard_map/scatter-add | solution.py:92
  95.9 1.7 %fusion.42 = f32[4,16,32,128]{3,2,1,0:T(8,128)} fusion(f32[4,16,32,128]{3,2,1,0:T(8,128)} %fusion.37, f32[1,16,32,128]{3,2,1,0:T(8,128)S(1)} %bitcast.64), kind=kLoop, calls=%fused_computation.85 | loop fusion | flops 65536 | bytes 786432 | tf_op jit(solution)/shard_map/scatter-add | solution.py:100
  (80 shorter events, 0.3 us)
Async XLA Ops:
  0.0 1.3 %copy-start.2 = (bf16[3,16,32,128]{3,2,1,0:T(8,128)(2,1)S(1)}, bf16[3,16,32,128]{3,2,1,0:T(8,128)(2,1)}, u32[]{:S(2)}) copy-start(bf16[3,16,32,128]{3,2,1,0:T(8,128)(2,1)} %param.18) | copy-start | bytes 1179652
  0.0 1.3 %copy-start.26 = (bf16[16,32,128]{2,1,0:T(8,128)(2,1)S(1)}, bf16[16,32,128]{2,1,0:T(8,128)(2,1)}, u32[]{:S(2)}) copy-start(bf16[16,32,128]{2,1,0:T(8,128)(2,1)} %param.19) | copy-start | bytes 393220
  0.0 1.4 %copy-start.25 = (bf16[16,32,128]{2,1,0:T(8,128)(2,1)S(1)}, bf16[16,32,128]{2,1,0:T(8,128)(2,1)}, u32[]{:S(2)}) copy-start(bf16[16,32,128]{2,1,0:T(8,128)(2,1)} %param.20) | copy-start | bytes 393220
  0.0 11.0 %copy-start.31 = (s32[1,1,64]{2,1,0:T(1,128)S(1)}, s32[1,1,64]{2,1,0:T(1,128)}, u32[]{:S(2)}) copy-start(s32[1,1,64]{2,1,0:T(1,128)} %param.22) | copy-start | bytes 772
  1.4 18.8 %copy-start.28 = (s32[1,1,16,16]{3,2,1,0:T(8,128)S(1)}, s32[1,1,16,16]{3,2,1,0:T(8,128)}, u32[]{:S(2)}) copy-start(s32[1,1,16,16]{3,2,1,0:T(8,128)} %param.23) | copy-start | bytes 3076
  1.4 27.1 %collective-permute-start = (bf16[5,1,32,128]{3,2,1,0:T(8,128)(2,1)S(1)}, bf16[5,1,32,128]{3,2,1,0:T(8,128)(2,1)S(1)}, u32[]{:S(2)}, u32[]{:S(2)}) collective-permute-start(bf16[5,1,32,128]{3,2,1,0:T(8,128)(2,1)S(1)} %get-tuple-element.79), channel_id=1, source_target_pairs={{0,16},{16,32},{32,48},{48,64},{64,80},{80,96},{96,112},{112,128},... | collective-permute-start | bytes 122888 | tf_op jit(solution)/shard_map/ppermute | solution.py:19
  5.3 23.3 %collective-permute-start.1 = (bf16[5,1,32,128]{3,2,1,0:T(8,128)(2,1)S(1)}, bf16[5,1,32,128]{3,2,1,0:T(8,128)(2,1)S(1)}, u32[]{:S(2)}, u32[]{:S(2)}) collective-permute-start(bf16[5,1,32,128]{3,2,1,0:T(8,128)(2,1)S(1)} %get-tuple-element.80), channel_id=1, source_target_pairs={{16,0},{32,16},{48,32},{64,48},{80,64},{96,80},{112,96},{128,112},... | collective-permute-start | bytes 122888 | tf_op jit(solution)/shard_map/ppermute | solution.py:20
  11.1 10.0 %copy-start.27 = (f32[1,1,16,16,128]{4,3,2,1,0:T(8,128)S(1)}, f32[1,1,16,16,128]{4,3,2,1,0:T(8,128)}, u32[]{:S(2)}) copy-start(f32[1,1,16,16,128]{4,3,2,1,0:T(8,128)} %param.25) | copy-start | bytes 393220
  12.1 16.2 %copy-start.29 = (s32[16,32]{1,0:T(8,128)S(1)}, s32[16,32]{1,0:T(8,128)}, u32[]{:S(2)}) copy-start(s32[16,32]{1,0:T(8,128)} %param.21) | copy-start | bytes 6148
  12.1 16.3 %copy-start.30 = (s32[1,1,16,16]{3,2,1,0:T(8,128)S(1)}, s32[1,1,16,16]{3,2,1,0:T(8,128)}, u32[]{:S(2)}) copy-start(s32[1,1,16,16]{3,2,1,0:T(8,128)} %param.24) | copy-start | bytes 3076
  12.2 28.2 %collective-permute-start.4 = (f32[4,1,32,128]{3,2,1,0:T(8,128)S(1)}, f32[4,1,32,128]{3,2,1,0:T(8,128)S(1)}, u32[]{:S(2)}, u32[]{:S(2)}) collective-permute-start(f32[4,1,32,128]{3,2,1,0:T(8,128)S(1)} %get-tuple-element.75), channel_id=1, source_target_pairs={{0,16},{16,32},{32,48},{48,64},{64,80},{80,96},{96,112},{112,128},... | collective-permute-start | bytes 196616 | tf_op jit(solution)/shard_map/ppermute | solution.py:19
  14.1 26.3 %collective-permute-start.5 = (f32[4,1,32,128]{3,2,1,0:T(8,128)S(1)}, f32[4,1,32,128]{3,2,1,0:T(8,128)S(1)}, u32[]{:S(2)}, u32[]{:S(2)}) collective-permute-start(f32[4,1,32,128]{3,2,1,0:T(8,128)S(1)} %get-tuple-element.76), channel_id=1, source_target_pairs={{16,0},{32,16},{48,32},{64,48},{80,64},{96,80},{112,96},{128,112},... | collective-permute-start | bytes 196616 | tf_op jit(solution)/shard_map/ppermute | solution.py:20
  21.8 31.9 %all-to-all-start = ((f32[16,16,128]{2,1,0:T(8,128)}), f32[16,16,128]{2,1,0:T(8,128)S(1)}, u32[]{:S(2)}, u32[]{:S(2)}) async-start(f32[16,16,128]{2,1,0:T(8,128)} %fusion.49), calls=%async_computation | async-start | bytes 262144 | tf_op jit(solution)/shard_map/all_to_all | solution.py:88
  28.5 24.9 %copy-start.11 = (f32[16,32,128]{2,1,0:T(8,128)}, f32[16,32,128]{2,1,0:T(8,128)S(1)}, u32[]{:S(2)}) copy-start(f32[16,32,128]{2,1,0:T(8,128)S(1)} %fusion.48) | copy-start | bytes 786436
  28.7 8.0 %collective-permute-start.2 = (bf16[5,18,1,128]{3,2,1,0:T(2,128)(2,1)S(1)}, bf16[5,18,1,128]{3,2,1,0:T(2,128)(2,1)S(1)}, u32[]{:S(2)}, u32[]{:S(2)}) collective-permute-start(bf16[5,18,1,128]{3,2,1,0:T(2,128)(2,1)S(1)} %get-tuple-element.77), channel_id=1, source_target_pairs={{0,1},{1,2},{2,3},{3,4},{4,5},{5,6},{6,7},{7,8},{8,9},{9,10},{10,1... | collective-permute-start | bytes 69128 | tf_op jit(solution)/shard_map/ppermute | solution.py:19
  30.6 7.8 %collective-permute-start.3 = (bf16[5,18,1,128]{3,2,1,0:T(2,128)(2,1)S(1)}, bf16[5,18,1,128]{3,2,1,0:T(2,128)(2,1)S(1)}, u32[]{:S(2)}, u32[]{:S(2)}) collective-permute-start(bf16[5,18,1,128]{3,2,1,0:T(2,128)(2,1)S(1)} %get-tuple-element.78), channel_id=1, source_target_pairs={{1,0},{2,1},{3,2},{4,3},{5,4},{6,5},{7,6},{8,7},{9,8},{10,9},{11,1... | collective-permute-start | bytes 69128 | tf_op jit(solution)/shard_map/ppermute | solution.py:20
  38.8 11.3 %copy-start.3 = (f32[18,34,128]{2,1,0:T(8,128)}, f32[18,34,128]{2,1,0:T(8,128)S(1)}, u32[]{:S(2)}) copy-start(f32[18,34,128]{2,1,0:T(8,128)S(1)} %get-tuple-element.55) | copy-start | bytes 940036
  38.8 11.2 %copy-start.4 = (f32[18,34,128]{2,1,0:T(8,128)}, f32[18,34,128]{2,1,0:T(8,128)S(1)}, u32[]{:S(2)}) copy-start(f32[18,34,128]{2,1,0:T(8,128)S(1)} %get-tuple-element.56) | copy-start | bytes 940036
  40.2 10.2 %copy-start.13 = (f32[16,32,128]{2,1,0:T(8,128)}, f32[16,32,128]{2,1,0:T(8,128)S(1)}, u32[]{:S(2)}) copy-start(f32[16,32,128]{2,1,0:T(8,128)S(1)} %get-tuple-element.85) | copy-start | bytes 786436
  40.2 10.2 %copy-start.15 = (f32[16,32,128]{2,1,0:T(8,128)}, f32[16,32,128]{2,1,0:T(8,128)S(1)}, u32[]{:S(2)}) copy-start(f32[16,32,128]{2,1,0:T(8,128)S(1)} %get-tuple-element.86) | copy-start | bytes 786436
  40.2 10.2 %copy-start.17 = (f32[16,32,128]{2,1,0:T(8,128)}, f32[16,32,128]{2,1,0:T(8,128)S(1)}, u32[]{:S(2)}) copy-start(f32[16,32,128]{2,1,0:T(8,128)S(1)} %get-tuple-element.87) | copy-start | bytes 786436
  40.3 10.2 %copy-start.19 = (f32[16,32,128]{2,1,0:T(8,128)}, f32[16,32,128]{2,1,0:T(8,128)S(1)}, u32[]{:S(2)}) copy-start(f32[16,32,128]{2,1,0:T(8,128)S(1)} %get-tuple-element.88) | copy-start | bytes 786436
  40.3 10.2 %copy-start.21 = (f32[16,32,128]{2,1,0:T(8,128)}, f32[16,32,128]{2,1,0:T(8,128)S(1)}, u32[]{:S(2)}) copy-start(f32[16,32,128]{2,1,0:T(8,128)S(1)} %get-tuple-element.89) | copy-start | bytes 786436
  40.3 10.2 %copy-start.23 = (f32[16,32,128]{2,1,0:T(8,128)}, f32[16,32,128]{2,1,0:T(8,128)S(1)}, u32[]{:S(2)}) copy-start(f32[16,32,128]{2,1,0:T(8,128)S(1)} %get-tuple-element.90) | copy-start | bytes 786436
  40.4 12.8 %copy-start.7 = (f32[1,16,32,128]{3,2,1,0:T(8,128)}, f32[1,16,32,128]{3,2,1,0:T(8,128)S(1)}, u32[]{:S(2)}) copy-start(f32[1,16,32,128]{3,2,1,0:T(8,128)S(1)} %get-tuple-element.81) | copy-start | bytes 786436
  40.4 12.8 %copy-start.9 = (f32[1,16,32,128]{3,2,1,0:T(8,128)}, f32[1,16,32,128]{3,2,1,0:T(8,128)S(1)}, u32[]{:S(2)}) copy-start(f32[1,16,32,128]{3,2,1,0:T(8,128)S(1)} %get-tuple-element.82) | copy-start | bytes 786436
  40.5 8.2 %collective-permute-start.6 = (f32[4,18,1,128]{3,2,1,0:T(1,128)S(1)}, f32[4,18,1,128]{3,2,1,0:T(1,128)S(1)}, u32[]{:S(2)}, u32[]{:S(2)}) collective-permute-start(f32[4,18,1,128]{3,2,1,0:T(1,128)S(1)} %get-tuple-element.64), channel_id=1, source_target_pairs={{0,1},{1,2},{2,3},{3,4},{4,5},{5,6},{6,7},{7,8},{8,9},{9,10},{10,1... | collective-permute-start | bytes 110600 | tf_op jit(solution)/shard_map/ppermute | solution.py:19
  43.9 6.2 %collective-permute-start.7 = (f32[4,18,1,128]{3,2,1,0:T(1,128)S(1)}, f32[4,18,1,128]{3,2,1,0:T(1,128)S(1)}, u32[]{:S(2)}, u32[]{:S(2)}) collective-permute-start(f32[4,18,1,128]{3,2,1,0:T(1,128)S(1)} %get-tuple-element.63), channel_id=1, source_target_pairs={{1,0},{2,1},{3,2},{4,3},{5,4},{6,5},{7,6},{8,7},{9,8},{10,9},{11,1... | collective-permute-start | bytes 110600 | tf_op jit(solution)/shard_map/ppermute | solution.py:20
  48.6 4.6 %copy-start.5 = (f32[1,16,32,128]{3,2,1,0:T(8,128)}, f32[1,16,32,128]{3,2,1,0:T(8,128)S(1)}, u32[]{:S(2)}) copy-start(f32[1,16,32,128]{3,2,1,0:T(8,128)S(1)} %multiply_bitcast_fusion) | copy-start | bytes 786436
  57.5 11.0 %collective-permute-start.8 = (f32[4,1,32,128]{3,2,1,0:T(8,128)}, f32[4,1,32,128]{3,2,1,0:T(8,128)S(1)}, u32[]{:S(2)}, u32[]{:S(2)}) collective-permute-start(f32[4,1,32,128]{3,2,1,0:T(8,128)} %get-tuple-element.69), channel_id=1, source_target_pairs={{0,16},{16,32},{32,48},{48,64},{64,80},{80,96},{96,112},{112,128},... | collective-permute-start | bytes 196616 | tf_op jit(solution)/shard_map/ppermute | solution.py:19
  60.9 7.6 %collective-permute-start.9 = (f32[4,1,32,128]{3,2,1,0:T(8,128)}, f32[4,1,32,128]{3,2,1,0:T(8,128)S(1)}, u32[]{:S(2)}, u32[]{:S(2)}) collective-permute-start(f32[4,1,32,128]{3,2,1,0:T(8,128)} %get-tuple-element.70), channel_id=1, source_target_pairs={{16,0},{32,16},{48,32},{64,48},{80,64},{96,80},{112,96},{128,112},... | collective-permute-start | bytes 196616 | tf_op jit(solution)/shard_map/ppermute | solution.py:20
  69.2 17.0 %collective-permute-start.10 = (f32[4,18,1,128]{3,2,1,0:T(1,128)}, f32[4,18,1,128]{3,2,1,0:T(1,128)}, u32[]{:S(2)}, u32[]{:S(2)}) collective-permute-start(f32[4,18,1,128]{3,2,1,0:T(1,128)} %get-tuple-element.62), channel_id=1, source_target_pairs={{0,1},{1,2},{2,3},{3,4},{4,5},{5,6},{6,7},{7,8},{8,9},{9,10},{10,1... | collective-permute-start | bytes 110600 | tf_op jit(solution)/shard_map/ppermute | solution.py:19
  71.2 15.1 %collective-permute-start.11 = (f32[4,18,1,128]{3,2,1,0:T(1,128)}, f32[4,18,1,128]{3,2,1,0:T(1,128)}, u32[]{:S(2)}, u32[]{:S(2)}) collective-permute-start(f32[4,18,1,128]{3,2,1,0:T(1,128)} %get-tuple-element.61), channel_id=1, source_target_pairs={{1,0},{2,1},{3,2},{4,3},{5,4},{6,5},{7,6},{8,7},{9,8},{10,9},{11,1... | collective-permute-start | bytes 110600 | tf_op jit(solution)/shard_map/ppermute | solution.py:20
  78.9 15.1 %all-to-all-start.1 = ((f32[16,16,128]{2,1,0:T(8,128)}), f32[16,16,128]{2,1,0:T(8,128)}, u32[]{:S(2)}, u32[]{:S(2)}) async-start(f32[16,16,128]{2,1,0:T(8,128)} %fusion.50), calls=%async_computation.1 | async-start | bytes 262144 | tf_op jit(solution)/shard_map/all_to_all | solution.py:88
  86.2 1.7 %copy-start = (f32[4,16,32,127]{3,2,1,0:T(8,128)S(1)}, f32[4,16,32,127]{3,2,1,0:T(8,128)}, u32[]{:S(2)}) copy-start(f32[4,16,32,127]{3,2,1,0:T(8,128)} %get-tuple-element.65) | copy-start | bytes 3121156
  86.2 1.8 %copy-start.1 = (f32[4,16,32,127]{3,2,1,0:T(8,128)S(1)}, f32[4,16,32,127]{3,2,1,0:T(8,128)}, u32[]{:S(2)}) copy-start(f32[4,16,32,127]{3,2,1,0:T(8,128)} %get-tuple-element.66) | copy-start | bytes 3121156
  86.2 1.8 %copy-start.14 = (f32[16,32,128]{2,1,0:T(8,128)S(1)}, f32[16,32,128]{2,1,0:T(8,128)}, u32[]{:S(2)}) copy-start(f32[16,32,128]{2,1,0:T(8,128)} %copy-done.13) | copy-start | bytes 786436
  86.2 1.9 %copy-start.16 = (f32[16,32,128]{2,1,0:T(8,128)S(1)}, f32[16,32,128]{2,1,0:T(8,128)}, u32[]{:S(2)}) copy-start(f32[16,32,128]{2,1,0:T(8,128)} %copy-done.15) | copy-start | bytes 786436
  86.2 2.0 %copy-start.18 = (f32[16,32,128]{2,1,0:T(8,128)S(1)}, f32[16,32,128]{2,1,0:T(8,128)}, u32[]{:S(2)}) copy-start(f32[16,32,128]{2,1,0:T(8,128)} %copy-done.17) | copy-start | bytes 786436
  86.2 2.0 %copy-start.20 = (f32[16,32,128]{2,1,0:T(8,128)S(1)}, f32[16,32,128]{2,1,0:T(8,128)}, u32[]{:S(2)}) copy-start(f32[16,32,128]{2,1,0:T(8,128)} %copy-done.19) | copy-start | bytes 786436
  86.2 2.1 %copy-start.22 = (f32[16,32,128]{2,1,0:T(8,128)S(1)}, f32[16,32,128]{2,1,0:T(8,128)}, u32[]{:S(2)}) copy-start(f32[16,32,128]{2,1,0:T(8,128)} %copy-done.21) | copy-start | bytes 786436
  86.2 2.2 %copy-start.24 = (f32[16,32,128]{2,1,0:T(8,128)S(1)}, f32[16,32,128]{2,1,0:T(8,128)}, u32[]{:S(2)}) copy-start(f32[16,32,128]{2,1,0:T(8,128)} %copy-done.23) | copy-start | bytes 786436
  88.4 3.5 %copy-start.6 = (f32[1,16,32,128]{3,2,1,0:T(8,128)S(1)}, f32[1,16,32,128]{3,2,1,0:T(8,128)}, u32[]{:S(2)}) copy-start(f32[1,16,32,128]{3,2,1,0:T(8,128)} %copy-done.5) | copy-start | bytes 786436
  88.4 3.5 %copy-start.8 = (f32[1,16,32,128]{3,2,1,0:T(8,128)S(1)}, f32[1,16,32,128]{3,2,1,0:T(8,128)}, u32[]{:S(2)}) copy-start(f32[1,16,32,128]{3,2,1,0:T(8,128)} %copy-done.7) | copy-start | bytes 786436
  88.4 3.5 %copy-start.10 = (f32[1,16,32,128]{3,2,1,0:T(8,128)S(1)}, f32[1,16,32,128]{3,2,1,0:T(8,128)}, u32[]{:S(2)}) copy-start(f32[1,16,32,128]{3,2,1,0:T(8,128)} %copy-done.9) | copy-start | bytes 786436
  91.8 1.0 copy-start.12
where the time goes:
time: 98.8 us; the launch traced here: 97.6 us
  starting transfers between devices  63.2 us (64%)
  other arithmetic  21.6 us (22%)
  local copies, waits for them, and re-layouts  8.89 us (9%)
  waiting for transfers between devices  3.16 us (3%)
    ppermute x6, starting transfers between devices, with_halo(): after = lax.ppermute(leading, axis, down)  33 us
    ppermute x6, starting transfers between devices, with_halo(): before = lax.ppermute(last, axis, up)  16.4 us
    all_to_all x2, starting transfers between devices, shards(): lax.all_to_all(blocks, 'gx', split_axis=0, concat_axis=0, tiled=True)  13.8 us
    mul x2, other arithmetic, field_operator(): return 0.5 * (transport + spread)  6.1 us
    scatter-add x2, other arithmetic, shards(): wall_sum = jnp.zeros((rows_x * rows_y, levels), jnp.float32).at[dst_cols]...  3.34 us
    ppermute x6, waiting for transfers between devices, with_halo(): after = lax.ppermute(leading, axis, down)  3.14 us
    slice x4, local copies, waits for them, and re-layouts, shift_up(): field[..., 1:]  3.02 us
    unnamed x65, local copies, waits for them, and re-layouts  2.74 us
  transfers between devices with their start and end apart: 14, of which 2 were waited for; matrix products, arithmetic and copies ran while one was open for 20% of the time, Pallas kernels for 0%

commit v1 on v0

v1 whole, which is shorter than its diff:
```python
import jax
import jax.numpy as jnp
from jax import lax
from jax.experimental import pallas as pl
from jax.experimental.pallas import tpu as pltpu
from jax.sharding import PartitionSpec as P

F32 = jnp.float32
BF16 = jnp.bfloat16
PADY = 8
VMEM = pl.BlockSpec(memory_space=pltpu.VMEM)
HBM = pl.BlockSpec(memory_space=pltpu.HBM)


def split3(x):
    hi = x.astype(BF16)
    rest = x - hi.astype(F32)
    mid = rest.astype(BF16)
    low = (rest - mid.astype(F32)).astype(BF16)
    return jnp.concatenate([hi, mid, low], axis=1)


def join3(x):
    return x[:, :128] + x[:, 128:256] + x[:, 256:384]


def row_values(table):
    n = table.shape[1]
    eye = lax.broadcasted_iota(jnp.int32, (n, n), 0) == lax.broadcasted_iota(jnp.int32, (n, n), 1)
    high = table >> 4
    low = table & 15
    ones = jnp.ones((n, 128), BF16)
    total = None
    for part in (high * 16, low):
        part = part.astype(F32)
        rows = [
            jnp.where(eye, jnp.broadcast_to(part[d : d + 1], (n, n)), 0.0)
            for d in range(table.shape[0])
        ]
        spread = jnp.concatenate(rows, axis=0).astype(BF16)
        value = jnp.dot(spread, ones, preferred_element_type=F32)
        total = value if total is None else total + value
    return total


def select_rows(table, cols):
    index = row_values(table).astype(jnp.int32)
    lane = lax.broadcasted_iota(jnp.int32, index.shape, 1)
    hot = [(index == lane + t).astype(F32).astype(BF16) for t in range(0, cols, 128)]
    return jnp.concatenate(hot, axis=1)


def select_cols(table, cols):
    d_count, n = table.shape
    slots = d_count * n
    tile = (
        lax.broadcasted_iota(jnp.int32, (n, slots), 1) % n
        == lax.broadcasted_iota(jnp.int32, (n, slots), 0)
    ).astype(F32).astype(BF16)
    mine = (
        lax.broadcasted_iota(jnp.int32, (d_count, slots), 1) // n
        == lax.broadcasted_iota(jnp.int32, (d_count, slots), 0)
    )
    high = ((table >> 4) * 16).astype(F32).astype(BF16)
    low = (table & 15).astype(F32).astype(BF16)
    value = jnp.dot(high, tile, preferred_element_type=F32) + jnp.dot(
        low, tile, preferred_element_type=F32
    )
    line = jnp.sum(jnp.where(mine, value, 0.0), axis=0, keepdims=True).astype(jnp.int32)
    col = lax.broadcasted_iota(jnp.int32, (cols, slots), 0)
    return (col == line).astype(F32).astype(BF16)


def scatter_blocks(table, blocks, cols):
    hot = select_cols(table, cols)
    return join3(jnp.dot(hot, split3(blocks), preferred_element_type=F32))


def receptor_counts(line, cols):
    entries = line.shape[1]
    col = lax.broadcasted_iota(jnp.int32, (cols, entries), 0)
    level = lax.broadcasted_iota(jnp.int32, (128, entries), 0)
    hot_col = (col == (line >> 7)).astype(F32).astype(BF16)
    hot_level = (level == (line & 127)).astype(F32).astype(BF16)
    return lax.dot_general(
        hot_col, hot_level, (((1,), (1,)), ((), ())), preferred_element_type=F32
    )


def make_kernels(nx, ny, cx, cy, owners, cap):
    cols = cx * cy
    slots = owners * cap
    px, py = cx + 2, cy + 2 * PADY
    inside = (pl.ds(1, cx), pl.ds(PADY, cy))

    def edges_at():
        par_x = lax.rem(lax.axis_index("gx"), 2)
        par_y = lax.rem(lax.axis_index("gy"), 2)
        return (
            (cx - 1) * (1 - par_x), (cx - 1) * par_x,
            (cy - 1) * (1 - par_y), (cy - 1) * par_y,
        )

    def start_all(copies):
        for copy in copies:
            copy.start()

    def wait_all(copies):
        for copy in copies:
            copy.wait()

    def clear_halo(pad_ref, planes):
        zero = jnp.zeros((px, PADY, 128), F32)
        row = jnp.zeros((cy, 128), F32)
        for k in planes:
            pad_ref[k, :, 0:PADY, :] = zero
            pad_ref[k, :, PADY + cy : py, :] = zero
            pad_ref[k, 0, PADY : PADY + cy, :] = row
            pad_ref[k, cx + 1, PADY : PADY + cy, :] = row

    def take_halo(pad_ref, plane, n, xe_ref, xo_ref, ye_ref, yo_ref, with_x, with_y):
        me_x, me_y = lax.axis_index("gx"), lax.axis_index("gy")
        par_x, par_y = lax.rem(me_x, 2), lax.rem(me_y, 2)
        if with_x:
            e, o = xe_ref[n], xo_ref[n]
            before = jnp.where(par_x == 0, o, e)
            after = jnp.where(par_x == 0, e, o)
            pad_ref[plane, 0, PADY : PADY + cy, :] = jnp.where(me_x == 0, 0.0, before)
            pad_ref[plane, cx + 1, PADY : PADY + cy, :] = jnp.where(me_x == nx - 1, 0.0, after)
        if with_y:
            e, o = ye_ref[n], yo_ref[n]
            before = jnp.where(me_y == 0, 0.0, jnp.where(par_y == 0, o, e))
            after = jnp.where(me_y == ny - 1, 0.0, jnp.where(par_y == 0, e, o))
            for i in range(cx):
                pad_ref[plane, i + 1, PADY - 1 : PADY, :] = before[i : i + 1]
                pad_ref[plane, i + 1, PADY + cy : PADY + cy + 1, :] = after[i : i + 1]

    def fill_pads(pad_ref, vel_ref, dif_ref, con_ref):
        pad_ref[0, 1 : cx + 1, PADY : PADY + cy, :] = vel_ref[0].astype(F32)
        pad_ref[1, 1 : cx + 1, PADY : PADY + cy, :] = vel_ref[1].astype(F32)
        pad_ref[2, 1 : cx + 1, PADY : PADY + cy, :] = dif_ref[...].astype(F32)
        pad_ref[3, 1 : cx + 1, PADY : PADY + cy, :] = con_ref[...].astype(F32)

    def coefficients(pad_ref, vel_ref, fluid_ref, coef_ref):
        lane = lax.broadcasted_iota(jnp.int32, (8, 128), 1)
        level = lane.astype(F32)
        top = lane == 127
        bottom = lane == 0

        def up(x):
            return jnp.where(top, 0.0, pltpu.roll(x, 127, axis=1))

        def down(x):
            return jnp.where(bottom, 0.0, pltpu.roll(x, 1, axis=1))

        def body(i, carry):
            for half in range(cy // 16):
                uz2 = vel_ref[2, i, 16 * half : 16 * half + 16, :].astype(F32)
                for sub in range(2):
                    jv = 2 * half + sub
                    j = PADY + 8 * jv
                    lo = 8 * jv
                    at = pl.ds(pl.multiple_of(i * cy + lo, 8), 8)
                    uz = uz2[8 * sub : 8 * sub + 8]
                    fluid = (level >= fluid_ref[at, :]).astype(F32)
                    e = 0.05 * fluid
                    fluid_ref[at, :] = e
                    k0 = pad_ref[2, i + 1, j : j + 8, :]
                    ends = None
                    n = 1
                    for plane, plus, minus in (
                        (0, (i + 2, j), (i, j)),
                        (1, (i + 1, j + 1), (i + 1, j - 1)),
                    ):
                        for sign, (a, b) in ((1.0, plus), (-1.0, minus)):
                            kn = k0 + pad_ref[2, a, b : b + 8, :]
                            un = pad_ref[plane, a, b : b + 8, :]
                            coef_ref[n, at, :] = e * (kn + un if sign > 0 else kn - un)
                            ends = kn if ends is None else ends + kn
                            n += 1
                        coef_ref[7 + plane, at, :] = e * (
                            pad_ref[3, plus[0], plus[1] : plus[1] + 8, :]
                            - pad_ref[3, minus[0], minus[1] : minus[1] + 8, :]
                        )
                    kn = k0 + up(k0)
                    ends = ends + kn
                    coef_ref[5, at, :] = jnp.where(top, 0.0, e * (kn + up(uz)))
                    kn = k0 + down(k0)
                    ends = ends + kn
                    coef_ref[6, at, :] = jnp.where(bottom, 0.0, e * (kn - down(uz)))
                    c0 = pad_ref[3, i + 1, j : j + 8, :]
                    coef_ref[9, at, :] = e * (up(c0) - down(c0))
                    coef_ref[0, at, :] = fluid - e * ends
            return carry

        lax.fori_loop(0, cx, body, 0)

    def stencil(state_ref, coef_ref, extra, next_ref):
        def body(i, carry):
            for jv in range(cy // 8):
                j = PADY + 8 * jv
                at = pl.ds(pl.multiple_of(i * cy + 8 * jv, 8), 8)
                c = [coef_ref[n, at, :] for n in range(10)]
                conc = None
                for k in (3, 0, 1, 2):
                    f = state_ref[k, i + 1, j : j + 8, :]
                    if k == 3:
                        conc = f
                    value = c[0] * f
                    value = value + c[1] * state_ref[k, i + 2, j : j + 8, :]
                    value = value + c[2] * state_ref[k, i, j : j + 8, :]
                    value = value + c[3] * state_ref[k, i + 1, j + 1 : j + 9, :]
                    value = value + c[4] * state_ref[k, i + 1, j - 1 : j + 7, :]
                    value = value + c[5] * pltpu.roll(f, 127, axis=1)
                    value = value + c[6] * pltpu.roll(f, 1, axis=1)
                    if k < 3:
                        value = value - c[7 + k] * conc
                    for component, ref in extra:
                        if component == k:
                            value = value + ref[at, :]
                    next_ref[k, at, :] = value
            return carry

        lax.fori_loop(0, cx, body, 0)

    def edge_row(ref, k, row):
        return ref[k, pl.ds(pl.multiple_of(row * cy, 8), cy), :]

    def edge_col(ref, k, col):
        return ref[k, pl.ds(col, cx, stride=cy), :]

    def first(
        adj_hbm, vel_hbm, dif_hbm, con_hbm, rec_hbm, src_hbm, weight_hbm,
        blocks_ref, xe_ref, xo_ref, ye_ref, yo_ref,
        adj_ref, vel_ref, dif_ref, con_ref, rec_ref, src_ref, weight_ref, side_ref, sem,
    ):
        copies = [
            pltpu.make_async_copy(rec_hbm, rec_ref, sem.at[0]),
            pltpu.make_async_copy(adj_hbm.at[3], adj_ref.at[3], sem.at[1]),
            pltpu.make_async_copy(src_hbm, src_ref, sem.at[2]),
            pltpu.make_async_copy(weight_hbm, weight_ref, sem.at[3]),
            pltpu.make_async_copy(vel_hbm.at[pl.ds(0, 2)], vel_ref, sem.at[4]),
            pltpu.make_async_copy(dif_hbm, dif_ref, sem.at[5]),
            pltpu.make_async_copy(con_hbm, con_ref, sem.at[6]),
            pltpu.make_async_copy(adj_hbm.at[pl.ds(0, 3)], adj_ref.at[pl.ds(0, 3)], sem.at[7]),
        ]
        start_all(copies)
        row_e, row_o, col_e, col_o = edges_at()
        copies[0].wait()
        counts = receptor_counts(rec_ref[...], cols)
        copies[2].wait()
        hot = select_rows(src_ref[...], cols)
        copies[1].wait()
        conc = adj_ref[3] + counts
        adj_ref[3] = conc
        picked = join3(jnp.dot(hot, split3(conc), preferred_element_type=F32))
        copies[3].wait()
        blocks_ref[...] = weight_ref[...] * picked
        wait_all(copies[4:7])
        side_ref[0] = vel_ref[1].astype(F32).reshape(cols, 128)
        side_ref[1] = dif_ref[...].astype(F32).reshape(cols, 128)
        side_ref[2] = con_ref[...].astype(F32).reshape(cols, 128)
        for row, out in ((row_e, xe_ref), (row_o, xo_ref)):
            out[4] = vel_ref[0, row].astype(F32)
            out[5] = dif_ref[row].astype(F32)
            out[6] = con_ref[row].astype(F32)
        for col, out in ((col_e, ye_ref), (col_o, yo_ref)):
            for k in range(3):
                out[4 + k] = edge_col(side_ref, k, col)
        copies[7].wait()
        for k in range(4):
            xe_ref[k] = edge_row(adj_ref, k, row_e)
            xo_ref[k] = edge_row(adj_ref, k, row_o)
            ye_ref[k] = edge_col(adj_ref, k, col_e)
            yo_ref[k] = edge_col(adj_ref, k, col_o)

    def second(
        adj_hbm, vel_hbm, dif_hbm, con_hbm, rec_hbm, height_hbm, dst_hbm, arrived_ref,
        next_hbm, conc_ref, xe_ref, xo_ref, ye_ref, yo_ref,
        state_ref, vel_ref, dif_ref, con_ref, rec_ref, height_ref, dst_ref,
        pad_ref, fluid_ref, coef_ref, count_ref, wall_ref, next_ref, sem,
    ):
        copies = [
            pltpu.make_async_copy(height_hbm, height_ref, sem.at[0]),
            pltpu.make_async_copy(vel_hbm, vel_ref, sem.at[1]),
            pltpu.make_async_copy(dif_hbm, dif_ref, sem.at[2]),
            pltpu.make_async_copy(con_hbm, con_ref, sem.at[3]),
            pltpu.make_async_copy(rec_hbm, rec_ref, sem.at[4]),
            pltpu.make_async_copy(dst_hbm, dst_ref, sem.at[5]),
            pltpu.make_async_copy(adj_hbm, state_ref.at[:, inside[0], inside[1], :], sem.at[6]),
        ]
        start_all(copies)
        row_e, row_o, col_e, col_o = edges_at()
        clear_halo(pad_ref, range(4))
        clear_halo(state_ref, range(4))
        copies[0].wait()
        fluid_ref[...] = row_values(height_ref[...])
        wait_all(copies[1:4])
        fill_pads(pad_ref, vel_ref, dif_ref, con_ref)
        wait_all(copies[4:6])
        count_ref[...] = receptor_counts(rec_ref[...], cols)
        wall_ref[...] = scatter_blocks(dst_ref[...], arrived_ref[...], cols)
        coefficients(pad_ref, vel_ref, fluid_ref, coef_ref)
        copies[6].wait()
        state_ref[3, 1 : cx + 1, PADY : PADY + cy, :] += count_ref[...].reshape(cx, cy, 128)
        stencil(state_ref, coef_ref, ((3, count_ref), (2, wall_ref)), next_ref)
        out = pltpu.make_async_copy(next_ref, next_hbm, sem.at[7])
        out.start()
        conc_ref[...] = next_ref[3]
        for k in range(4):
            xe_ref[k] = edge_row(next_ref, k, row_e)
            xo_ref[k] = edge_row(next_ref, k, row_o)
            ye_ref[k] = edge_col(next_ref, k, col_e)
            yo_ref[k] = edge_col(next_ref, k, col_o)
        xe_ref[4] = fluid_ref[pl.ds(pl.multiple_of(row_e * cy, 8), cy), :]
        xo_ref[4] = fluid_ref[pl.ds(pl.multiple_of(row_o * cy, 8), cy), :]
        ye_ref[4] = fluid_ref[pl.ds(col_e, cx, stride=cy), :]
        yo_ref[4] = fluid_ref[pl.ds(col_o, cx, stride=cy), :]
        out.wait()

    def edge_signs():
        me_x, me_y = lax.axis_index("gx"), lax.axis_index("gy")
        sx = (1 - 2 * lax.rem(me_x, 2)).astype(F32)
        sy = (1 - 2 * lax.rem(me_y, 2)).astype(F32)
        wrap_x = jnp.logical_or(me_x == 0, me_x == nx - 1)
        wrap_y = jnp.logical_or(me_y == 0, me_y == ny - 1)
        return sx, sy, wrap_x, wrap_y

    def third(
        conc_in, oxe, oxo, oye, oyo, hxe, hxo, hye, hyo, pxe, pxo, pye, pyo, src_ref, weight_ref,
        blocks_ref, xe_ref, xo_ref, ye_ref, yo_ref,
        conc_ref, dxe, dxo, dye, dyo,
    ):
        row_e, row_o, col_e, col_o = edges_at()
        sx, sy, wrap_x, wrap_y = edge_signs()
        hot = select_rows(src_ref[...], cols)
        for own, halo, part, add, out, sign, wrap, axis in (
            (oxe, hxe, pxe, dxe, xe_ref, sx, None, 0),
            (oxo, hxo, pxo, dxo, xo_ref, -sx, wrap_x, 0),
            (oye, hye, pye, dye, ye_ref, sy, None, 1),
            (oyo, hyo, pyo, dyo, yo_ref, -sy, wrap_y, 1),
        ):
            e = part[4]
            if wrap is not None:
                e = jnp.where(wrap, 0.0, e)
            there = halo[5]
            near = e * (own[5] + there + sign * halo[4])
            far = e * there
            slope = e * (sign * halo[6])
            for k in range(4):
                value = near * halo[k] - far * own[k]
                if k == axis:
                    value = value - slope * own[3]
                add[k] = value
                out[k] = part[k] + value
        for k in range(4):
            for row, out, dx in ((row_e, xe_ref, dxe), (row_o, xo_ref, dxo)):
                for col, dy in ((col_e, dye), (col_o, dyo)):
                    out[k, pl.ds(col, 1), :] += dy[k, pl.ds(row, 1), :]
            for col, out in ((col_e, ye_ref), (col_o, yo_ref)):
                for row, dx in ((row_e, dxe), (row_o, dxo)):
                    out[k, pl.ds(row, 1), :] += dx[k, pl.ds(col, 1), :]
        conc_ref[...] = conc_in[...]
        conc_ref[pl.ds(pl.multiple_of(row_e * cy, 8), cy), :] = xe_ref[3]
        conc_ref[pl.ds(pl.multiple_of(row_o * cy, 8), cy), :] = xo_ref[3]
        conc_ref[pl.ds(col_e, cx, stride=cy), :] = ye_ref[3]
        conc_ref[pl.ds(col_o, cx, stride=cy), :] = yo_ref[3]
        picked = join3(jnp.dot(hot, split3(conc_ref[...]), preferred_element_type=F32))
        blocks_ref[...] = weight_ref[...] * picked

    def fourth(
        next_hbm, vel_hbm, dif_hbm, con_hbm, height_hbm, dst_hbm,
        hxe, hxo, hye, hyo, exe, exo, eye, eyo, arrived_ref,
        out_hbm, sxe_ref, sxo_ref, sye_ref, syo_ref, cxe_ref, cxo_ref, cye_ref, cyo_ref,
        state_ref, vel_ref, dif_ref, con_ref, height_ref, dst_ref,
        pad_ref, fluid_ref, coef_ref, wall_ref, last_ref, sem,
    ):
        copies = [
            pltpu.make_async_copy(height_hbm, height_ref, sem.at[0]),
            pltpu.make_async_copy(vel_hbm, vel_ref, sem.at[1]),
            pltpu.make_async_copy(dif_hbm, dif_ref, sem.at[2]),
            pltpu.make_async_copy(con_hbm, con_ref, sem.at[3]),
            pltpu.make_async_copy(dst_hbm, dst_ref, sem.at[4]),
            pltpu.make_async_copy(next_hbm, state_ref.at[:, inside[0], inside[1], :], sem.at[5]),
        ]
        start_all(copies)
        row_e, row_o, col_e, col_o = edges_at()
        clear_halo(state_ref, range(4))
        copies[0].wait()
        fluid_ref[...] = row_values(height_ref[...])
        wait_all(copies[1:4])
        fill_pads(pad_ref, vel_ref, dif_ref, con_ref)
        halo = (hxe, hxo, hye, hyo)
        take_halo(pad_ref, 0, 4, *halo, True, False)
        take_halo(pad_ref, 1, 4, *halo, False, True)
        take_halo(pad_ref, 2, 5, *halo, True, True)
        take_halo(pad_ref, 3, 6, *halo, True, True)
        copies[4].wait()
        wall_ref[...] = scatter_blocks(dst_ref[...], arrived_ref[...], cols)
        coefficients(pad_ref, vel_ref, fluid_ref, coef_ref)
        copies[5].wait()
        for k in range(4):
            state_ref[k, row_e + 1, PADY : PADY + cy, :] = exe[k]
            state_ref[k, row_o + 1, PADY : PADY + cy, :] = exo[k]
            for i in range(cx):
                state_ref[k, i + 1, pl.ds(PADY + col_e, 1), :] = eye[k, i : i + 1, :]
                state_ref[k, i + 1, pl.ds(PADY + col_o, 1), :] = eyo[k, i : i + 1, :]
        stencil(state_ref, coef_ref, ((2, wall_ref),), last_ref)
        out = pltpu.make_async_copy(last_ref, out_hbm, sem.at[6])
        out.start()
        tile_e = col_e // 8 * 8
        tile_o = col_o // 8 * 8
        for k in range(4):
            sxe_ref[k] = edge_row(last_ref, k, row_e)
            sxo_ref[k] = edge_row(last_ref, k, row_o)
            for i in range(cx):
                at_e = pl.ds(pl.multiple_of(i * cy + tile_e, 8), 8)
                at_o = pl.ds(pl.multiple_of(i * cy + tile_o, 8), 8)
                sye_ref[k, i] = last_ref[k, at_e, :]
                syo_ref[k, i] = last_ref[k, at_o, :]
        par_x = lax.rem(lax.axis_index("gx"), 2)
        par_y = lax.rem(lax.axis_index("gy"), 2)
        cxe_ref[...] = coef_ref[1 + par_x, pl.ds(pl.multiple_of(row_e * cy, 8), cy), :]
        cxo_ref[...] = coef_ref[2 - par_x, pl.ds(pl.multiple_of(row_o * cy, 8), cy), :]
        cye_ref[...] = edge_col(coef_ref, 3 + par_y, col_e)
        cyo_ref[...] = edge_col(coef_ref, 4 - par_y, col_o)
        out.wait()

    def fifth(
        last_hbm, sxe, sxo, sye, syo, cxe, cxo, cye, cyo, hxe, hxo, hye, hyo,
        out_hbm, txe, txo, tye, tyo, dye, dyo, sem,
    ):
        row_e, row_o, col_e, col_o = edges_at()
        _, _, wrap_x, wrap_y = edge_signs()
        near_e, near_o = cye[...], jnp.where(wrap_y, 0.0, cyo[...])
        tile_e = col_e // 8 * 8
        tile_o = col_o // 8 * 8
        for k in range(4):
            dye[k] = near_e * hye[k]
            dyo[k] = near_o * hyo[k]
            tye[k] = sye[k]
            tyo[k] = syo[k]
            for i in range(1, cx - 1):
                tye[k, i, pl.ds(col_e - tile_e, 1), :] += dye[k, i : i + 1, :]
                tyo[k, i, pl.ds(col_o - tile_o, 1), :] += dyo[k, i : i + 1, :]
        copies = [
            pltpu.make_async_copy(
                strip.at[:, pl.ds(1, cx - 2)],
                out_hbm.at[:, pl.ds(1, cx - 2), pl.ds(pl.multiple_of(tile, 8), 8), :],
                sem.at[n],
            )
            for n, (strip, tile) in enumerate(((tye, tile_e), (tyo, tile_o)))
        ]
        start_all(copies)
        near_e, near_o = cxe[...], jnp.where(wrap_x, 0.0, cxo[...])
        for k in range(4):
            txe[k] = sxe[k] + near_e * hxe[k]
            txo[k] = sxo[k] + near_o * hxo[k]
            for row, out in ((row_e, txe), (row_o, txo)):
                for col, dy in ((col_e, dye), (col_o, dyo)):
                    out[k, pl.ds(col, 1), :] += dy[k, pl.ds(row, 1), :]
        more = [
            pltpu.make_async_copy(strip, out_hbm.at[:, row], sem.at[n])
            for n, (strip, row) in enumerate(((txe, row_e), (txo, row_o)), 2)
        ]
        start_all(more)
        wait_all(copies + more)

    def sds(*shape):
        return jax.ShapeDtypeStruct(shape, F32)

    def vm(*shape, dtype=F32):
        return pltpu.VMEM(shape, dtype)

    def dma(count):
        return pltpu.SemaphoreType.DMA((count,))

    def call(body, name, ins, outs, shapes, scratch, cost, limit=24, **more):
        return pl.pallas_call(
            body,
            name=name,
            out_shape=shapes,
            in_specs=ins,
            out_specs=outs,
            scratch_shapes=scratch,
            compiler_params=pltpu.CompilerParams(vmem_limit_bytes=limit << 20),
            cost_estimate=pl.CostEstimate(flops=cost, bytes_accessed=cost, transcendentals=0),
            **more,
        )

    int_table = vm(owners, cap, dtype=jnp.int32)
    three = [vm(3, cx, cy, 128, dtype=BF16)] + [vm(cx, cy, 128, dtype=BF16)] * 2
    strips = (sds(4, cy, 128), sds(4, cy, 128), sds(4, cx, 128), sds(4, cx, 128))

    def kernels(rcp):
        line = vm(1, rcp, dtype=jnp.int32)
        height = vm(cx, cy, dtype=jnp.int32)
        one = call(
            first, "first", [HBM] * 7, (VMEM,) * 5,
            (sds(slots, 128), sds(7, cy, 128), sds(7, cy, 128), sds(7, cx, 128), sds(7, cx, 128)),
            [vm(4, cols, 128), vm(2, cx, cy, 128, dtype=BF16)] + three[1:]
            + [line, int_table, vm(slots, 128), vm(3, cols, 128), dma(8)],
            4 << 20,
        )
        two = call(
            second, "second", [HBM] * 7 + [VMEM], (HBM,) + (VMEM,) * 5,
            (
                sds(4, cols, 128), sds(cols, 128),
                sds(5, cy, 128), sds(5, cy, 128), sds(5, cx, 128), sds(5, cx, 128),
            ),
            [vm(4, px, py, 128)] + three + [line, height, int_table]
            + [vm(4, px, py, 128), vm(cols, 128), vm(10, cols, 128), vm(cols, 128),
               vm(cols, 128), vm(4, cols, 128), dma(8)],
            8 << 20,
        )
        three_ = call(
            third, "third", [VMEM] * 15, (VMEM,) * 5, (sds(slots, 128),) + strips,
            [vm(cols, 128), vm(4, cy, 128), vm(4, cy, 128), vm(4, cx, 128), vm(4, cx, 128)],
            3 << 20,
        )
        four = call(
            fourth, "fourth", [HBM] * 6 + [VMEM] * 9, (HBM,) + (VMEM,) * 8,
            (sds(4, cols, 128), sds(4, cy, 128), sds(4, cy, 128),
             sds(4, cx, 8, 128), sds(4, cx, 8, 128),
             sds(cy, 128), sds(cy, 128), sds(cx, 128), sds(cx, 128)),
            [vm(4, px, py, 128)] + three + [height, int_table]
            + [vm(4, px, py, 128), vm(cols, 128), vm(10, cols, 128), vm(cols, 128),
               vm(4, cols, 128), dma(7)],
            8 << 20,
        )
        five = call(
            fifth, "fifth", [HBM] + [VMEM] * 12, HBM, sds(4, cx, cy, 128),
            [vm(4, cy, 128), vm(4, cy, 128), vm(4, cx, 8, 128), vm(4, cx, 8, 128),
             vm(4, cx, 128), vm(4, cx, 128), dma(4)],
            2 << 20,
            input_output_aliases={0: 0},
        )
        return one, two, three_, four, five

    return kernels


def shards(
    adjoint, velocity, diffusivity, concentration, heights, receptors, face_src, face_dst, face_coef
):
    nx, ny = lax.axis_size("gx"), lax.axis_size("gy")
    cx, cy, levels = adjoint.shape[1:]
    owners, cap = face_src.shape[2:]
    kernels = make_kernels(nx, ny, cx, cy, owners, cap)
    first, second, third, fourth, fifth = kernels(receptors.shape[2])

    def pairs(count):
        even = [(i, i ^ 1) for i in range(count)]
        odd = [(i, (i + 1) % count) for i in range(1, count, 2)]
        return even, odd + [(j, i) for i, j in odd]

    x_even, x_odd = pairs(nx)
    y_even, y_odd = pairs(ny)

    def exchange(xe, xo, ye, yo):
        yo = lax.ppermute(yo, "gy", y_odd)
        xo = lax.ppermute(xo, "gx", x_odd)
        xe = lax.ppermute(xe, "gx", x_even)
        ye = lax.ppermute(ye, "gy", y_even)
        return xe, xo, ye, yo

    def deliver(blocks):
        sent = blocks.reshape(owners, cap, levels)
        got = lax.all_to_all(sent, "gx", split_axis=0, concat_axis=0, tiled=True)
        return got.reshape(owners * cap, levels)

    src = face_src.reshape(owners, cap)
    dst = face_dst.reshape(owners, cap)
    weight = face_coef.reshape(owners * cap, levels)
    line = receptors.reshape(1, -1)
    flat = adjoint.reshape(4, cx * cy, levels)
    pinned = [
        pltpu.with_memory_space_constraint(x, pltpu.HBM)
        for x in (flat, velocity, diffusivity, concentration, line, src, weight)
    ]
    blocks, *own = first(*pinned)
    arrived = deliver(blocks)
    halos = exchange(*own)
    inner, conc, *part = second(
        adjoint, velocity, diffusivity, concentration, line, heights, dst, arrived
    )
    blocks, *edges = third(conc, *own, *halos, *part, src, weight)
    arrived = deliver(blocks)
    later = exchange(*edges)
    last, *strips = fourth(
        inner.reshape(4, cx, cy, levels), velocity, diffusivity, concentration, heights, dst,
        *halos, *edges, arrived,
    )
    return fifth(last.reshape(4, cx, cy, levels), *strips, *later)


def solution(mesh):
    placed = (
        P(None, "gx", "gy", None),
        P(None, "gx", "gy", None),
        P("gx", "gy", None),
        P("gx", "gy", None),
        P("gx", "gy"),
        P("gx", "gy", None),
        P("gx", "gy", None, None),
        P("gx", "gy", None, None),
        P("gx", "gy", None, None, None),
    )
    return jax.shard_map(
        shards, mesh=mesh, in_specs=placed, out_specs=P(None, "gx", "gy", None), check_vma=False
    )
```

time: 98.8 us -> 50.1 us (0.51)
  the two profiles are of different devices: /device:TPU:10 before, /device:TPU:8 now
where the time goes in v1:
time: 50.1 us; the launch traced here: 49.7 us
  starting transfers between devices  31.8 us (63%)
  Pallas kernels  16.3 us (33%)
  local copies, waits for them, and re-layouts  1.28 us (3%)
    all_to_all x2, starting transfers between devices, deliver(): got = lax.all_to_all(sent, 'gx', split_axis=0, concat_axis=0, tiled=True)  15.5 us
    ppermute x2, starting transfers between devices, exchange(): yo = lax.ppermute(yo, 'gy', y_odd)  7.94 us
    pallas_call x1, Pallas kernels, shards(): fourth(inner.reshape(4, cx, cy, levels), velocity, diffusivity, concentra...  5.84 us
    ppermute x2, starting transfers between devices, exchange(): xo = lax.ppermute(xo, 'gx', x_odd)  5.32 us
    pallas_call x1, Pallas kernels, shards(): second(adjoint, velocity, diffusivity, concentration, line, heights, dst,...  5.12 us
    ppermute x2, starting transfers between devices, exchange(): xe = lax.ppermute(xe, 'gx', x_even)  3.02 us
    pallas_call x1, Pallas kernels, shards(): blocks, *own = first(*pinned)  2.4 us
    pallas_call x1, Pallas kernels, shards(): blocks, *edges = third(conc, *own, *halos, *part, src, weight)  1.98 us
  transfers between devices with their start and end apart: 10, of which 1 were waited for; matrix products, arithmetic and copies ran while one was open for 0% of the time, Pallas kernels for 22%

profile of v1, /device:TPU:8, one launch (start us, length us, event | category | flops | bytes accessed | tf_op | source)
XLA Modules:
  0.0 49.7 jit_solution(8894896378570279164)
XLA Ops:
  0.0 0.0 copy-start
  0.0 0.0 copy-start.1
  0.0 0.0 copy-start.7
  0.0 2.4 %first.1 = (f32[256,128]{1,0:T(8,128)}, f32[7,32,128]{2,1,0:T(8,128)S(1)}, f32[7,32,128]{2,1,0:T(8,128)S(1)}, f32[7,16,128]{2,1,0:T(8,128)S(1)}, f32[7,16,128]{2,1,0:T(8,128)}) custom-call(f32[4,512,128]{2,1,0:T(8,128)} %bitcast.11, bf16[3,16,32,128]{3,2,1,0:T(8,128)(2,1)} %vel_hbm.5, bf16[16,32,128]{2,1,0:T(8,128)(2,1)} %dif_hbm.5, ...), custom_call_target="tpu_custom_call" | custom-call | flops 4194304 | bytes 4194304 | tf_op jit(solution)/shard_map/first/pallas_call | solution.py:581
  2.4 0.0 copy-start.2
  2.4 0.0 copy-start.3
  2.4 10.1 %all-to-all-start = ((f32[16,16,128]{2,1,0:T(8,128)}), f32[16,16,128]{2,1,0:T(8,128)S(1)}, u32[]{:S(2)}, u32[]{:S(2)}) async-start(f32[16,16,128]{2,1,0:T(8,128)} %bitcast.5), calls=%async_computation | async-start | bytes 262144 | tf_op jit(solution)/shard_map/all_to_all | solution.py:569
  12.5 0.0 copy-start.6
  12.5 1.6 %collective-permute-start = (f32[7,32,128]{2,1,0:T(8,128)S(1)}, f32[7,32,128]{2,1,0:T(8,128)S(1)}, u32[]{:S(2)}, u32[]{:S(2)}) collective-permute-start(f32[7,32,128]{2,1,0:T(8,128)S(1)} %get-tuple-element.32.oxe), channel_id=1, source_target_pairs={{0,16},{16,0},{32,48},{48,32},{64,80},{80,64},{96,112},{112,96},{1... | collective-permute-start | bytes 344072 | tf_op jit(solution)/shard_map/ppermute | solution.py:563
  14.1 2.7 %collective-permute-start.1 = (f32[7,32,128]{2,1,0:T(8,128)S(1)}, f32[7,32,128]{2,1,0:T(8,128)S(1)}, u32[]{:S(2)}, u32[]{:S(2)}) collective-permute-start(f32[7,32,128]{2,1,0:T(8,128)S(1)} %get-tuple-element.33.oxo), channel_id=1, source_target_pairs={{16,32},{48,64},{80,96},{112,128},{144,160},{176,192},{208,224},{2... | collective-permute-start | bytes 344072 | tf_op jit(solution)/shard_map/ppermute | solution.py:562
  16.8 0.0 collective-permute-start.2
  16.8 4.6 %collective-permute-start.3 = (f32[7,16,128]{2,1,0:T(8,128)}, f32[7,16,128]{2,1,0:T(8,128)S(1)}, u32[]{:S(2)}, u32[]{:S(2)}) collective-permute-start(f32[7,16,128]{2,1,0:T(8,128)} %get-tuple-element.35.oyo), channel_id=1, source_target_pairs={{1,2},{3,4},{5,6},{7,8},{9,10},{11,12},{13,14},{15,0},{2,1},{4,3},... | collective-permute-start | bytes 172040 | tf_op jit(solution)/shard_map/ppermute | solution.py:561
  21.4 0.0 all-to-all-done
  21.4 0.0 copy-start.8
  21.4 0.0 copy-done
  21.4 0.0 copy-done.1
  21.4 0.0 copy-done.7
  21.4 0.0 copy-done.2
  21.4 0.0 copy-done.3
  21.4 0.0 copy-done.6
  21.4 0.6 %copy-done.8 = s32[1,1,64]{2,1,0:T(1,128)S(1)} copy-done((s32[1,1,64]{2,1,0:T(1,128)S(1)}, s32[1,1,64]{2,1,0:T(1,128)}, u32[]{:S(2)}) %copy-start.8) | copy-done | bytes 280
  22.0 0.0 copy-start.4
  22.0 5.1 %second.1 = (f32[4,512,128]{2,1,0:T(8,128)S(1)}, f32[512,128]{1,0:T(8,128)S(1)}, f32[5,32,128]{2,1,0:T(8,128)S(1)}, f32[5,32,128]{2,1,0:T(8,128)S(1)}, f32[5,16,...) custom-call(f32[4,16,32,128]{3,2,1,0:T(8,128)S(1)} %copy-done, bf16[3,16,32,128]{3,2,1,0:T(8,128)(2,1)S(1)} %copy-done.1, ...), custom_call_target="tpu_custom_call" | custom-call | flops 8388608 | bytes 8388608 | tf_op jit(solution)/shard_map/second/pallas_call | solution.py:584
  27.2 0.0 copy-start.5
  27.2 0.0 collective-permute-done.2.hye
  27.2 0.0 collective-permute-done.3.hyo
  27.2 0.0 collective-permute-done.hxe
  27.2 0.0 collective-permute-done.1.hxo
  27.2 0.0 copy-done.4
  27.2 0.6 %copy-done.5 = s32[1,1,16,16]{3,2,1,0:T(8,128)S(1)} copy-done((s32[1,1,16,16]{3,2,1,0:T(8,128)S(1)}, s32[1,1,16,16]{3,2,1,0:T(8,128)}, u32[]{:S(2)}) %copy-start.5) | copy-done | bytes 1048
  27.9 2.0 %third.1 = (f32[256,128]{1,0:T(8,128)}, f32[4,32,128]{2,1,0:T(8,128)S(1)}, f32[4,32,128]{2,1,0:T(8,128)S(1)}, f32[4,16,128]{2,1,0:T(8,128)S(1)}, f32[4,16,128]{2,1,0:T(8,128)S(1)}) custom-call(f32[512,128]{1,0:T(8,128)S(1)} %get-tuple-element.36.conc_in, f32[7,32,128]{2,1,0:T(8,128)S(1)} %get-tuple-element.32.oxe, f32[7,32,128]{2,1,0:T(8,128)S(1)} %get-tuple-element.33.oxo, ...), custom_call_target="tpu_custom_call" | custom-call | flops 3145728 | bytes 3145728 | tf_op jit(solution)/shard_map/third/pallas_call | solution.py:587
  29.8 5.4 %all-to-all-start.1 = ((f32[16,16,128]{2,1,0:T(8,128)}), f32[16,16,128]{2,1,0:T(8,128)S(1)}, u32[]{:S(2)}, u32[]{:S(2)}) async-start(f32[16,16,128]{2,1,0:T(8,128)} %bitcast.8), calls=%async_computation.1 | async-start | bytes 262144 | tf_op jit(solution)/shard_map/all_to_all | solution.py:569
  35.3 1.5 %collective-permute-start.4 = (f32[4,32,128]{2,1,0:T(8,128)S(1)}, f32[4,32,128]{2,1,0:T(8,128)S(1)}, u32[]{:S(2)}, u32[]{:S(2)}) collective-permute-start(f32[4,32,128]{2,1,0:T(8,128)S(1)} %get-tuple-element.41.exe), channel_id=1, source_target_pairs={{0,16},{16,0},{32,48},{48,32},{64,80},{80,64},{96,112},{112,96},{1... | collective-permute-start | bytes 196616 | tf_op jit(solution)/shard_map/ppermute | solution.py:563
  36.7 2.7 %collective-permute-start.5 = (f32[4,32,128]{2,1,0:T(8,128)S(1)}, f32[4,32,128]{2,1,0:T(8,128)S(1)}, u32[]{:S(2)}, u32[]{:S(2)}) collective-permute-start(f32[4,32,128]{2,1,0:T(8,128)S(1)} %get-tuple-element.42.exo), channel_id=1, source_target_pairs={{16,32},{48,64},{80,96},{112,128},{144,160},{176,192},{208,224},{2... | collective-permute-start | bytes 196616 | tf_op jit(solution)/shard_map/ppermute | solution.py:562
  39.4 0.0 collective-permute-start.6
  39.4 3.3 %collective-permute-start.7 = (f32[4,16,128]{2,1,0:T(8,128)S(1)}, f32[4,16,128]{2,1,0:T(8,128)S(1)}, u32[]{:S(2)}, u32[]{:S(2)}) collective-permute-start(f32[4,16,128]{2,1,0:T(8,128)S(1)} %get-tuple-element.44.eyo), channel_id=1, source_target_pairs={{1,2},{3,4},{5,6},{7,8},{9,10},{11,12},{13,14},{15,0},{2,1},{4,3},... | collective-permute-start | bytes 98312 | tf_op jit(solution)/shard_map/ppermute | solution.py:561
  42.7 0.2 all-to-all-done.1
  42.9 5.8 %fourth.1 = (f32[4,512,128]{2,1,0:T(8,128)}, f32[4,32,128]{2,1,0:T(8,128)S(1)}, f32[4,32,128]{2,1,0:T(8,128)S(1)}, f32[4,16,8,128]{3,2,1,0:T(8,128)S(1)}, f32[4,...) custom-call(f32[4,16,32,128]{3,2,1,0:T(8,128)S(1)} %bitcast.12, ...), custom_call_target="tpu_custom_call" | custom-call | flops 8388608 | bytes 8388608 | tf_op jit(solution)/shard_map/fourth/pallas_call | solution.py:590
  48.8 0.0 collective-permute-done.6.hye
  48.8 0.0 collective-permute-done.7.hyo
  48.8 0.0 collective-permute-done.4.hxe
  48.8 0.0 collective-permute-done.5.hxo
  48.8 0.9 %fifth.1 = f32[4,16,32,128]{3,2,1,0:T(8,128)} custom-call(f32[4,16,32,128]{3,2,1,0:T(8,128)} %bitcast.23, f32[4,32,128]{2,1,0:T(8,128)S(1)} %get-tuple-element.47.sxe, f32[4,32,128]{2,1,0:T(8,128)S(1)} %get-tuple-element.48.sxo, f32[4,16,8,128]{3,2,1,0:T(8,128)S(1)} %get-tuple-element.49.sye, ...), custom_call_target="tpu_custom_call", output_to_operand_aliasing={{}: (0, {})} | custom-call | flops 2097152 | bytes 2097152 | tf_op jit(solution)/shard_map/fifth/pallas_call | solution.py:594
Async XLA Ops:
  0.0 21.4 %copy-start = (f32[4,16,32,128]{3,2,1,0:T(8,128)S(1)}, f32[4,16,32,128]{3,2,1,0:T(8,128)}, u32[]{:S(2)}) copy-start(f32[4,16,32,128]{3,2,1,0:T(8,128)} %adj_hbm.1) | copy-start | bytes 3145732
  0.0 21.4 %copy-start.1 = (bf16[3,16,32,128]{3,2,1,0:T(8,128)(2,1)S(1)}, bf16[3,16,32,128]{3,2,1,0:T(8,128)(2,1)}, u32[]{:S(2)}) copy-start(bf16[3,16,32,128]{3,2,1,0:T(8,128)(2,1)} %vel_hbm.5) | copy-start | bytes 1179652
  0.0 21.4 %copy-start.7 = (s32[1,1,16,16]{3,2,1,0:T(8,128)S(1)}, s32[1,1,16,16]{3,2,1,0:T(8,128)}, u32[]{:S(2)}) copy-start(s32[1,1,16,16]{3,2,1,0:T(8,128)} %param.16) | copy-start | bytes 3076
  2.4 19.0 %copy-start.2 = (bf16[16,32,128]{2,1,0:T(8,128)(2,1)S(1)}, bf16[16,32,128]{2,1,0:T(8,128)(2,1)}, u32[]{:S(2)}) copy-start(bf16[16,32,128]{2,1,0:T(8,128)(2,1)} %dif_hbm.5) | copy-start | bytes 393220
  2.4 19.0 %copy-start.3 = (bf16[16,32,128]{2,1,0:T(8,128)(2,1)S(1)}, bf16[16,32,128]{2,1,0:T(8,128)(2,1)}, u32[]{:S(2)}) copy-start(bf16[16,32,128]{2,1,0:T(8,128)(2,1)} %con_hbm.5) | copy-start | bytes 393220
  2.4 18.9 %all-to-all-start = ((f32[16,16,128]{2,1,0:T(8,128)}), f32[16,16,128]{2,1,0:T(8,128)S(1)}, u32[]{:S(2)}, u32[]{:S(2)}) async-start(f32[16,16,128]{2,1,0:T(8,128)} %bitcast.5), calls=%async_computation | async-start | bytes 262144 | tf_op jit(solution)/shard_map/all_to_all | solution.py:569
  12.5 8.9 %copy-start.6 = (s32[16,32]{1,0:T(8,128)S(1)}, s32[16,32]{1,0:T(8,128)}, u32[]{:S(2)}) copy-start(s32[16,32]{1,0:T(8,128)} %height_hbm.3) | copy-start | bytes 6148
  12.5 14.7 %collective-permute-start = (f32[7,32,128]{2,1,0:T(8,128)S(1)}, f32[7,32,128]{2,1,0:T(8,128)S(1)}, u32[]{:S(2)}, u32[]{:S(2)}) collective-permute-start(f32[7,32,128]{2,1,0:T(8,128)S(1)} %get-tuple-element.32.oxe), channel_id=1, source_target_pairs={{0,16},{16,0},{32,48},{48,32},{64,80},{80,64},{96,112},{112,96},{1... | collective-permute-start | bytes 344072 | tf_op jit(solution)/shard_map/ppermute | solution.py:563
  14.1 13.1 %collective-permute-start.1 = (f32[7,32,128]{2,1,0:T(8,128)S(1)}, f32[7,32,128]{2,1,0:T(8,128)S(1)}, u32[]{:S(2)}, u32[]{:S(2)}) collective-permute-start(f32[7,32,128]{2,1,0:T(8,128)S(1)} %get-tuple-element.33.oxo), channel_id=1, source_target_pairs={{16,32},{48,64},{80,96},{112,128},{144,160},{176,192},{208,224},{2... | collective-permute-start | bytes 344072 | tf_op jit(solution)/shard_map/ppermute | solution.py:562
  16.8 10.4 %collective-permute-start.2 = (f32[7,16,128]{2,1,0:T(8,128)S(1)}, f32[7,16,128]{2,1,0:T(8,128)S(1)}, u32[]{:S(2)}, u32[]{:S(2)}) collective-permute-start(f32[7,16,128]{2,1,0:T(8,128)S(1)} %get-tuple-element.34.oye), channel_id=1, source_target_pairs={{0,1},{1,0},{2,3},{3,2},{4,5},{5,4},{6,7},{7,6},{8,9},{9,8},{10,11... | collective-permute-start | bytes 172040 | tf_op jit(solution)/shard_map/ppermute | solution.py:564
  16.8 10.4 %collective-permute-start.3 = (f32[7,16,128]{2,1,0:T(8,128)}, f32[7,16,128]{2,1,0:T(8,128)S(1)}, u32[]{:S(2)}, u32[]{:S(2)}) collective-permute-start(f32[7,16,128]{2,1,0:T(8,128)} %get-tuple-element.35.oyo), channel_id=1, source_target_pairs={{1,2},{3,4},{5,6},{7,8},{9,10},{11,12},{13,14},{15,0},{2,1},{4,3},... | collective-permute-start | bytes 172040 | tf_op jit(solution)/shard_map/ppermute | solution.py:561
  21.4 0.7 %copy-start.8 = (s32[1,1,64]{2,1,0:T(1,128)S(1)}, s32[1,1,64]{2,1,0:T(1,128)}, u32[]{:S(2)}) copy-start(s32[1,1,64]{2,1,0:T(1,128)} %param.14) | copy-start | bytes 772
  22.0 5.2 %copy-start.4 = (f32[1,1,16,16,128]{4,3,2,1,0:T(8,128)S(1)}, f32[1,1,16,16,128]{4,3,2,1,0:T(8,128)}, u32[]{:S(2)}) copy-start(f32[1,1,16,16,128]{4,3,2,1,0:T(8,128)} %param.17) | copy-start | bytes 393220
  27.2 0.7 %copy-start.5 = (s32[1,1,16,16]{3,2,1,0:T(8,128)S(1)}, s32[1,1,16,16]{3,2,1,0:T(8,128)}, u32[]{:S(2)}) copy-start(s32[1,1,16,16]{3,2,1,0:T(8,128)} %param.15) | copy-start | bytes 3076
  29.8 13.1 %all-to-all-start.1 = ((f32[16,16,128]{2,1,0:T(8,128)}), f32[16,16,128]{2,1,0:T(8,128)S(1)}, u32[]{:S(2)}, u32[]{:S(2)}) async-start(f32[16,16,128]{2,1,0:T(8,128)} %bitcast.8), calls=%async_computation.1 | async-start | bytes 262144 | tf_op jit(solution)/shard_map/all_to_all | solution.py:569
  35.3 13.5 %collective-permute-start.4 = (f32[4,32,128]{2,1,0:T(8,128)S(1)}, f32[4,32,128]{2,1,0:T(8,128)S(1)}, u32[]{:S(2)}, u32[]{:S(2)}) collective-permute-start(f32[4,32,128]{2,1,0:T(8,128)S(1)} %get-tuple-element.41.exe), channel_id=1, source_target_pairs={{0,16},{16,0},{32,48},{48,32},{64,80},{80,64},{96,112},{112,96},{1... | collective-permute-start | bytes 196616 | tf_op jit(solution)/shard_map/ppermute | solution.py:563
  36.7 12.1 %collective-permute-start.5 = (f32[4,32,128]{2,1,0:T(8,128)S(1)}, f32[4,32,128]{2,1,0:T(8,128)S(1)}, u32[]{:S(2)}, u32[]{:S(2)}) collective-permute-start(f32[4,32,128]{2,1,0:T(8,128)S(1)} %get-tuple-element.42.exo), channel_id=1, source_target_pairs={{16,32},{48,64},{80,96},{112,128},{144,160},{176,192},{208,224},{2... | collective-permute-start | bytes 196616 | tf_op jit(solution)/shard_map/ppermute | solution.py:562
  39.4 9.4 %collective-permute-start.6 = (f32[4,16,128]{2,1,0:T(8,128)S(1)}, f32[4,16,128]{2,1,0:T(8,128)S(1)}, u32[]{:S(2)}, u32[]{:S(2)}) collective-permute-start(f32[4,16,128]{2,1,0:T(8,128)S(1)} %get-tuple-element.43.eye), channel_id=1, source_target_pairs={{0,1},{1,0},{2,3},{3,2},{4,5},{5,4},{6,7},{7,6},{8,9},{9,8},{10,11... | collective-permute-start | bytes 98312 | tf_op jit(solution)/shard_map/ppermute | solution.py:564
  39.4 9.4 %collective-permute-start.7 = (f32[4,16,128]{2,1,0:T(8,128)S(1)}, f32[4,16,128]{2,1,0:T(8,128)S(1)}, u32[]{:S(2)}, u32[]{:S(2)}) collective-permute-start(f32[4,16,128]{2,1,0:T(8,128)S(1)} %get-tuple-element.44.eyo), channel_id=1, source_target_pairs={{1,2},{3,4},{5,6},{7,8},{9,10},{11,12},{13,14},{15,0},{2,1},{4,3},... | collective-permute-start | bytes 98312 | tf_op jit(solution)/shard_map/ppermute | solution.py:561

commit v2 on v1

v2 whole, which is shorter than its diff:
```python
import jax
import jax.numpy as jnp
from jax import lax
from jax.experimental import pallas as pl
from jax.experimental.pallas import tpu as pltpu
from jax.sharding import PartitionSpec as P

F32 = jnp.float32
BF16 = jnp.bfloat16
PADY = 8
VMEM = pl.BlockSpec(memory_space=pltpu.VMEM)
HBM = pl.BlockSpec(memory_space=pltpu.HBM)


def split3(x):
    hi = x.astype(BF16)
    rest = x - hi.astype(F32)
    mid = rest.astype(BF16)
    low = (rest - mid.astype(F32)).astype(BF16)
    return jnp.concatenate([hi, mid, low], axis=1)


def join3(x):
    return x[:, :128] + x[:, 128:256] + x[:, 256:384]


def row_values(table):
    n = table.shape[1]
    eye = lax.broadcasted_iota(jnp.int32, (n, n), 0) == lax.broadcasted_iota(jnp.int32, (n, n), 1)
    high = table >> 4
    low = table & 15
    ones = jnp.ones((n, 128), BF16)
    total = None
    for part in (high * 16, low):
        part = part.astype(F32)
        rows = [
            jnp.where(eye, jnp.broadcast_to(part[d : d + 1], (n, n)), 0.0)
            for d in range(table.shape[0])
        ]
        spread = jnp.concatenate(rows, axis=0).astype(BF16)
        value = jnp.dot(spread, ones, preferred_element_type=F32)
        total = value if total is None else total + value
    return total


def select_cols(table, cols):
    d_count, n = table.shape
    slots = d_count * n
    tile = (
        lax.broadcasted_iota(jnp.int32, (n, slots), 1) % n
        == lax.broadcasted_iota(jnp.int32, (n, slots), 0)
    ).astype(F32).astype(BF16)
    mine = (
        lax.broadcasted_iota(jnp.int32, (d_count, slots), 1) // n
        == lax.broadcasted_iota(jnp.int32, (d_count, slots), 0)
    )
    high = ((table >> 4) * 16).astype(F32).astype(BF16)
    low = (table & 15).astype(F32).astype(BF16)
    value = jnp.dot(high, tile, preferred_element_type=F32) + jnp.dot(
        low, tile, preferred_element_type=F32
    )
    line = jnp.sum(jnp.where(mine, value, 0.0), axis=0, keepdims=True).astype(jnp.int32)
    col = lax.broadcasted_iota(jnp.int32, (cols, slots), 0)
    return (col == line).astype(F32).astype(BF16)


def receptor_counts(line, cols):
    entries = line.shape[1]
    col = lax.broadcasted_iota(jnp.int32, (cols, entries), 0)
    level = lax.broadcasted_iota(jnp.int32, (128, entries), 0)
    hot_col = (col == (line >> 7)).astype(F32).astype(BF16)
    hot_level = (level == (line & 127)).astype(F32).astype(BF16)
    return lax.dot_general(
        hot_col, hot_level, (((1,), (1,)), ((), ())), preferred_element_type=F32
    )


def make_kernels(nx, ny, cx, cy, owners, cap):
    cols = cx * cy
    slots = owners * cap
    px, py = cx + 2, cy + 2 * PADY
    inside = (pl.ds(1, cx), pl.ds(PADY, cy))

    def edges_at():
        par_x = lax.rem(lax.axis_index("gx"), 2)
        par_y = lax.rem(lax.axis_index("gy"), 2)
        return (
            (cx - 1) * (1 - par_x), (cx - 1) * par_x,
            (cy - 1) * (1 - par_y), (cy - 1) * par_y,
        )

    def start_all(copies):
        for copy in copies:
            copy.start()

    def wait_all(copies):
        for copy in copies:
            copy.wait()

    def clear_halo(pad_ref, planes):
        zero = jnp.zeros((px, PADY, 128), F32)
        row = jnp.zeros((cy, 128), F32)
        for k in planes:
            pad_ref[k, :, 0:PADY, :] = zero
            pad_ref[k, :, PADY + cy : py, :] = zero
            pad_ref[k, 0, PADY : PADY + cy, :] = row
            pad_ref[k, cx + 1, PADY : PADY + cy, :] = row

    def take_halo(pad_ref, plane, n, xe_ref, xo_ref, ye_ref, yo_ref, with_x, with_y):
        me_x, me_y = lax.axis_index("gx"), lax.axis_index("gy")
        par_x, par_y = lax.rem(me_x, 2), lax.rem(me_y, 2)
        if with_x:
            e, o = xe_ref[n], xo_ref[n]
            before = jnp.where(par_x == 0, o, e)
            after = jnp.where(par_x == 0, e, o)
            pad_ref[plane, 0, PADY : PADY + cy, :] = jnp.where(me_x == 0, 0.0, before)
            pad_ref[plane, cx + 1, PADY : PADY + cy, :] = jnp.where(me_x == nx - 1, 0.0, after)
        if with_y:
            e, o = ye_ref[n], yo_ref[n]
            before = jnp.where(me_y == 0, 0.0, jnp.where(par_y == 0, o, e))
            after = jnp.where(me_y == ny - 1, 0.0, jnp.where(par_y == 0, e, o))
            for i in range(cx):
                pad_ref[plane, i + 1, PADY - 1 : PADY, :] = before[i : i + 1]
                pad_ref[plane, i + 1, PADY + cy : PADY + cy + 1, :] = after[i : i + 1]

    def fill_pads(pad_ref, vel_ref, dif_ref, con_ref=None):
        pad_ref[0, 1 : cx + 1, PADY : PADY + cy, :] = vel_ref[0].astype(F32)
        pad_ref[1, 1 : cx + 1, PADY : PADY + cy, :] = vel_ref[1].astype(F32)
        pad_ref[2, 1 : cx + 1, PADY : PADY + cy, :] = dif_ref[...].astype(F32)
        if con_ref is not None:
            pad_ref[3, 1 : cx + 1, PADY : PADY + cy, :] = con_ref[...].astype(F32)

    def cell_coefficients(i, jv, uz, pad_ref, fluid_ref):
        lane = lax.broadcasted_iota(jnp.int32, (8, 128), 1)
        top = lane == 127
        bottom = lane == 0

        def up(x):
            return jnp.where(top, 0.0, pltpu.roll(x, 127, axis=1))

        def down(x):
            return jnp.where(bottom, 0.0, pltpu.roll(x, 1, axis=1))

        j = PADY + 8 * jv
        at = pl.ds(i * cy + 8 * jv, 8)
        fluid = (lane.astype(F32) >= fluid_ref[at, :]).astype(F32)
        e = 0.05 * fluid
        k0 = pad_ref[2, i + 1, j : j + 8, :]
        ends = None
        out = [None]
        for plane, sign, a, b in (
            (0, 1.0, i + 2, j), (0, -1.0, i, j), (1, 1.0, i + 1, j + 1), (1, -1.0, i + 1, j - 1),
        ):
            kn = k0 + pad_ref[2, a, b : b + 8, :]
            un = pad_ref[plane, a, b : b + 8, :]
            out.append(e * (kn + un if sign > 0 else kn - un))
            ends = kn if ends is None else ends + kn
        kn = k0 + up(k0)
        ends = ends + kn
        out.append(jnp.where(top, 0.0, e * (kn + up(uz))))
        kn = k0 + down(k0)
        ends = ends + kn
        out.append(jnp.where(bottom, 0.0, e * (kn - down(uz))))
        out[0] = fluid - e * ends
        return out, e

    def cell_gradients(i, jv, e, pad_ref):
        lane = lax.broadcasted_iota(jnp.int32, (8, 128), 1)
        j = PADY + 8 * jv
        c0 = pad_ref[3, i + 1, j : j + 8, :]
        above = jnp.where(lane == 127, 0.0, pltpu.roll(c0, 127, axis=1))
        below = jnp.where(lane == 0, 0.0, pltpu.roll(c0, 1, axis=1))
        return [
            e * (pad_ref[3, i + 2, j : j + 8, :] - pad_ref[3, i, j : j + 8, :]),
            e * (pad_ref[3, i + 1, j + 1 : j + 9, :] - pad_ref[3, i + 1, j - 1 : j + 7, :]),
            e * (above - below),
        ]

    def cells():
        return [(i, jv) for i in range(cx) for jv in range(cy // 8)]

    def vertical(vel_ref, i, jv):
        pair = vel_ref[2, i, 16 * (jv // 2) : 16 * (jv // 2) + 16, :].astype(F32)
        return pair[8 * (jv % 2) : 8 * (jv % 2) + 8]

    def cell_step(i, jv, c, state_ref, k):
        j = PADY + 8 * jv
        f = state_ref[k, i + 1, j : j + 8, :]
        value = c[0] * f
        value = value + c[1] * state_ref[k, i + 2, j : j + 8, :]
        value = value + c[2] * state_ref[k, i, j : j + 8, :]
        value = value + c[3] * state_ref[k, i + 1, j + 1 : j + 9, :]
        value = value + c[4] * state_ref[k, i + 1, j - 1 : j + 7, :]
        value = value + c[5] * pltpu.roll(f, 127, axis=1)
        value = value + c[6] * pltpu.roll(f, 1, axis=1)
        return value

    def edge_row(ref, k, row):
        return ref[k, pl.ds(pl.multiple_of(row * cy, 8), cy), :]

    def edge_col(ref, k, col):
        return ref[k, pl.ds(col, cx, stride=cy), :]

    def first(
        adj_hbm, vel_hbm, dif_hbm, con_hbm, rec_hbm,
        xe_ref, xo_ref, ye_ref, yo_ref,
        adj_ref, vel_ref, dif_ref, con_ref, rec_ref, side_ref, sem,
    ):
        copies = [
            pltpu.make_async_copy(rec_hbm, rec_ref, sem.at[0]),
            pltpu.make_async_copy(vel_hbm.at[pl.ds(0, 2)], vel_ref, sem.at[1]),
            pltpu.make_async_copy(dif_hbm, dif_ref, sem.at[2]),
            pltpu.make_async_copy(con_hbm, con_ref, sem.at[3]),
            pltpu.make_async_copy(adj_hbm, adj_ref, sem.at[4]),
        ]
        start_all(copies)
        row_e, row_o, col_e, col_o = edges_at()
        copies[0].wait()
        counts = receptor_counts(rec_ref[...], cols)
        wait_all(copies[1:4])
        side_ref[0] = vel_ref[1].astype(F32).reshape(cols, 128)
        side_ref[1] = dif_ref[...].astype(F32).reshape(cols, 128)
        side_ref[2] = con_ref[...].astype(F32).reshape(cols, 128)
        for row, out in ((row_e, xe_ref), (row_o, xo_ref)):
            out[4] = vel_ref[0, row].astype(F32)
            out[5] = dif_ref[row].astype(F32)
            out[6] = con_ref[row].astype(F32)
        for col, out in ((col_e, ye_ref), (col_o, yo_ref)):
            for k in range(3):
                out[4 + k] = edge_col(side_ref, k, col)
        copies[4].wait()
        adj_ref[3] += counts
        for k in range(4):
            xe_ref[k] = edge_row(adj_ref, k, row_e)
            xo_ref[k] = edge_row(adj_ref, k, row_o)
            ye_ref[k] = edge_col(adj_ref, k, col_e)
            yo_ref[k] = edge_col(adj_ref, k, col_o)

    def second(
        adj_hbm, vel_hbm, dif_hbm, rec_hbm, height_hbm, src_hbm, weight_hbm,
        now_ref, soon_ref, hot_ref, weight_ref, exe_ref, exo_ref, eye_ref, eyo_ref,
        state_ref, vel_ref, dif_ref, rec_ref, height_ref, src_ref,
        pad_ref, fluid_ref, count_ref, next_ref, sem,
    ):
        copies = [
            pltpu.make_async_copy(src_hbm, src_ref, sem.at[0]),
            pltpu.make_async_copy(height_hbm, height_ref, sem.at[1]),
            pltpu.make_async_copy(rec_hbm, rec_ref, sem.at[2]),
            pltpu.make_async_copy(dif_hbm, dif_ref, sem.at[3]),
            pltpu.make_async_copy(
                adj_hbm.at[3], state_ref.at[0, inside[0], inside[1], :], sem.at[4]
            ),
            pltpu.make_async_copy(vel_hbm, vel_ref, sem.at[5]),
            pltpu.make_async_copy(weight_hbm, weight_ref, sem.at[6]),
        ]
        start_all(copies)
        row_e, row_o, col_e, col_o = edges_at()
        clear_halo(pad_ref, range(3))
        clear_halo(state_ref, range(1))
        copies[0].wait()
        index = row_values(src_ref[...]).astype(jnp.int32)
        copies[1].wait()
        fluid_ref[...] = row_values(height_ref[...])
        copies[2].wait()
        count_ref[...] = receptor_counts(rec_ref[...], cols)
        wait_all(copies[3:6])
        fill_pads(pad_ref, vel_ref, dif_ref)
        state_ref[0, 1 : cx + 1, PADY : PADY + cy, :] += count_ref[...].reshape(cx, cy, 128)
        for i, jv in cells():
            at = pl.ds(i * cy + 8 * jv, 8)
            c, e = cell_coefficients(i, jv, vertical(vel_ref, i, jv), pad_ref, fluid_ref)
            fluid_ref[at, :] = e
            next_ref[at, :] = cell_step(i, jv, c, state_ref, 0) + count_ref[at, :]
        lane = lax.broadcasted_iota(jnp.int32, index.shape, 1)
        i, j = index // cy, index % cy
        near = jnp.logical_or(
            jnp.logical_or(
                jnp.logical_and(i == row_e, j == lane),
                jnp.logical_and(i == row_o, j + cy == lane),
            ),
            jnp.logical_or(
                jnp.logical_and(j == col_e, i + 2 * cy == lane),
                jnp.logical_and(j == col_o, i + 2 * cy + cx == lane),
            ),
        )
        hot_ref[...] = jnp.where(jnp.logical_and(near, index >= 0), 1.0, 0.0).astype(BF16)
        hot = [(index == lane + t).astype(F32).astype(BF16) for t in range(0, cols, 128)]
        hot = jnp.concatenate(hot, axis=1)
        copies[6].wait()
        weight = weight_ref[...]
        conc = state_ref[0, 1 : cx + 1, PADY : PADY + cy, :].reshape(cols, 128)
        both = jnp.concatenate([split3(conc), split3(next_ref[...])], axis=1)
        picked = jnp.dot(hot, both, preferred_element_type=F32)
        now_ref[...] = weight * join3(picked[:, :384])
        soon_ref[...] = weight * join3(picked[:, 384:])
        exe_ref[...] = fluid_ref[pl.ds(pl.multiple_of(row_e * cy, 8), cy), :]
        exo_ref[...] = fluid_ref[pl.ds(pl.multiple_of(row_o * cy, 8), cy), :]
        eye_ref[...] = fluid_ref[pl.ds(col_e, cx, stride=cy), :]
        eyo_ref[...] = fluid_ref[pl.ds(col_o, cx, stride=cy), :]

    def edge_signs():
        me_x, me_y = lax.axis_index("gx"), lax.axis_index("gy")
        sx = (1 - 2 * lax.rem(me_x, 2)).astype(F32)
        sy = (1 - 2 * lax.rem(me_y, 2)).astype(F32)
        wrap_x = jnp.logical_or(me_x == 0, me_x == nx - 1)
        wrap_y = jnp.logical_or(me_y == 0, me_y == ny - 1)
        return sx, sy, wrap_x, wrap_y

    def edge_terms(own, halo, e, sign, wrap):
        e = e[...]
        if wrap is not None:
            e = jnp.where(wrap, 0.0, e)
        there = halo[5]
        return e * ((own[5] + there + sign * halo[4]) * halo[3] - there * own[3])

    def third(
        oxe, oxo, oye, oyo, hxe, hxo, hye, hyo, exe, exo, eye, eyo,
        now_ref, soon_ref, hot_ref, weight_ref, blocks_ref,
    ):
        sx, sy, wrap_x, wrap_y = edge_signs()
        edges = [
            edge_terms(oxe, hxe, exe, sx, None),
            edge_terms(oxo, hxo, exo, -sx, wrap_x),
            edge_terms(oye, hye, eye, sy, None),
            edge_terms(oyo, hyo, eyo, -sy, wrap_y),
        ]
        used = 2 * (cx + cy)
        edges = jnp.concatenate(edges + [jnp.zeros((128 - used, 128), F32)], axis=0)
        more = join3(jnp.dot(hot_ref[...], split3(edges), preferred_element_type=F32))
        blocks_ref[:, 0:cap, :] = now_ref[...].reshape(owners, cap, 128)
        soon = soon_ref[...] + weight_ref[...] * more
        blocks_ref[:, cap : 2 * cap, :] = soon.reshape(owners, cap, 128)

    def fourth(
        adj_hbm, vel_hbm, dif_hbm, con_hbm, rec_hbm, height_hbm, dst_hbm, hxe, hxo, hye, hyo,
        last_hbm, coef_hbm, hot_ref, xe_ref, xo_ref, ye_ref, yo_ref,
        cxe_ref, cxo_ref, cye_ref, cyo_ref,
        state_ref, vel_ref, dif_ref, con_ref, rec_ref, height_ref, dst_ref,
        pad_ref, fluid_ref, count_ref, coef_ref, next_ref, flat_ref, last_ref, sem,
    ):
        copies = [
            pltpu.make_async_copy(height_hbm, height_ref, sem.at[0]),
            pltpu.make_async_copy(vel_hbm, vel_ref, sem.at[1]),
            pltpu.make_async_copy(dif_hbm, dif_ref, sem.at[2]),
            pltpu.make_async_copy(con_hbm, con_ref, sem.at[3]),
            pltpu.make_async_copy(dst_hbm, dst_ref, sem.at[4]),
            pltpu.make_async_copy(rec_hbm, rec_ref, sem.at[5]),
            pltpu.make_async_copy(adj_hbm, state_ref.at[:, inside[0], inside[1], :], sem.at[6]),
        ]
        start_all(copies)
        row_e, row_o, col_e, col_o = edges_at()
        clear_halo(next_ref, range(4))
        halo = (hxe, hxo, hye, hyo)
        take_halo(pad_ref, 0, 4, *halo, True, False)
        take_halo(pad_ref, 1, 4, *halo, False, True)
        take_halo(pad_ref, 2, 5, *halo, True, True)
        take_halo(pad_ref, 3, 6, *halo, True, True)
        for k in range(4):
            take_halo(state_ref, k, k, *halo, True, True)
        copies[0].wait()
        fluid_ref[...] = row_values(height_ref[...])
        wait_all(copies[1:4])
        fill_pads(pad_ref, vel_ref, dif_ref, con_ref)
        wait_all(copies[4:7])
        hot_ref[...] = select_cols(dst_ref[...], cols)
        count_ref[...] = receptor_counts(rec_ref[...], cols)
        state_ref[3, 1 : cx + 1, PADY : PADY + cy, :] += count_ref[...].reshape(cx, cy, 128)
        for i, jv in cells():
            at = pl.ds(i * cy + 8 * jv, 8)
            j = PADY + 8 * jv
            c, e = cell_coefficients(i, jv, vertical(vel_ref, i, jv), pad_ref, fluid_ref)
            c = c + cell_gradients(i, jv, e, pad_ref)
            for n in range(10):
                coef_ref[n, at, :] = c[n]
            conc = state_ref[3, i + 1, j : j + 8, :]
            for k in range(4):
                value = cell_step(i, jv, c, state_ref, k)
                value = value + count_ref[at, :] if k == 3 else value - c[7 + k] * conc
                next_ref[k, i + 1, j : j + 8, :] = value
                flat_ref[k, at, :] = value
        outs = [pltpu.make_async_copy(coef_ref.at[pl.ds(0, 7)], coef_hbm, sem.at[7])]
        outs[0].start()
        for k in range(4):
            xe_ref[k] = edge_row(flat_ref, k, row_e)
            xo_ref[k] = edge_row(flat_ref, k, row_o)
            ye_ref[k] = edge_col(flat_ref, k, col_e)
            yo_ref[k] = edge_col(flat_ref, k, col_o)
        for i, jv in cells():
            at = pl.ds(i * cy + 8 * jv, 8)
            j = PADY + 8 * jv
            c = [coef_ref[n, at, :] for n in range(10)]
            conc = next_ref[3, i + 1, j : j + 8, :]
            for k in range(4):
                value = cell_step(i, jv, c, next_ref, k)
                if k < 3:
                    value = value - c[7 + k] * conc
                last_ref[k, i, 8 * jv : 8 * jv + 8, :] = value
        outs.append(pltpu.make_async_copy(last_ref, last_hbm, sem.at[8]))
        outs[1].start()
        par_x = lax.rem(lax.axis_index("gx"), 2)
        par_y = lax.rem(lax.axis_index("gy"), 2)
        cxe_ref[...] = coef_ref[1 + par_x, pl.ds(pl.multiple_of(row_e * cy, 8), cy), :]
        cxo_ref[...] = coef_ref[2 - par_x, pl.ds(pl.multiple_of(row_o * cy, 8), cy), :]
        cye_ref[...] = edge_col(coef_ref, 3 + par_y, col_e)
        cyo_ref[...] = edge_col(coef_ref, 4 - par_y, col_o)
        wait_all(outs)

    def fifth(
        arrived_ref, hot_ref, xe_in, xo_in, ye_in, yo_in,
        wall_ref, xe_ref, xo_ref, ye_ref, yo_ref,
    ):
        row_e, row_o, col_e, col_o = edges_at()
        blocks = split3(arrived_ref[:, 0:cap, :].reshape(slots, 128))
        wall_ref[0] = join3(jnp.dot(hot_ref[...], blocks, preferred_element_type=F32))
        xe_ref[...] = xe_in[...]
        xo_ref[...] = xo_in[...]
        ye_ref[...] = ye_in[...]
        yo_ref[...] = yo_in[...]
        xe_ref[2] += edge_row(wall_ref, 0, row_e)
        xo_ref[2] += edge_row(wall_ref, 0, row_o)
        ye_ref[2] += edge_col(wall_ref, 0, col_e)
        yo_ref[2] += edge_col(wall_ref, 0, col_o)

    def sixth(
        last_hbm, coef_hbm, wall_ref, arrived_ref, hot_ref,
        out_hbm, sxe_ref, sxo_ref, sye_ref, syo_ref,
        coef_ref, pad_ref, final_ref, add_ref, sem,
    ):
        row_e, row_o, col_e, col_o = edges_at()
        tile_e = pl.ds(pl.multiple_of(col_e // 8 * 8, 8), 8)
        tile_o = pl.ds(pl.multiple_of(col_o // 8 * 8, 8), 8)
        copies = [
            pltpu.make_async_copy(last_hbm.at[2], final_ref, sem.at[0]),
            pltpu.make_async_copy(coef_hbm, coef_ref, sem.at[1]),
            pltpu.make_async_copy(last_hbm.at[:, row_e], sxe_ref, sem.at[2]),
            pltpu.make_async_copy(last_hbm.at[:, row_o], sxo_ref, sem.at[3]),
            pltpu.make_async_copy(last_hbm.at[:, :, tile_e, :], sye_ref, sem.at[4]),
            pltpu.make_async_copy(last_hbm.at[:, :, tile_o, :], syo_ref, sem.at[5]),
        ]
        start_all(copies)
        blocks = split3(arrived_ref[:, cap : 2 * cap, :].reshape(slots, 128))
        add_ref[...] = join3(jnp.dot(hot_ref[...], blocks, preferred_element_type=F32))
        clear_halo(pad_ref, (0,))
        pad_ref[0, 1 : cx + 1, PADY : PADY + cy, :] = wall_ref[0].reshape(cx, cy, 128)
        wait_all(copies)
        for i, jv in cells():
            at = pl.ds(i * cy + 8 * jv, 8)
            c = [coef_ref[n, at, :] for n in range(7)]
            value = final_ref[i, 8 * jv : 8 * jv + 8, :] + add_ref[at, :]
            final_ref[i, 8 * jv : 8 * jv + 8, :] = value + cell_step(i, jv, c, pad_ref, 0)
        copy = pltpu.make_async_copy(final_ref, out_hbm.at[2], sem.at[6])
        copy.start()
        sxe_ref[2] = final_ref[row_e]
        sxo_ref[2] = final_ref[row_o]
        sye_ref[2] = final_ref[:, tile_e, :]
        syo_ref[2] = final_ref[:, tile_o, :]
        copy.wait()

    def seventh(
        last_hbm, sxe, sxo, sye, syo, cxe, cxo, cye, cyo, hxe, hxo, hye, hyo,
        out_hbm, txe, txo, tye, tyo, dye, dyo, sem,
    ):
        row_e, row_o, col_e, col_o = edges_at()
        _, _, wrap_x, wrap_y = edge_signs()
        near_e, near_o = cye[...], jnp.where(wrap_y, 0.0, cyo[...])
        tile_e = col_e // 8 * 8
        tile_o = col_o // 8 * 8
        for k in range(4):
            dye[k] = near_e * hye[k]
            dyo[k] = near_o * hyo[k]
            tye[k] = sye[k]
            tyo[k] = syo[k]
            for i in range(1, cx - 1):
                tye[k, i, pl.ds(col_e - tile_e, 1), :] += dye[k, i : i + 1, :]
                tyo[k, i, pl.ds(col_o - tile_o, 1), :] += dyo[k, i : i + 1, :]
        copies = [
            pltpu.make_async_copy(
                strip.at[:, pl.ds(1, cx - 2)],
                out_hbm.at[:, pl.ds(1, cx - 2), pl.ds(pl.multiple_of(tile, 8), 8), :],
                sem.at[n],
            )
            for n, (strip, tile) in enumerate(((tye, tile_e), (tyo, tile_o)))
        ]
        start_all(copies)
        near_e, near_o = cxe[...], jnp.where(wrap_x, 0.0, cxo[...])
        for k in range(4):
            txe[k] = sxe[k] + near_e * hxe[k]
            txo[k] = sxo[k] + near_o * hxo[k]
            for row, out in ((row_e, txe), (row_o, txo)):
                for col, dy in ((col_e, dye), (col_o, dyo)):
                    out[k, pl.ds(col, 1), :] += dy[k, pl.ds(row, 1), :]
        more = [
            pltpu.make_async_copy(strip, out_hbm.at[:, row], sem.at[n])
            for n, (strip, row) in enumerate(((txe, row_e), (txo, row_o)), 2)
        ]
        start_all(more)
        wait_all(copies + more)

    def sds(*shape):
        return jax.ShapeDtypeStruct(shape, F32)

    def hbm(*shape):
        return pltpu.HBM(shape, F32)

    def vm(*shape, dtype=F32):
        return pltpu.VMEM(shape, dtype)

    def dma(count):
        return pltpu.SemaphoreType.DMA((count,))

    def call(body, name, ins, outs, shapes, scratch, cost, limit=24, **more):
        return pl.pallas_call(
            body,
            name=name,
            out_shape=shapes,
            in_specs=ins,
            out_specs=outs,
            scratch_shapes=scratch,
            compiler_params=pltpu.CompilerParams(vmem_limit_bytes=limit << 20),
            cost_estimate=pl.CostEstimate(flops=cost, bytes_accessed=cost, transcendentals=0),
            **more,
        )

    int_table = vm(owners, cap, dtype=jnp.int32)
    three = [vm(3, cx, cy, 128, dtype=BF16)] + [vm(cx, cy, 128, dtype=BF16)] * 2
    strips = (sds(4, cy, 128), sds(4, cy, 128), sds(4, cx, 128), sds(4, cx, 128))
    sides = (sds(cy, 128), sds(cy, 128), sds(cx, 128), sds(cx, 128))
    height = vm(cx, cy, dtype=jnp.int32)
    padded = vm(4, px, py, 128)

    def kernels(rcp):
        line = vm(1, rcp, dtype=jnp.int32)
        return (
            call(
                first, "first", [HBM] * 5, (VMEM,) * 4,
                (sds(7, cy, 128), sds(7, cy, 128), sds(7, cx, 128), sds(7, cx, 128)),
                [vm(4, cols, 128), vm(2, cx, cy, 128, dtype=BF16)] + three[1:]
                + [line, vm(3, cols, 128), dma(5)],
                4 << 20,
            ),
            call(
                second, "second", [HBM] * 7, (VMEM,) * 8,
                (sds(slots, 128), sds(slots, 128),
                 jax.ShapeDtypeStruct((slots, 128), BF16), sds(slots, 128)) + sides,
                [vm(1, px, py, 128)] + three[:2] + [line, height, int_table]
                + [vm(3, px, py, 128), vm(cols, 128), vm(cols, 128), vm(cols, 128), dma(7)],
                8 << 20,
            ),
            call(
                third, "third", [VMEM] * 16, VMEM, sds(owners, 2 * cap, 128), [], 2 << 20,
            ),
            call(
                fourth, "fourth", [HBM] * 7 + [VMEM] * 4, (HBM,) * 2 + (VMEM,) * 9,
                (hbm(4, cx, cy, 128), hbm(7, cols, 128), jax.ShapeDtypeStruct((cols, slots), BF16))
                + strips + sides,
                [padded] + three + [line, height, int_table]
                + [padded, vm(cols, 128), vm(cols, 128), vm(10, cols, 128), padded,
                   vm(4, cols, 128), vm(4, cx, cy, 128), dma(9)],
                10 << 20,
            ),
            call(
                fifth, "fifth", [VMEM] * 6, (VMEM,) * 5, (sds(1, cols, 128),) + strips, [],
                2 << 20,
            ),
            call(
                sixth, "sixth", [HBM] * 2 + [VMEM] * 3, (HBM,) + (VMEM,) * 4,
                (hbm(4, cx, cy, 128), sds(4, cy, 128), sds(4, cy, 128),
                 sds(4, cx, 8, 128), sds(4, cx, 8, 128)),
                [vm(7, cols, 128), vm(1, px, py, 128), vm(cx, cy, 128), vm(cols, 128), dma(7)],
                5 << 20,
                input_output_aliases={0: 0},
            ),
            call(
                seventh, "seventh", [HBM] + [VMEM] * 12, HBM, sds(4, cx, cy, 128),
                [vm(4, cy, 128), vm(4, cy, 128), vm(4, cx, 8, 128), vm(4, cx, 8, 128),
                 vm(4, cx, 128), vm(4, cx, 128), dma(4)],
                2 << 20,
                input_output_aliases={0: 0},
            ),
        )

    return kernels


def shards(
    adjoint, velocity, diffusivity, concentration, heights, receptors, face_src, face_dst, face_coef
):
    nx, ny = lax.axis_size("gx"), lax.axis_size("gy")
    cx, cy, levels = adjoint.shape[1:]
    owners, cap = face_src.shape[2:]
    kernels = make_kernels(nx, ny, cx, cy, owners, cap)
    first, second, third, fourth, fifth, sixth, seventh = kernels(receptors.shape[2])

    def swap(partner):
        return [
            (x * ny + y, px * ny + py)
            for x in range(nx) for y in range(ny) for px, py in (partner(x, y),)
        ]

    def odd(i):
        return i - 1 if i % 2 == 0 else i + 1

    x_even = swap(lambda x, y: (x ^ 1, y))
    x_odd = swap(lambda x, y: (odd(x), y) if 0 < x < nx - 1 else (x, y ^ 1))
    y_even = swap(lambda x, y: (x, y ^ 1))
    y_odd = swap(lambda x, y: (x, odd(y)) if 0 < y < ny - 1 else (x ^ 1, y))

    def exchange(*edges):
        swaps = (x_even, x_odd, y_even, y_odd)
        return [lax.ppermute(e, ("gx", "gy"), pairs) for e, pairs in zip(edges, swaps)]

    src = face_src.reshape(owners, cap)
    dst = face_dst.reshape(owners, cap)
    weight = face_coef.reshape(owners * cap, levels)
    line = receptors.reshape(1, -1)
    flat = adjoint.reshape(4, cx * cy, levels)

    def pinned(*arrays):
        return [pltpu.with_memory_space_constraint(x, pltpu.HBM) for x in arrays]

    own = first(*pinned(flat, velocity, diffusivity, concentration, line))
    halos = exchange(*own)
    now, soon, hot, weight, *fluid = second(
        *pinned(adjoint), velocity, *pinned(diffusivity, line, heights, src, weight)
    )
    blocks = third(*own, *halos, *fluid, now, soon, hot, weight)
    arrived = lax.all_to_all(blocks, "gx", split_axis=0, concat_axis=0, tiled=True)
    last, coefs, hot, *rest = fourth(
        *pinned(adjoint), velocity, diffusivity, concentration, *pinned(line, heights, dst), *halos
    )
    edges, sides = rest[:4], rest[4:]
    wall, *edges = fifth(arrived, hot, *edges)
    halos = exchange(*edges)
    out, *strips = sixth(*pinned(last, coefs), wall, arrived, hot)
    return seventh(*pinned(out), *strips, *sides, *halos)


def solution(mesh):
    placed = (
        P(None, "gx", "gy", None),
        P(None, "gx", "gy", None),
        P("gx", "gy", None),
        P("gx", "gy", None),
        P("gx", "gy"),
        P("gx", "gy", None),
        P("gx", "gy", None, None),
        P("gx", "gy", None, None),
        P("gx", "gy", None, None, None),
    )
    return jax.shard_map(
        shards, mesh=mesh, in_specs=placed, out_specs=P(None, "gx", "gy", None), check_vma=False
    )
```

time: 50.1 us -> 41.8 us (0.83)
  the two profiles are of different devices: /device:TPU:8 before, /device:TPU:10 now
where the time goes in v2:
time: 41.8 us; the launch traced here: 41.1 us
  starting transfers between devices  20.1 us (48%)
  Pallas kernels  14.8 us (35%)
  waiting for transfers between devices  6.11 us (15%)
    ppermute x8, starting transfers between devices, exchange(): lax.ppermute(e, ('gx', 'gy'), pairs)  15.3 us
    pallas_call x1, Pallas kernels, shards(): fourth(*pinned(adjoint), velocity, diffusivity, concentration, *pinned(li...  5.24 us
    all_to_all x1, waiting for transfers between devices, shards(): lax.all_to_all(blocks, 'gx', split_axis=0, concat_axis=0, tiled=True)  4.85 us
    all_to_all x1, starting transfers between devices, shards(): lax.all_to_all(blocks, 'gx', split_axis=0, concat_axis=0, tiled=True)  4.81 us
    pallas_call x1, Pallas kernels, shards(): out, *strips = sixth(*pinned(last, coefs), wall, arrived, hot)  2.87 us
    pallas_call x1, Pallas kernels, shards(): second(*pinned(adjoint), velocity, *pinned(diffusivity, line, heights, sr...  2.83 us
    pallas_call x1, Pallas kernels, shards(): own = first(*pinned(flat, velocity, diffusivity, concentration, line))  1.64 us
    ppermute x8, waiting for transfers between devices, exchange(): lax.ppermute(e, ('gx', 'gy'), pairs)  1.26 us
  transfers between devices with their start and end apart: 9, of which 3 were waited for; matrix products, arithmetic and copies ran while one was open for 0% of the time, Pallas kernels for 27%

profile of v2, /device:TPU:10, one launch (start us, length us, event | category | flops | bytes accessed | tf_op | source)
XLA Modules:
  0.0 41.1 jit_solution(14543514370963155997)
XLA Ops:
  0.0 0.0 copy-start
  0.0 1.6 %first.1 = (f32[7,32,128]{2,1,0:T(8,128)S(1)}, f32[7,32,128]{2,1,0:T(8,128)S(1)}, f32[7,16,128]{2,1,0:T(8,128)S(1)}, f32[7,16,128]{2,1,0:T(8,128)S(1)}) custom-call(f32[4,512,128]{2,1,0:T(8,128)} %bitcast.5, bf16[3,16,32,128]{3,2,1,0:T(8,128)(2,1)} %vel_hbm.5, bf16[16,32,128]{2,1,0:T(8,128)(2,1)} %dif_hbm.5, bf16[16,32,128]{2,1,0:T(8,128)(2,1)} %con_hbm.3, ...), custom_call_target="tpu_custom_call" | custom-call | flops 4194304 | bytes 4194304 | tf_op jit(solution)/shard_map/first/pallas_call | solution.py:621
  1.7 2.0 %collective-permute-start = (f32[7,32,128]{2,1,0:T(8,128)S(1)}, f32[7,32,128]{2,1,0:T(8,128)S(1)}, u32[]{:S(2)}, u32[]{:S(2)}) collective-permute-start(f32[7,32,128]{2,1,0:T(8,128)S(1)} %get-tuple-element.38.oxe), channel_id=1, source_target_pairs={{0,16},{1,17},{2,18},{3,19},{4,20},{5,21},{6,22},{7,23},{8,24},{9,... | collective-permute-start | bytes 344072 | tf_op jit(solution)/shard_map/ppermute | solution.py:610
  3.7 4.8 %collective-permute-start.1 = (f32[7,32,128]{2,1,0:T(8,128)S(1)}, f32[7,32,128]{2,1,0:T(8,128)S(1)}, u32[]{:S(2)}, u32[]{:S(2)}) collective-permute-start(f32[7,32,128]{2,1,0:T(8,128)S(1)} %get-tuple-element.39.oxo), channel_id=1, source_target_pairs={{0,1},{1,0},{2,3},{3,2},{4,5},{5,4},{6,7},{7,6},{8,9},{9,8},{10,11... | collective-permute-start | bytes 344072 | tf_op jit(solution)/shard_map/ppermute | solution.py:610
  8.5 0.0 collective-permute-start.2
  8.5 2.7 %collective-permute-start.3 = (f32[7,16,128]{2,1,0:T(8,128)S(1)}, f32[7,16,128]{2,1,0:T(8,128)S(1)}, u32[]{:S(2)}, u32[]{:S(2)}) collective-permute-start(f32[7,16,128]{2,1,0:T(8,128)S(1)} %get-tuple-element.41.oyo), channel_id=1, source_target_pairs={{0,16},{1,2},{2,1},{3,4},{4,3},{5,6},{6,5},{7,8},{8,7},{9,10},{10,... | collective-permute-start | bytes 172040 | tf_op jit(solution)/shard_map/ppermute | solution.py:610
  11.2 0.0 copy-done
  11.2 0.0 copy-start.1
  11.2 0.0 copy-start.2
  11.2 2.8 %second.1 = (f32[256,128]{1,0:T(8,128)S(1)}, f32[256,128]{1,0:T(8,128)S(1)}, bf16[256,128]{1,0:T(8,128)(2,1)S(1)}, f32[256,128]{1,0:T(8,128)S(1)}, f32[32,128]{1...) custom-call(f32[4,16,32,128]{3,2,1,0:T(8,128)} %adj_hbm.3, ...), custom_call_target="tpu_custom_call" | custom-call | flops 8388608 | bytes 8388608 | tf_op jit(solution)/shard_map/second/pallas_call | solution.py:623
  14.0 0.0 collective-permute-done.2.hye
  14.0 0.6 %collective-permute-done.3.hyo = f32[7,16,128]{2,1,0:T(8,128)S(1)} collective-permute-done((f32[7,16,128]{2,1,0:T(8,128)S(1)}, f32[7,16,128]{2,1,0:T(8,128)S(1)}, u32[]{:S(2)}, u32[]{:S(2)}) %collective-permute-start.3) | collective-permute-done | bytes 57376 | tf_op jit(solution)/shard_map/ppermute | solution.py:610
  14.6 0.0 collective-permute-done.hxe
  14.6 0.0 collective-permute-done.1.hxo
  14.6 1.0 %third.1 = f32[16,32,128]{2,1,0:T(8,128)} custom-call(f32[7,32,128]{2,1,0:T(8,128)S(1)} %get-tuple-element.38.oxe, f32[7,32,128]{2,1,0:T(8,128)S(1)} %get-tuple-element.39.oxo, f32[7,16,128]{2,1,0:T(8,128)S(1)} %get-tuple-element.40.oye, f32[7,16,128]{2,1,0:T(8,128)S(1)} %get-tuple-element.41.oyo, f32[7,32,128]{2,1,0:T(8,128)S(1)} %collective-permute-done.hxe, ...), custom_call_target="tpu_custom_call" | custom-call | flops 2097152 | bytes 2097152 | tf_op jit(solution)/shard_map/third/pallas_call | solution.py:626
  15.6 4.8 %all-to-all-start = ((f32[16,32,128]{2,1,0:T(8,128)}), f32[16,32,128]{2,1,0:T(8,128)S(1)}, u32[]{:S(2)}, u32[]{:S(2)}) async-start(f32[16,32,128]{2,1,0:T(8,128)} %third.1), calls=%async_computation | async-start | bytes 524288 | tf_op jit(solution)/shard_map/all_to_all | solution.py:627
  20.4 0.0 copy-done.1
  20.4 0.0 copy-done.2
  20.4 5.2 %fourth.1 = (f32[4,16,32,128]{3,2,1,0:T(8,128)}, f32[7,512,128]{2,1,0:T(8,128)}, bf16[512,256]{1,0:T(8,128)(2,1)S(1)}, f32[4,32,128]{2,1,0:T(8,128)S(1)}, f32[4,...) custom-call(f32[4,16,32,128]{3,2,1,0:T(8,128)} %adj_hbm.3, ...), custom_call_target="tpu_custom_call" | custom-call | flops 10485760 | bytes 10485760 | tf_op jit(solution)/shard_map/fourth/pallas_call | solution.py:628
  25.6 4.8 %all-to-all-done.arrived_ref = f32[16,32,128]{2,1,0:T(8,128)S(1)} async-done(((f32[16,32,128]{2,1,0:T(8,128)}), f32[16,32,128]{2,1,0:T(8,128)S(1)}, u32[]{:S(2)}, u32[]{:S(2)}) %all-to-all-start) | async-done | bytes 262176 | tf_op jit(solution)/shard_map/all_to_all | solution.py:627
  30.5 0.3 fifth.1
  30.8 2.3 %collective-permute-start.4 = (f32[4,32,128]{2,1,0:T(8,128)S(1)}, f32[4,32,128]{2,1,0:T(8,128)S(1)}, u32[]{:S(2)}, u32[]{:S(2)}) collective-permute-start(f32[4,32,128]{2,1,0:T(8,128)S(1)} %get-tuple-element.67), channel_id=1, source_target_pairs={{0,16},{1,17},{2,18},{3,19},{4,20},{5,21},{6,22},{7,23},{8,24},{9,... | collective-permute-start | bytes 196616 | tf_op jit(solution)/shard_map/ppermute | solution.py:610
  33.1 1.1 %collective-permute-start.5 = (f32[4,32,128]{2,1,0:T(8,128)S(1)}, f32[4,32,128]{2,1,0:T(8,128)S(1)}, u32[]{:S(2)}, u32[]{:S(2)}) collective-permute-start(f32[4,32,128]{2,1,0:T(8,128)S(1)} %get-tuple-element.68), channel_id=1, source_target_pairs={{0,1},{1,0},{2,3},{3,2},{4,5},{5,4},{6,7},{7,6},{8,9},{9,8},{10,11... | collective-permute-start | bytes 196616 | tf_op jit(solution)/shard_map/ppermute | solution.py:610
  34.3 0.0 collective-permute-start.6
  34.3 2.3 %collective-permute-start.7 = (f32[4,16,128]{2,1,0:T(8,128)S(1)}, f32[4,16,128]{2,1,0:T(8,128)S(1)}, u32[]{:S(2)}, u32[]{:S(2)}) collective-permute-start(f32[4,16,128]{2,1,0:T(8,128)S(1)} %get-tuple-element.70), channel_id=1, source_target_pairs={{0,16},{1,2},{2,1},{3,4},{4,3},{5,6},{6,5},{7,8},{8,7},{9,10},{10,... | collective-permute-start | bytes 98312 | tf_op jit(solution)/shard_map/ppermute | solution.py:610
  36.6 2.9 %sixth.1 = (f32[4,16,32,128]{3,2,1,0:T(8,128)}, f32[4,32,128]{2,1,0:T(8,128)S(1)}, f32[4,32,128]{2,1,0:T(8,128)S(1)}, f32[4,16,8,128]{3,2,1,0:T(8,128)S(1)}, f32[4,16,8,128]{3,2,1,0:T(8,128)S(1)}) custom-call(f32[4,16,32,128]{3,2,1,0:T(8,128)} %get-tuple-element.42.last_hbm, ...), custom_call_target="tpu_custom_call", output_to_operand_aliasing={{0}: (0, {})} | custom-call | flops 5242880 | bytes 5242880 | tf_op jit(solution)/shard_map/sixth/pallas_call | solution.py:634
  39.4 0.0 collective-permute-done.6.hye
  39.4 0.7 %collective-permute-done.7.hyo = f32[4,16,128]{2,1,0:T(8,128)S(1)} collective-permute-done((f32[4,16,128]{2,1,0:T(8,128)S(1)}, f32[4,16,128]{2,1,0:T(8,128)S(1)}, u32[]{:S(2)}, u32[]{:S(2)}) %collective-permute-start.7) | collective-permute-done | bytes 32800 | tf_op jit(solution)/shard_map/ppermute | solution.py:610
  40.1 0.0 collective-permute-done.4.hxe
  40.1 0.0 collective-permute-done.5.hxo
  40.1 0.9 %seventh.1 = f32[4,16,32,128]{3,2,1,0:T(8,128)} custom-call(f32[4,16,32,128]{3,2,1,0:T(8,128)} %get-tuple-element.58.last_hbm, f32[4,32,128]{2,1,0:T(8,128)S(1)} %get-tuple-element.59.sxe, f32[4,32,128]{2,1,0:T(8,128)S(1)} %get-tuple-element.60.sxo, f32[4,16,8,128]{3,2,1,0:T(8,128)S(1)} %get-tuple-element.61.sye, ...), custom_call_target="tpu_custom_call", output_to_operand_aliasing={{}: (0, {})} | custom-call | flops 2097152 | bytes 2097152 | tf_op jit(solution)/shard_map/seventh/pallas_call | solution.py:635
Async XLA Ops:
  0.0 11.2 %copy-start = (bf16[3,16,32,128]{3,2,1,0:T(8,128)(2,1)S(1)}, bf16[3,16,32,128]{3,2,1,0:T(8,128)(2,1)}, u32[]{:S(2)}) copy-start(bf16[3,16,32,128]{3,2,1,0:T(8,128)(2,1)} %vel_hbm.5) | copy-start | bytes 1179652
  1.7 13.0 %collective-permute-start = (f32[7,32,128]{2,1,0:T(8,128)S(1)}, f32[7,32,128]{2,1,0:T(8,128)S(1)}, u32[]{:S(2)}, u32[]{:S(2)}) collective-permute-start(f32[7,32,128]{2,1,0:T(8,128)S(1)} %get-tuple-element.38.oxe), channel_id=1, source_target_pairs={{0,16},{1,17},{2,18},{3,19},{4,20},{5,21},{6,22},{7,23},{8,24},{9,... | collective-permute-start | bytes 344072 | tf_op jit(solution)/shard_map/ppermute | solution.py:610
  3.7 10.9 %collective-permute-start.1 = (f32[7,32,128]{2,1,0:T(8,128)S(1)}, f32[7,32,128]{2,1,0:T(8,128)S(1)}, u32[]{:S(2)}, u32[]{:S(2)}) collective-permute-start(f32[7,32,128]{2,1,0:T(8,128)S(1)} %get-tuple-element.39.oxo), channel_id=1, source_target_pairs={{0,1},{1,0},{2,3},{3,2},{4,5},{5,4},{6,7},{7,6},{8,9},{9,8},{10,11... | collective-permute-start | bytes 344072 | tf_op jit(solution)/shard_map/ppermute | solution.py:610
  8.5 5.5 %collective-permute-start.2 = (f32[7,16,128]{2,1,0:T(8,128)S(1)}, f32[7,16,128]{2,1,0:T(8,128)S(1)}, u32[]{:S(2)}, u32[]{:S(2)}) collective-permute-start(f32[7,16,128]{2,1,0:T(8,128)S(1)} %get-tuple-element.40.oye), channel_id=1, source_target_pairs={{0,1},{1,0},{2,3},{3,2},{4,5},{5,4},{6,7},{7,6},{8,9},{9,8},{10,11... | collective-permute-start | bytes 172040 | tf_op jit(solution)/shard_map/ppermute | solution.py:610
  8.5 6.1 %collective-permute-start.3 = (f32[7,16,128]{2,1,0:T(8,128)S(1)}, f32[7,16,128]{2,1,0:T(8,128)S(1)}, u32[]{:S(2)}, u32[]{:S(2)}) collective-permute-start(f32[7,16,128]{2,1,0:T(8,128)S(1)} %get-tuple-element.41.oyo), channel_id=1, source_target_pairs={{0,16},{1,2},{2,1},{3,4},{4,3},{5,6},{6,5},{7,8},{8,7},{9,10},{10,... | collective-permute-start | bytes 172040 | tf_op jit(solution)/shard_map/ppermute | solution.py:610
  11.2 9.2 %copy-start.1 = (bf16[16,32,128]{2,1,0:T(8,128)(2,1)S(1)}, bf16[16,32,128]{2,1,0:T(8,128)(2,1)}, u32[]{:S(2)}) copy-start(bf16[16,32,128]{2,1,0:T(8,128)(2,1)} %dif_hbm.5) | copy-start | bytes 393220
  11.2 9.2 %copy-start.2 = (bf16[16,32,128]{2,1,0:T(8,128)(2,1)S(1)}, bf16[16,32,128]{2,1,0:T(8,128)(2,1)}, u32[]{:S(2)}) copy-start(bf16[16,32,128]{2,1,0:T(8,128)(2,1)} %con_hbm.3) | copy-start | bytes 393220
  15.6 14.9 %all-to-all-start = ((f32[16,32,128]{2,1,0:T(8,128)}), f32[16,32,128]{2,1,0:T(8,128)S(1)}, u32[]{:S(2)}, u32[]{:S(2)}) async-start(f32[16,32,128]{2,1,0:T(8,128)} %third.1), calls=%async_computation | async-start | bytes 524288 | tf_op jit(solution)/shard_map/all_to_all | solution.py:627
  30.8 9.3 %collective-permute-start.4 = (f32[4,32,128]{2,1,0:T(8,128)S(1)}, f32[4,32,128]{2,1,0:T(8,128)S(1)}, u32[]{:S(2)}, u32[]{:S(2)}) collective-permute-start(f32[4,32,128]{2,1,0:T(8,128)S(1)} %get-tuple-element.67), channel_id=1, source_target_pairs={{0,16},{1,17},{2,18},{3,19},{4,20},{5,21},{6,22},{7,23},{8,24},{9,... | collective-permute-start | bytes 196616 | tf_op jit(solution)/shard_map/ppermute | solution.py:610
  33.1 7.0 %collective-permute-start.5 = (f32[4,32,128]{2,1,0:T(8,128)S(1)}, f32[4,32,128]{2,1,0:T(8,128)S(1)}, u32[]{:S(2)}, u32[]{:S(2)}) collective-permute-start(f32[4,32,128]{2,1,0:T(8,128)S(1)} %get-tuple-element.68), channel_id=1, source_target_pairs={{0,1},{1,0},{2,3},{3,2},{4,5},{5,4},{6,7},{7,6},{8,9},{9,8},{10,11... | collective-permute-start | bytes 196616 | tf_op jit(solution)/shard_map/ppermute | solution.py:610
  34.3 5.2 %collective-permute-start.6 = (f32[4,16,128]{2,1,0:T(8,128)S(1)}, f32[4,16,128]{2,1,0:T(8,128)S(1)}, u32[]{:S(2)}, u32[]{:S(2)}) collective-permute-start(f32[4,16,128]{2,1,0:T(8,128)S(1)} %get-tuple-element.69), channel_id=1, source_target_pairs={{0,1},{1,0},{2,3},{3,2},{4,5},{5,4},{6,7},{7,6},{8,9},{9,8},{10,11... | collective-permute-start | bytes 98312 | tf_op jit(solution)/shard_map/ppermute | solution.py:610
  34.3 5.8 %collective-permute-start.7 = (f32[4,16,128]{2,1,0:T(8,128)S(1)}, f32[4,16,128]{2,1,0:T(8,128)S(1)}, u32[]{:S(2)}, u32[]{:S(2)}) collective-permute-start(f32[4,16,128]{2,1,0:T(8,128)S(1)} %get-tuple-element.70), channel_id=1, source_target_pairs={{0,16},{1,2},{2,1},{3,4},{4,3},{5,6},{6,5},{7,8},{8,7},{9,10},{10,... | collective-permute-start | bytes 98312 | tf_op jit(solution)/shard_map/ppermute | solution.py:610

commit v3 on v2

--- a/solution.py
+++ b/solution.py
@@ -314,7 +314,7 @@
         return e * ((own[5] + there + sign * halo[4]) * halo[3] - there * own[3])
 
     def third(
-        oxe, oxo, oye, oyo, hxe, hxo, hye, hyo, exe, exo, eye, eyo,
+        hxe, hxo, hyo, hye, oxe, oxo, oye, oyo, exe, exo, eye, eyo,
         now_ref, soon_ref, hot_ref, weight_ref, blocks_ref,
     ):
         sx, sy, wrap_x, wrap_y = edge_signs()
@@ -332,7 +332,7 @@
         blocks_ref[:, cap : 2 * cap, :] = soon.reshape(owners, cap, 128)
 
     def fourth(
-        adj_hbm, vel_hbm, dif_hbm, con_hbm, rec_hbm, height_hbm, dst_hbm, hxe, hxo, hye, hyo,
+        adj_hbm, vel_hbm, dif_hbm, con_hbm, rec_hbm, height_hbm, dst_hbm, hxe, hxo, hyo, hye,
         last_hbm, coef_hbm, hot_ref, xe_ref, xo_ref, ye_ref, yo_ref,
         cxe_ref, cxo_ref, cye_ref, cyo_ref,
         state_ref, vel_ref, dif_ref, con_ref, rec_ref, height_ref, dst_ref,
@@ -457,7 +457,7 @@
         copy.wait()
 
     def seventh(
-        last_hbm, sxe, sxo, sye, syo, cxe, cxo, cye, cyo, hxe, hxo, hye, hyo,
+        last_hbm, sxe, sxo, sye, syo, hxe, hxo, hyo, hye, cxe, cxo, cye, cyo,
         out_hbm, txe, txo, tye, tyo, dye, dyo, sem,
     ):
         row_e, row_o, col_e, col_o = edges_at()
@@ -621,18 +621,18 @@
     own = first(*pinned(flat, velocity, diffusivity, concentration, line))
     halos = exchange(*own)
     now, soon, hot, weight, *fluid = second(
-        *pinned(adjoint), velocity, *pinned(diffusivity, line, heights, src, weight)
+        *pinned(adjoint, velocity, diffusivity, line, heights, src, weight)
     )
-    blocks = third(*own, *halos, *fluid, now, soon, hot, weight)
+    blocks = third(*[halos[n] for n in [0, 1, 3, 2]], *own, *fluid, now, soon, hot, weight)
     arrived = lax.all_to_all(blocks, "gx", split_axis=0, concat_axis=0, tiled=True)
     last, coefs, hot, *rest = fourth(
-        *pinned(adjoint), velocity, diffusivity, concentration, *pinned(line, heights, dst), *halos
+        *pinned(adjoint, velocity, diffusivity, concentration, line, heights, dst), *[halos[n] for n in [0, 1, 3, 2]]
     )
     edges, sides = rest[:4], rest[4:]
     wall, *edges = fifth(arrived, hot, *edges)
     halos = exchange(*edges)
     out, *strips = sixth(*pinned(last, coefs), wall, arrived, hot)
-    return seventh(*pinned(out), *strips, *sides, *halos)
+    return seventh(*pinned(out), *strips, *[halos[n] for n in [0, 1, 3, 2]], *sides)
 
 
 def solution(mesh):

time: 41.8 us -> 41.4 us (level)
  waiting for transfers between devices: 6.11 us -> 8.25 us
  starting transfers between devices: 20.1 us -> 18.9 us
  Pallas kernels: 14.8 us -> 13.8 us
    ppermute x8, waiting for transfers between devices: 1.26 us -> 2.41 us  [exchange(): lax.ppermute(e, ('gx', 'gy'), pairs)]
    ppermute x8, starting transfers between devices: 15.3 us -> 14.1 us  [exchange(): lax.ppermute(e, ('gx', 'gy'), pairs)]
    all_to_all x1, waiting for transfers between devices: 4.85 us -> 5.84 us  [shards(): lax.all_to_all(blocks, 'gx', split_axis=0, concat_axis=0, tiled=True)]
    pallas_call x4, Pallas kernels: 9.96 us -> 9.05 us  [the longest x1 4.37 us: shards(): fourth(*pinned(adjoint, velocity, diffusivity, concentration, line, heigh...]
  transfers between devices with their start and end apart: 9 -> 9, of which waited for: 3 -> 3; matrix products, arithmetic and copies ran while one was open for 0% -> 0% of each run, Pallas kernels for 27% -> 24%
where the time goes in v3:
time: 41.4 us; the launch traced here: 41 us
  starting transfers between devices  18.9 us (46%)
  Pallas kernels  13.8 us (33%)
  waiting for transfers between devices  8.25 us (20%)
    ppermute x8, starting transfers between devices, exchange(): lax.ppermute(e, ('gx', 'gy'), pairs)  14.1 us
    all_to_all x1, waiting for transfers between devices, shards(): lax.all_to_all(blocks, 'gx', split_axis=0, concat_axis=0, tiled=True)  5.84 us
    all_to_all x1, starting transfers between devices, shards(): lax.all_to_all(blocks, 'gx', split_axis=0, concat_axis=0, tiled=True)  4.78 us
    pallas_call x1, Pallas kernels, shards(): fourth(*pinned(adjoint, velocity, diffusivity, concentration, line, heigh...  4.37 us
    pallas_call x1, Pallas kernels, shards(): out, *strips = sixth(*pinned(last, coefs), wall, arrived, hot)  2.87 us
    pallas_call x1, Pallas kernels, shards(): second(*pinned(adjoint, velocity, diffusivity, line, heights, src, weight))  2.79 us
    ppermute x8, waiting for transfers between devices, exchange(): lax.ppermute(e, ('gx', 'gy'), pairs)  2.41 us
    pallas_call x1, Pallas kernels, shards(): own = first(*pinned(flat, velocity, diffusivity, concentration, line))  1.6 us
  transfers between devices with their start and end apart: 9, of which 3 were waited for; matrix products, arithmetic and copies ran while one was open for 0% of the time, Pallas kernels for 24%

profile of v3, /device:TPU:10, one launch (start us, length us, event | category | flops | bytes accessed | tf_op | source)
XLA Modules:
  0.0 41.0 jit_solution(14535457997928983086)
XLA Ops:
  0.0 1.6 %first.1 = (f32[7,32,128]{2,1,0:T(8,128)S(1)}, f32[7,32,128]{2,1,0:T(8,128)S(1)}, f32[7,16,128]{2,1,0:T(8,128)S(1)}, f32[7,16,128]{2,1,0:T(8,128)S(1)}) custom-call(f32[4,512,128]{2,1,0:T(8,128)} %bitcast.5, bf16[3,16,32,128]{3,2,1,0:T(8,128)(2,1)} %vel_hbm.5, bf16[16,32,128]{2,1,0:T(8,128)(2,1)} %dif_hbm.5, bf16[16,32,128]{2,1,0:T(8,128)(2,1)} %con_hbm.3, ...), custom_call_target="tpu_custom_call" | custom-call | flops 4194304 | bytes 4194304 | tf_op jit(solution)/shard_map/first/pallas_call | solution.py:621
  1.6 2.0 %collective-permute-start = (f32[7,32,128]{2,1,0:T(8,128)S(1)}, f32[7,32,128]{2,1,0:T(8,128)S(1)}, u32[]{:S(2)}, u32[]{:S(2)}) collective-permute-start(f32[7,32,128]{2,1,0:T(8,128)S(1)} %get-tuple-element.38.oxe), channel_id=1, source_target_pairs={{0,16},{1,17},{2,18},{3,19},{4,20},{5,21},{6,22},{7,23},{8,24},{9,... | collective-permute-start | bytes 344072 | tf_op jit(solution)/shard_map/ppermute | solution.py:610
  3.6 4.8 %collective-permute-start.1 = (f32[7,32,128]{2,1,0:T(8,128)S(1)}, f32[7,32,128]{2,1,0:T(8,128)S(1)}, u32[]{:S(2)}, u32[]{:S(2)}) collective-permute-start(f32[7,32,128]{2,1,0:T(8,128)S(1)} %get-tuple-element.39.oxo), channel_id=1, source_target_pairs={{0,1},{1,0},{2,3},{3,2},{4,5},{5,4},{6,7},{7,6},{8,9},{9,8},{10,11... | collective-permute-start | bytes 344072 | tf_op jit(solution)/shard_map/ppermute | solution.py:610
  8.4 1.4 %collective-permute-start.2 = (f32[7,16,128]{2,1,0:T(8,128)S(1)}, f32[7,16,128]{2,1,0:T(8,128)S(1)}, u32[]{:S(2)}, u32[]{:S(2)}) collective-permute-start(f32[7,16,128]{2,1,0:T(8,128)S(1)} %get-tuple-element.40.oyo), channel_id=1, source_target_pairs={{0,16},{1,2},{2,1},{3,4},{4,3},{5,6},{6,5},{7,8},{8,7},{9,10},{10,... | collective-permute-start | bytes 172040 | tf_op jit(solution)/shard_map/ppermute | solution.py:610
  9.9 1.3 %collective-permute-start.3 = (f32[7,16,128]{2,1,0:T(8,128)S(1)}, f32[7,16,128]{2,1,0:T(8,128)S(1)}, u32[]{:S(2)}, u32[]{:S(2)}) collective-permute-start(f32[7,16,128]{2,1,0:T(8,128)S(1)} %get-tuple-element.41.oye), channel_id=1, source_target_pairs={{0,1},{1,0},{2,3},{3,2},{4,5},{5,4},{6,7},{7,6},{8,9},{9,8},{10,11... | collective-permute-start | bytes 172040 | tf_op jit(solution)/shard_map/ppermute | solution.py:610
  11.1 2.8 %second.1 = (f32[256,128]{1,0:T(8,128)S(1)}, f32[256,128]{1,0:T(8,128)S(1)}, bf16[256,128]{1,0:T(8,128)(2,1)S(1)}, f32[256,128]{1,0:T(8,128)S(1)}, f32[32,128]{1...) custom-call(f32[4,16,32,128]{3,2,1,0:T(8,128)} %adj_hbm.3, ...), custom_call_target="tpu_custom_call" | custom-call | flops 8388608 | bytes 8388608 | tf_op jit(solution)/shard_map/second/pallas_call | solution.py:623
  13.9 0.5 %collective-permute-done.2.hyo = f32[7,16,128]{2,1,0:T(8,128)S(1)} collective-permute-done((f32[7,16,128]{2,1,0:T(8,128)S(1)}, f32[7,16,128]{2,1,0:T(8,128)S(1)}, u32[]{:S(2)}, u32[]{:S(2)}) %collective-permute-start.2) | collective-permute-done | bytes 57376 | tf_op jit(solution)/shard_map/ppermute | solution.py:610
  14.5 0.0 collective-permute-done.3.hye
  14.5 0.0 collective-permute-done.hxe
  14.5 0.0 collective-permute-done.1.hxo
  14.5 1.0 %third.1 = f32[16,32,128]{2,1,0:T(8,128)} custom-call(f32[7,32,128]{2,1,0:T(8,128)S(1)} %collective-permute-done.hxe, f32[7,32,128]{2,1,0:T(8,128)S(1)} %collective-permute-done.1.hxo, f32[7,16,128]{2,1,0:T(8,128)S(1)} %collective-permute-done.2.hyo, f32[7,16,128]{2,1,0:T(8,128)S(1)} %collective-permute-done.3.hye, f32[7,32,128]{2,1,0:T(8,128)S(1)} %get-tuple-element.38.oxe, ...), custom_call_target="tpu_custom_call" | custom-call | flops 2097152 | bytes 2097152 | tf_op jit(solution)/shard_map/third/pallas_call | solution.py:626
  15.4 4.8 %all-to-all-start = ((f32[16,32,128]{2,1,0:T(8,128)}), f32[16,32,128]{2,1,0:T(8,128)S(1)}, u32[]{:S(2)}, u32[]{:S(2)}) async-start(f32[16,32,128]{2,1,0:T(8,128)} %third.1), calls=%async_computation | async-start | bytes 524288 | tf_op jit(solution)/shard_map/all_to_all | solution.py:627
  20.2 4.4 %fourth.1 = (f32[4,16,32,128]{3,2,1,0:T(8,128)}, f32[7,512,128]{2,1,0:T(8,128)}, bf16[512,256]{1,0:T(8,128)(2,1)S(1)}, f32[4,32,128]{2,1,0:T(8,128)S(1)}, f32[4,...) custom-call(f32[4,16,32,128]{3,2,1,0:T(8,128)} %adj_hbm.3, ...), custom_call_target="tpu_custom_call" | custom-call | flops 10485760 | bytes 10485760 | tf_op jit(solution)/shard_map/fourth/pallas_call | solution.py:628
  24.6 5.8 %all-to-all-done.arrived_ref = f32[16,32,128]{2,1,0:T(8,128)S(1)} async-done(((f32[16,32,128]{2,1,0:T(8,128)}), f32[16,32,128]{2,1,0:T(8,128)S(1)}, u32[]{:S(2)}, u32[]{:S(2)}) %all-to-all-start) | async-done | bytes 262176 | tf_op jit(solution)/shard_map/all_to_all | solution.py:627
  30.4 0.3 fifth.1
  30.7 2.3 %collective-permute-start.4 = (f32[4,32,128]{2,1,0:T(8,128)S(1)}, f32[4,32,128]{2,1,0:T(8,128)S(1)}, u32[]{:S(2)}, u32[]{:S(2)}) collective-permute-start(f32[4,32,128]{2,1,0:T(8,128)S(1)} %get-tuple-element.63), channel_id=1, source_target_pairs={{0,16},{1,17},{2,18},{3,19},{4,20},{5,21},{6,22},{7,23},{8,24},{9,... | collective-permute-start | bytes 196616 | tf_op jit(solution)/shard_map/ppermute | solution.py:610
  33.1 1.3 %collective-permute-start.5 = (f32[4,32,128]{2,1,0:T(8,128)S(1)}, f32[4,32,128]{2,1,0:T(8,128)S(1)}, u32[]{:S(2)}, u32[]{:S(2)}) collective-permute-start(f32[4,32,128]{2,1,0:T(8,128)S(1)} %get-tuple-element.64), channel_id=1, source_target_pairs={{0,1},{1,0},{2,3},{3,2},{4,5},{5,4},{6,7},{7,6},{8,9},{9,8},{10,11... | collective-permute-start | bytes 196616 | tf_op jit(solution)/shard_map/ppermute | solution.py:610
  34.3 0.0 collective-permute-start.6
  34.4 1.0 %collective-permute-start.7 = (f32[4,16,128]{2,1,0:T(8,128)S(1)}, f32[4,16,128]{2,1,0:T(8,128)S(1)}, u32[]{:S(2)}, u32[]{:S(2)}) collective-permute-start(f32[4,16,128]{2,1,0:T(8,128)S(1)} %get-tuple-element.66), channel_id=1, source_target_pairs={{0,1},{1,0},{2,3},{3,2},{4,5},{5,4},{6,7},{7,6},{8,9},{9,8},{10,11... | collective-permute-start | bytes 98312 | tf_op jit(solution)/shard_map/ppermute | solution.py:610
  35.3 2.9 %sixth.1 = (f32[4,16,32,128]{3,2,1,0:T(8,128)}, f32[4,32,128]{2,1,0:T(8,128)S(1)}, f32[4,32,128]{2,1,0:T(8,128)S(1)}, f32[4,16,8,128]{3,2,1,0:T(8,128)S(1)}, f32[4,16,8,128]{3,2,1,0:T(8,128)S(1)}) custom-call(f32[4,16,32,128]{3,2,1,0:T(8,128)} %get-tuple-element.42.last_hbm, ...), custom_call_target="tpu_custom_call", output_to_operand_aliasing={{0}: (0, {})} | custom-call | flops 5242880 | bytes 5242880 | tf_op jit(solution)/shard_map/sixth/pallas_call | solution.py:634
  38.2 1.9 %collective-permute-done.6.hyo = f32[4,16,128]{2,1,0:T(8,128)S(1)} collective-permute-done((f32[4,16,128]{2,1,0:T(8,128)S(1)}, f32[4,16,128]{2,1,0:T(8,128)S(1)}, u32[]{:S(2)}, u32[]{:S(2)}) %collective-permute-start.6) | collective-permute-done | bytes 32800 | tf_op jit(solution)/shard_map/ppermute | solution.py:610
  40.1 0.0 collective-permute-done.7.hye
  40.1 0.0 collective-permute-done.4.hxe
  40.1 0.0 collective-permute-done.5.hxo
  40.1 0.9 %seventh.1 = f32[4,16,32,128]{3,2,1,0:T(8,128)} custom-call(f32[4,16,32,128]{3,2,1,0:T(8,128)} %get-tuple-element.58.last_hbm, f32[4,32,128]{2,1,0:T(8,128)S(1)} %get-tuple-element.59.sxe, f32[4,32,128]{2,1,0:T(8,128)S(1)} %get-tuple-element.60.sxo, f32[4,16,8,128]{3,2,1,0:T(8,128)S(1)} %get-tuple-element.61.sye, ...), custom_call_target="tpu_custom_call", output_to_operand_aliasing={{}: (0, {})} | custom-call | flops 2097152 | bytes 2097152 | tf_op jit(solution)/shard_map/seventh/pallas_call | solution.py:635
Async XLA Ops:
  1.6 12.9 %collective-permute-start = (f32[7,32,128]{2,1,0:T(8,128)S(1)}, f32[7,32,128]{2,1,0:T(8,128)S(1)}, u32[]{:S(2)}, u32[]{:S(2)}) collective-permute-start(f32[7,32,128]{2,1,0:T(8,128)S(1)} %get-tuple-element.38.oxe), channel_id=1, source_target_pairs={{0,16},{1,17},{2,18},{3,19},{4,20},{5,21},{6,22},{7,23},{8,24},{9,... | collective-permute-start | bytes 344072 | tf_op jit(solution)/shard_map/ppermute | solution.py:610
  3.6 10.8 %collective-permute-start.1 = (f32[7,32,128]{2,1,0:T(8,128)S(1)}, f32[7,32,128]{2,1,0:T(8,128)S(1)}, u32[]{:S(2)}, u32[]{:S(2)}) collective-permute-start(f32[7,32,128]{2,1,0:T(8,128)S(1)} %get-tuple-element.39.oxo), channel_id=1, source_target_pairs={{0,1},{1,0},{2,3},{3,2},{4,5},{5,4},{6,7},{7,6},{8,9},{9,8},{10,11... | collective-permute-start | bytes 344072 | tf_op jit(solution)/shard_map/ppermute | solution.py:610
  8.4 6.0 %collective-permute-start.2 = (f32[7,16,128]{2,1,0:T(8,128)S(1)}, f32[7,16,128]{2,1,0:T(8,128)S(1)}, u32[]{:S(2)}, u32[]{:S(2)}) collective-permute-start(f32[7,16,128]{2,1,0:T(8,128)S(1)} %get-tuple-element.40.oyo), channel_id=1, source_target_pairs={{0,16},{1,2},{2,1},{3,4},{4,3},{5,6},{6,5},{7,8},{8,7},{9,10},{10,... | collective-permute-start | bytes 172040 | tf_op jit(solution)/shard_map/ppermute | solution.py:610
  9.9 4.6 %collective-permute-start.3 = (f32[7,16,128]{2,1,0:T(8,128)S(1)}, f32[7,16,128]{2,1,0:T(8,128)S(1)}, u32[]{:S(2)}, u32[]{:S(2)}) collective-permute-start(f32[7,16,128]{2,1,0:T(8,128)S(1)} %get-tuple-element.41.oye), channel_id=1, source_target_pairs={{0,1},{1,0},{2,3},{3,2},{4,5},{5,4},{6,7},{7,6},{8,9},{9,8},{10,11... | collective-permute-start | bytes 172040 | tf_op jit(solution)/shard_map/ppermute | solution.py:610
  15.4 15.0 %all-to-all-start = ((f32[16,32,128]{2,1,0:T(8,128)}), f32[16,32,128]{2,1,0:T(8,128)S(1)}, u32[]{:S(2)}, u32[]{:S(2)}) async-start(f32[16,32,128]{2,1,0:T(8,128)} %third.1), calls=%async_computation | async-start | bytes 524288 | tf_op jit(solution)/shard_map/all_to_all | solution.py:627
  30.7 9.4 %collective-permute-start.4 = (f32[4,32,128]{2,1,0:T(8,128)S(1)}, f32[4,32,128]{2,1,0:T(8,128)S(1)}, u32[]{:S(2)}, u32[]{:S(2)}) collective-permute-start(f32[4,32,128]{2,1,0:T(8,128)S(1)} %get-tuple-element.63), channel_id=1, source_target_pairs={{0,16},{1,17},{2,18},{3,19},{4,20},{5,21},{6,22},{7,23},{8,24},{9,... | collective-permute-start | bytes 196616 | tf_op jit(solution)/shard_map/ppermute | solution.py:610
  33.1 7.0 %collective-permute-start.5 = (f32[4,32,128]{2,1,0:T(8,128)S(1)}, f32[4,32,128]{2,1,0:T(8,128)S(1)}, u32[]{:S(2)}, u32[]{:S(2)}) collective-permute-start(f32[4,32,128]{2,1,0:T(8,128)S(1)} %get-tuple-element.64), channel_id=1, source_target_pairs={{0,1},{1,0},{2,3},{3,2},{4,5},{5,4},{6,7},{7,6},{8,9},{9,8},{10,11... | collective-permute-start | bytes 196616 | tf_op jit(solution)/shard_map/ppermute | solution.py:610
  34.3 5.7 %collective-permute-start.6 = (f32[4,16,128]{2,1,0:T(8,128)S(1)}, f32[4,16,128]{2,1,0:T(8,128)S(1)}, u32[]{:S(2)}, u32[]{:S(2)}) collective-permute-start(f32[4,16,128]{2,1,0:T(8,128)S(1)} %get-tuple-element.65), channel_id=1, source_target_pairs={{0,16},{1,2},{2,1},{3,4},{4,3},{5,6},{6,5},{7,8},{8,7},{9,10},{10,... | collective-permute-start | bytes 98312 | tf_op jit(solution)/shard_map/ppermute | solution.py:610
  34.4 5.7 %collective-permute-start.7 = (f32[4,16,128]{2,1,0:T(8,128)S(1)}, f32[4,16,128]{2,1,0:T(8,128)S(1)}, u32[]{:S(2)}, u32[]{:S(2)}) collective-permute-start(f32[4,16,128]{2,1,0:T(8,128)S(1)} %get-tuple-element.66), channel_id=1, source_target_pairs={{0,1},{1,0},{2,3},{3,2},{4,5},{5,4},{6,7},{7,6},{8,9},{9,8},{10,11... | collective-permute-start | bytes 98312 | tf_op jit(solution)/shard_map/ppermute | solution.py:610

commit v4 on v3

--- a/solution.py
+++ b/solution.py
@@ -203,7 +203,7 @@
 
     def first(
         adj_hbm, vel_hbm, dif_hbm, con_hbm, rec_hbm,
-        xe_ref, xo_ref, ye_ref, yo_ref,
+        conc_ref, count_ref, xe_ref, xo_ref, ye_ref, yo_ref,
         adj_ref, vel_ref, dif_ref, con_ref, rec_ref, side_ref, sem,
     ):
         copies = [
@@ -217,6 +217,7 @@
         row_e, row_o, col_e, col_o = edges_at()
         copies[0].wait()
         counts = receptor_counts(rec_ref[...], cols)
+        count_ref[...] = counts
         wait_all(copies[1:4])
         side_ref[0] = vel_ref[1].astype(F32).reshape(cols, 128)
         side_ref[1] = dif_ref[...].astype(F32).reshape(cols, 128)
@@ -229,7 +230,9 @@
             for k in range(3):
                 out[4 + k] = edge_col(side_ref, k, col)
         copies[4].wait()
-        adj_ref[3] += counts
+        conc = adj_ref[3] + counts
+        adj_ref[3] = conc
+        conc_ref[...] = conc
         for k in range(4):
             xe_ref[k] = edge_row(adj_ref, k, row_e)
             xo_ref[k] = edge_row(adj_ref, k, row_o)
@@ -237,21 +240,17 @@
             yo_ref[k] = edge_col(adj_ref, k, col_o)
 
     def second(
-        adj_hbm, vel_hbm, dif_hbm, rec_hbm, height_hbm, src_hbm, weight_hbm,
+        conc_ref, count_ref, vel_hbm, dif_hbm, height_hbm, src_hbm, weight_hbm,
         now_ref, soon_ref, hot_ref, weight_ref, exe_ref, exo_ref, eye_ref, eyo_ref,
-        state_ref, vel_ref, dif_ref, rec_ref, height_ref, src_ref,
-        pad_ref, fluid_ref, count_ref, next_ref, sem,
+        state_ref, vel_ref, dif_ref, height_ref, src_ref,
+        pad_ref, fluid_ref, next_ref, sem,
     ):
         copies = [
             pltpu.make_async_copy(src_hbm, src_ref, sem.at[0]),
             pltpu.make_async_copy(height_hbm, height_ref, sem.at[1]),
-            pltpu.make_async_copy(rec_hbm, rec_ref, sem.at[2]),
-            pltpu.make_async_copy(dif_hbm, dif_ref, sem.at[3]),
-            pltpu.make_async_copy(
-                adj_hbm.at[3], state_ref.at[0, inside[0], inside[1], :], sem.at[4]
-            ),
-            pltpu.make_async_copy(vel_hbm, vel_ref, sem.at[5]),
-            pltpu.make_async_copy(weight_hbm, weight_ref, sem.at[6]),
+            pltpu.make_async_copy(dif_hbm, dif_ref, sem.at[2]),
+            pltpu.make_async_copy(vel_hbm, vel_ref, sem.at[3]),
+            pltpu.make_async_copy(weight_hbm, weight_ref, sem.at[4]),
         ]
         start_all(copies)
         row_e, row_o, col_e, col_o = edges_at()
@@ -261,11 +260,9 @@
         index = row_values(src_ref[...]).astype(jnp.int32)
         copies[1].wait()
         fluid_ref[...] = row_values(height_ref[...])
-        copies[2].wait()
-        count_ref[...] = receptor_counts(rec_ref[...], cols)
-        wait_all(copies[3:6])
+        state_ref[0, 1 : cx + 1, PADY : PADY + cy, :] = conc_ref[...].reshape(cx, cy, 128)
+        wait_all(copies[2:4])
         fill_pads(pad_ref, vel_ref, dif_ref)
-        state_ref[0, 1 : cx + 1, PADY : PADY + cy, :] += count_ref[...].reshape(cx, cy, 128)
         for i, jv in cells():
             at = pl.ds(i * cy + 8 * jv, 8)
             c, e = cell_coefficients(i, jv, vertical(vel_ref, i, jv), pad_ref, fluid_ref)
@@ -286,9 +283,9 @@
         hot_ref[...] = jnp.where(jnp.logical_and(near, index >= 0), 1.0, 0.0).astype(BF16)
         hot = [(index == lane + t).astype(F32).astype(BF16) for t in range(0, cols, 128)]
         hot = jnp.concatenate(hot, axis=1)
-        copies[6].wait()
+        copies[4].wait()
         weight = weight_ref[...]
-        conc = state_ref[0, 1 : cx + 1, PADY : PADY + cy, :].reshape(cols, 128)
+        conc = conc_ref[...]
         both = jnp.concatenate([split3(conc), split3(next_ref[...])], axis=1)
         picked = jnp.dot(hot, both, preferred_element_type=F32)
         now_ref[...] = weight * join3(picked[:, :384])
@@ -333,7 +330,7 @@
 
     def fourth(
         adj_hbm, vel_hbm, dif_hbm, con_hbm, rec_hbm, height_hbm, dst_hbm, hxe, hxo, hyo, hye,
-        last_hbm, coef_hbm, hot_ref, xe_ref, xo_ref, ye_ref, yo_ref,
+        last_hbm, coef_out, hot_ref, xe_ref, xo_ref, ye_ref, yo_ref,
         cxe_ref, cxo_ref, cye_ref, cyo_ref,
         state_ref, vel_ref, dif_ref, con_ref, rec_ref, height_ref, dst_ref,
         pad_ref, fluid_ref, count_ref, coef_ref, next_ref, flat_ref, last_ref, sem,
@@ -371,6 +368,8 @@
             c, e = cell_coefficients(i, jv, vertical(vel_ref, i, jv), pad_ref, fluid_ref)
             c = c + cell_gradients(i, jv, e, pad_ref)
             for n in range(10):
+                if n < 7:
+                    coef_out[n, at, :] = c[n]
                 coef_ref[n, at, :] = c[n]
             conc = state_ref[3, i + 1, j : j + 8, :]
             for k in range(4):
@@ -378,8 +377,6 @@
                 value = value + count_ref[at, :] if k == 3 else value - c[7 + k] * conc
                 next_ref[k, i + 1, j : j + 8, :] = value
                 flat_ref[k, at, :] = value
-        outs = [pltpu.make_async_copy(coef_ref.at[pl.ds(0, 7)], coef_hbm, sem.at[7])]
-        outs[0].start()
         for k in range(4):
             xe_ref[k] = edge_row(flat_ref, k, row_e)
             xo_ref[k] = edge_row(flat_ref, k, row_o)
@@ -395,15 +392,15 @@
                 if k < 3:
                     value = value - c[7 + k] * conc
                 last_ref[k, i, 8 * jv : 8 * jv + 8, :] = value
-        outs.append(pltpu.make_async_copy(last_ref, last_hbm, sem.at[8]))
-        outs[1].start()
+        out = pltpu.make_async_copy(last_ref, last_hbm, sem.at[7])
+        out.start()
         par_x = lax.rem(lax.axis_index("gx"), 2)
         par_y = lax.rem(lax.axis_index("gy"), 2)
         cxe_ref[...] = coef_ref[1 + par_x, pl.ds(pl.multiple_of(row_e * cy, 8), cy), :]
         cxo_ref[...] = coef_ref[2 - par_x, pl.ds(pl.multiple_of(row_o * cy, 8), cy), :]
         cye_ref[...] = edge_col(coef_ref, 3 + par_y, col_e)
         cyo_ref[...] = edge_col(coef_ref, 4 - par_y, col_o)
-        wait_all(outs)
+        out.wait()
 
     def fifth(
         arrived_ref, hot_ref, xe_in, xo_in, ye_in, yo_in,
@@ -422,16 +419,15 @@
         yo_ref[2] += edge_col(wall_ref, 0, col_o)
 
     def sixth(
-        last_hbm, coef_hbm, wall_ref, arrived_ref, hot_ref,
+        last_hbm, coef_ref, wall_ref, arrived_ref, hot_ref,
         out_hbm, sxe_ref, sxo_ref, sye_ref, syo_ref,
-        coef_ref, pad_ref, final_ref, add_ref, sem,
+        pad_ref, final_ref, add_ref, sem,
     ):
         row_e, row_o, col_e, col_o = edges_at()
         tile_e = pl.ds(pl.multiple_of(col_e // 8 * 8, 8), 8)
         tile_o = pl.ds(pl.multiple_of(col_o // 8 * 8, 8), 8)
         copies = [
             pltpu.make_async_copy(last_hbm.at[2], final_ref, sem.at[0]),
-            pltpu.make_async_copy(coef_hbm, coef_ref, sem.at[1]),
             pltpu.make_async_copy(last_hbm.at[:, row_e], sxe_ref, sem.at[2]),
             pltpu.make_async_copy(last_hbm.at[:, row_o], sxo_ref, sem.at[3]),
             pltpu.make_async_copy(last_hbm.at[:, :, tile_e, :], sye_ref, sem.at[4]),
@@ -443,18 +439,26 @@
         clear_halo(pad_ref, (0,))
         pad_ref[0, 1 : cx + 1, PADY : PADY + cy, :] = wall_ref[0].reshape(cx, cy, 128)
         wait_all(copies)
+        outs = []
         for i, jv in cells():
             at = pl.ds(i * cy + 8 * jv, 8)
             c = [coef_ref[n, at, :] for n in range(7)]
             value = final_ref[i, 8 * jv : 8 * jv + 8, :] + add_ref[at, :]
             final_ref[i, 8 * jv : 8 * jv + 8, :] = value + cell_step(i, jv, c, pad_ref, 0)
-        copy = pltpu.make_async_copy(final_ref, out_hbm.at[2], sem.at[6])
-        copy.start()
+            if (i + 1) % (cx // 4) == 0 and jv == cy // 8 - 1:
+                rows = pl.ds(i + 1 - cx // 4, cx // 4)
+                done = len(outs)
+                outs.append(
+                    pltpu.make_async_copy(
+                        final_ref.at[rows], out_hbm.at[2, rows], sem.at[6 + done]
+                    )
+                )
+                outs[done].start()
         sxe_ref[2] = final_ref[row_e]
         sxo_ref[2] = final_ref[row_o]
         sye_ref[2] = final_ref[:, tile_e, :]
         syo_ref[2] = final_ref[:, tile_o, :]
-        copy.wait()
+        wait_all(outs)
 
     def seventh(
         last_hbm, sxe, sxo, sye, syo, hxe, hxo, hyo, hye, cxe, cxo, cye, cyo,
@@ -532,30 +536,30 @@
         line = vm(1, rcp, dtype=jnp.int32)
         return (
             call(
-                first, "first", [HBM] * 5, (VMEM,) * 4,
-                (sds(7, cy, 128), sds(7, cy, 128), sds(7, cx, 128), sds(7, cx, 128)),
+                first, "first", [HBM] * 5, (VMEM,) * 6,
+                (sds(cols, 128), sds(cols, 128), sds(7, cy, 128), sds(7, cy, 128), sds(7, cx, 128), sds(7, cx, 128)),
                 [vm(4, cols, 128), vm(2, cx, cy, 128, dtype=BF16)] + three[1:]
                 + [line, vm(3, cols, 128), dma(5)],
                 4 << 20,
             ),
             call(
-                second, "second", [HBM] * 7, (VMEM,) * 8,
+                second, "second", [VMEM] * 2 + [HBM] * 5, (VMEM,) * 8,
                 (sds(slots, 128), sds(slots, 128),
                  jax.ShapeDtypeStruct((slots, 128), BF16), sds(slots, 128)) + sides,
-                [vm(1, px, py, 128)] + three[:2] + [line, height, int_table]
-                + [vm(3, px, py, 128), vm(cols, 128), vm(cols, 128), vm(cols, 128), dma(7)],
+                [vm(1, px, py, 128)] + three[:2] + [height, int_table]
+                + [vm(3, px, py, 128), vm(cols, 128), vm(cols, 128), dma(5)],
                 8 << 20,
             ),
             call(
                 third, "third", [VMEM] * 16, VMEM, sds(owners, 2 * cap, 128), [], 2 << 20,
             ),
             call(
-                fourth, "fourth", [HBM] * 7 + [VMEM] * 4, (HBM,) * 2 + (VMEM,) * 9,
-                (hbm(4, cx, cy, 128), hbm(7, cols, 128), jax.ShapeDtypeStruct((cols, slots), BF16))
+                fourth, "fourth", [HBM] * 7 + [VMEM] * 4, (HBM,) + (VMEM,) * 10,
+                (hbm(4, cx, cy, 128), sds(7, cols, 128), jax.ShapeDtypeStruct((cols, slots), BF16))
                 + strips + sides,
                 [padded] + three + [line, height, int_table]
                 + [padded, vm(cols, 128), vm(cols, 128), vm(10, cols, 128), padded,
-                   vm(4, cols, 128), vm(4, cx, cy, 128), dma(9)],
+                   vm(4, cols, 128), vm(4, cx, cy, 128), dma(8)],
                 10 << 20,
             ),
             call(
@@ -563,10 +567,10 @@
                 2 << 20,
             ),
             call(
-                sixth, "sixth", [HBM] * 2 + [VMEM] * 3, (HBM,) + (VMEM,) * 4,
+                sixth, "sixth", [HBM] + [VMEM] * 4, (HBM,) + (VMEM,) * 4,
                 (hbm(4, cx, cy, 128), sds(4, cy, 128), sds(4, cy, 128),
                  sds(4, cx, 8, 128), sds(4, cx, 8, 128)),
-                [vm(7, cols, 128), vm(1, px, py, 128), vm(cx, cy, 128), vm(cols, 128), dma(7)],
+                [vm(1, px, py, 128), vm(cx, cy, 128), vm(cols, 128), dma(10)],
                 5 << 20,
                 input_output_aliases={0: 0},
             ),
@@ -618,10 +622,10 @@
     def pinned(*arrays):
         return [pltpu.with_memory_space_constraint(x, pltpu.HBM) for x in arrays]
 
-    own = first(*pinned(flat, velocity, diffusivity, concentration, line))
+    conc, counts, *own = first(*pinned(flat, velocity, diffusivity, concentration, line))
     halos = exchange(*own)
     now, soon, hot, weight, *fluid = second(
-        *pinned(adjoint, velocity, diffusivity, line, heights, src, weight)
+        conc, counts, *pinned(velocity, diffusivity, heights, src, weight)
     )
     blocks = third(*[halos[n] for n in [0, 1, 3, 2]], *own, *fluid, now, soon, hot, weight)
     arrived = lax.all_to_all(blocks, "gx", split_axis=0, concat_axis=0, tiled=True)
@@ -631,7 +635,7 @@
     edges, sides = rest[:4], rest[4:]
     wall, *edges = fifth(arrived, hot, *edges)
     halos = exchange(*edges)
-    out, *strips = sixth(*pinned(last, coefs), wall, arrived, hot)
+    out, *strips = sixth(*pinned(last), coefs, wall, arrived, hot)
     return seventh(*pinned(out), *strips, *[halos[n] for n in [0, 1, 3, 2]], *sides)
 
 

time: 41.4 us -> 41.4 us (level)
  waiting for transfers between devices: 8.25 us -> 9.07 us
  Pallas kernels: 13.8 us -> 13 us
    ppermute x8, waiting for transfers between devices: 2.41 us -> 3.27 us  [exchange(): lax.ppermute(e, ('gx', 'gy'), pairs)]
    pallas_call x3, Pallas kernels: 7.26 us -> 6.41 us  [the longest x1 2.52 us: shards(): second(conc, counts, *pinned(velocity, diffusivity, heights, src, weight))]
  transfers between devices with their start and end apart: 9 -> 9, of which waited for: 3 -> 3; matrix products, arithmetic and copies ran while one was open for 0% -> 0% of each run, Pallas kernels for 24% -> 22%
where the time goes in v4:
time: 41.4 us; the launch traced here: 41 us
  starting transfers between devices  18.9 us (46%)
  Pallas kernels  13 us (31%)
  waiting for transfers between devices  9.07 us (22%)
    ppermute x8, starting transfers between devices, exchange(): lax.ppermute(e, ('gx', 'gy'), pairs)  14.1 us
    all_to_all x1, waiting for transfers between devices, shards(): lax.all_to_all(blocks, 'gx', split_axis=0, concat_axis=0, tiled=True)  5.8 us
    all_to_all x1, starting transfers between devices, shards(): lax.all_to_all(blocks, 'gx', split_axis=0, concat_axis=0, tiled=True)  4.79 us
    pallas_call x1, Pallas kernels, shards(): fourth(*pinned(adjoint, velocity, diffusivity, concentration, line, heigh...  4.42 us
    ppermute x8, waiting for transfers between devices, exchange(): lax.ppermute(e, ('gx', 'gy'), pairs)  3.27 us
    pallas_call x1, Pallas kernels, shards(): second(conc, counts, *pinned(velocity, diffusivity, heights, src, weight))  2.52 us
    pallas_call x1, Pallas kernels, shards(): out, *strips = sixth(*pinned(last), coefs, wall, arrived, hot)  2.28 us
    pallas_call x1, Pallas kernels, shards(): first(*pinned(flat, velocity, diffusivity, concentration, line))  1.61 us
  transfers between devices with their start and end apart: 9, of which 3 were waited for; matrix products, arithmetic and copies ran while one was open for 0% of the time, Pallas kernels for 22%

profile of v4, /device:TPU:10, one launch (start us, length us, event | category | flops | bytes accessed | tf_op | source)
XLA Modules:
  0.0 41.0 jit_solution(11997987808860335861)
XLA Ops:
  0.0 1.6 %first.1 = (f32[512,128]{1,0:T(8,128)S(1)}, f32[512,128]{1,0:T(8,128)S(1)}, f32[7,32,128]{2,1,0:T(8,128)S(1)}, f32[7,32,128]{2,1,0:T(8,128)S(1)}, f32[7,16,128]{2,1,0:T(8,128)S(1)}, /*index=5*/f32[7,16,128]{2,1,0:T(8,128)S(1)}) custom-call(f32[4,512,128]{2,1,0:T(8,128)} %bitcast.5, bf16[3,16,32,128]{3,2,1,0:T(8,128)(2,1)} %vel_hbm.5, ...), custom_call_target="tpu_custom_call" | custom-call | flops 4194304 | bytes 4194304 | tf_op jit(solution)/shard_map/first/pallas_call | solution.py:625
  1.6 2.0 %collective-permute-start = (f32[7,32,128]{2,1,0:T(8,128)S(1)}, f32[7,32,128]{2,1,0:T(8,128)S(1)}, u32[]{:S(2)}, u32[]{:S(2)}) collective-permute-start(f32[7,32,128]{2,1,0:T(8,128)S(1)} %get-tuple-element.40.oxe), channel_id=1, source_target_pairs={{0,16},{1,17},{2,18},{3,19},{4,20},{5,21},{6,22},{7,23},{8,24},{9,... | collective-permute-start | bytes 344072 | tf_op jit(solution)/shard_map/ppermute | solution.py:614
  3.6 4.8 %collective-permute-start.1 = (f32[7,32,128]{2,1,0:T(8,128)S(1)}, f32[7,32,128]{2,1,0:T(8,128)S(1)}, u32[]{:S(2)}, u32[]{:S(2)}) collective-permute-start(f32[7,32,128]{2,1,0:T(8,128)S(1)} %get-tuple-element.41.oxo), channel_id=1, source_target_pairs={{0,1},{1,0},{2,3},{3,2},{4,5},{5,4},{6,7},{7,6},{8,9},{9,8},{10,11... | collective-permute-start | bytes 344072 | tf_op jit(solution)/shard_map/ppermute | solution.py:614
  8.5 1.4 %collective-permute-start.2 = (f32[7,16,128]{2,1,0:T(8,128)S(1)}, f32[7,16,128]{2,1,0:T(8,128)S(1)}, u32[]{:S(2)}, u32[]{:S(2)}) collective-permute-start(f32[7,16,128]{2,1,0:T(8,128)S(1)} %get-tuple-element.42.oyo), channel_id=1, source_target_pairs={{0,16},{1,2},{2,1},{3,4},{4,3},{5,6},{6,5},{7,8},{8,7},{9,10},{10,... | collective-permute-start | bytes 172040 | tf_op jit(solution)/shard_map/ppermute | solution.py:614
  9.9 1.3 %collective-permute-start.3 = (f32[7,16,128]{2,1,0:T(8,128)S(1)}, f32[7,16,128]{2,1,0:T(8,128)S(1)}, u32[]{:S(2)}, u32[]{:S(2)}) collective-permute-start(f32[7,16,128]{2,1,0:T(8,128)S(1)} %get-tuple-element.43.oye), channel_id=1, source_target_pairs={{0,1},{1,0},{2,3},{3,2},{4,5},{5,4},{6,7},{7,6},{8,9},{9,8},{10,11... | collective-permute-start | bytes 172040 | tf_op jit(solution)/shard_map/ppermute | solution.py:614
  11.2 2.5 %second.1 = (f32[256,128]{1,0:T(8,128)S(1)}, f32[256,128]{1,0:T(8,128)S(1)}, bf16[256,128]{1,0:T(8,128)(2,1)S(1)}, f32[256,128]{1,0:T(8,128)S(1)}, f32[32,128]{1...) custom-call(f32[512,128]{1,0:T(8,128)S(1)} %get-tuple-element.46.conc_ref, ...), custom_call_target="tpu_custom_call" | custom-call | flops 8388608 | bytes 8388608 | tf_op jit(solution)/shard_map/second/pallas_call | solution.py:627
  13.7 0.8 %collective-permute-done.2.hyo = f32[7,16,128]{2,1,0:T(8,128)S(1)} collective-permute-done((f32[7,16,128]{2,1,0:T(8,128)S(1)}, f32[7,16,128]{2,1,0:T(8,128)S(1)}, u32[]{:S(2)}, u32[]{:S(2)}) %collective-permute-start.2) | collective-permute-done | bytes 57376 | tf_op jit(solution)/shard_map/ppermute | solution.py:614
  14.5 0.0 collective-permute-done.3.hye
  14.5 0.0 collective-permute-done.hxe
  14.5 0.0 collective-permute-done.1.hxo
  14.5 0.9 %third.1 = f32[16,32,128]{2,1,0:T(8,128)} custom-call(f32[7,32,128]{2,1,0:T(8,128)S(1)} %collective-permute-done.hxe, f32[7,32,128]{2,1,0:T(8,128)S(1)} %collective-permute-done.1.hxo, f32[7,16,128]{2,1,0:T(8,128)S(1)} %collective-permute-done.2.hyo, f32[7,16,128]{2,1,0:T(8,128)S(1)} %collective-permute-done.3.hye, f32[7,32,128]{2,1,0:T(8,128)S(1)} %get-tuple-element.40.oxe, ...), custom_call_target="tpu_custom_call" | custom-call | flops 2097152 | bytes 2097152 | tf_op jit(solution)/shard_map/third/pallas_call | solution.py:630
  15.4 4.8 %all-to-all-start = ((f32[16,32,128]{2,1,0:T(8,128)}), f32[16,32,128]{2,1,0:T(8,128)S(1)}, u32[]{:S(2)}, u32[]{:S(2)}) async-start(f32[16,32,128]{2,1,0:T(8,128)} %third.1), calls=%async_computation | async-start | bytes 524288 | tf_op jit(solution)/shard_map/all_to_all | solution.py:631
  20.2 4.4 %fourth.1 = (f32[4,16,32,128]{3,2,1,0:T(8,128)}, f32[7,512,128]{2,1,0:T(8,128)S(1)}, bf16[512,256]{1,0:T(8,128)(2,1)S(1)}, f32[4,32,128]{2,1,0:T(8,128)S(1)}, f3...) custom-call(f32[4,16,32,128]{3,2,1,0:T(8,128)} %adj_hbm.1, ...), custom_call_target="tpu_custom_call" | custom-call | flops 10485760 | bytes 10485760 | tf_op jit(solution)/shard_map/fourth/pallas_call | solution.py:632
  24.6 5.8 %all-to-all-done.arrived_ref = f32[16,32,128]{2,1,0:T(8,128)S(1)} async-done(((f32[16,32,128]{2,1,0:T(8,128)}), f32[16,32,128]{2,1,0:T(8,128)S(1)}, u32[]{:S(2)}, u32[]{:S(2)}) %all-to-all-start) | async-done | bytes 262176 | tf_op jit(solution)/shard_map/all_to_all | solution.py:631
  30.4 0.3 fifth.1
  30.7 2.3 %collective-permute-start.4 = (f32[4,32,128]{2,1,0:T(8,128)S(1)}, f32[4,32,128]{2,1,0:T(8,128)S(1)}, u32[]{:S(2)}, u32[]{:S(2)}) collective-permute-start(f32[4,32,128]{2,1,0:T(8,128)S(1)} %get-tuple-element.67), channel_id=1, source_target_pairs={{0,16},{1,17},{2,18},{3,19},{4,20},{5,21},{6,22},{7,23},{8,24},{9,... | collective-permute-start | bytes 196616 | tf_op jit(solution)/shard_map/ppermute | solution.py:614
  33.1 1.3 %collective-permute-start.5 = (f32[4,32,128]{2,1,0:T(8,128)S(1)}, f32[4,32,128]{2,1,0:T(8,128)S(1)}, u32[]{:S(2)}, u32[]{:S(2)}) collective-permute-start(f32[4,32,128]{2,1,0:T(8,128)S(1)} %get-tuple-element.68), channel_id=1, source_target_pairs={{0,1},{1,0},{2,3},{3,2},{4,5},{5,4},{6,7},{7,6},{8,9},{9,8},{10,11... | collective-permute-start | bytes 196616 | tf_op jit(solution)/shard_map/ppermute | solution.py:614
  34.3 0.0 collective-permute-start.6
  34.3 1.0 %collective-permute-start.7 = (f32[4,16,128]{2,1,0:T(8,128)S(1)}, f32[4,16,128]{2,1,0:T(8,128)S(1)}, u32[]{:S(2)}, u32[]{:S(2)}) collective-permute-start(f32[4,16,128]{2,1,0:T(8,128)S(1)} %get-tuple-element.70), channel_id=1, source_target_pairs={{0,1},{1,0},{2,3},{3,2},{4,5},{5,4},{6,7},{7,6},{8,9},{9,8},{10,11... | collective-permute-start | bytes 98312 | tf_op jit(solution)/shard_map/ppermute | solution.py:614
  35.3 2.3 %sixth.1 = (f32[4,16,32,128]{3,2,1,0:T(8,128)}, f32[4,32,128]{2,1,0:T(8,128)S(1)}, f32[4,32,128]{2,1,0:T(8,128)S(1)}, f32[4,16,8,128]{3,2,1,0:T(8,128)S(1)}, f32[4,16,8,128]{3,2,1,0:T(8,128)S(1)}) custom-call(f32[4,16,32,128]{3,2,1,0:T(8,128)} %get-tuple-element.44.last_hbm, ...), custom_call_target="tpu_custom_call", output_to_operand_aliasing={{0}: (0, {})} | custom-call | flops 5242880 | bytes 5242880 | tf_op jit(solution)/shard_map/sixth/pallas_call | solution.py:638
  37.6 2.5 %collective-permute-done.6.hyo = f32[4,16,128]{2,1,0:T(8,128)S(1)} collective-permute-done((f32[4,16,128]{2,1,0:T(8,128)S(1)}, f32[4,16,128]{2,1,0:T(8,128)S(1)}, u32[]{:S(2)}, u32[]{:S(2)}) %collective-permute-start.6) | collective-permute-done | bytes 32800 | tf_op jit(solution)/shard_map/ppermute | solution.py:614
  40.1 0.0 collective-permute-done.7.hye
  40.1 0.0 collective-permute-done.4.hxe
  40.1 0.0 collective-permute-done.5.hxo
  40.1 0.9 %seventh.1 = f32[4,16,32,128]{3,2,1,0:T(8,128)} custom-call(f32[4,16,32,128]{3,2,1,0:T(8,128)} %get-tuple-element.62.last_hbm, f32[4,32,128]{2,1,0:T(8,128)S(1)} %get-tuple-element.63.sxe, f32[4,32,128]{2,1,0:T(8,128)S(1)} %get-tuple-element.64.sxo, f32[4,16,8,128]{3,2,1,0:T(8,128)S(1)} %get-tuple-element.65.sye, ...), custom_call_target="tpu_custom_call", output_to_operand_aliasing={{}: (0, {})} | custom-call | flops 2097152 | bytes 2097152 | tf_op jit(solution)/shard_map/seventh/pallas_call | solution.py:639
Async XLA Ops:
  1.6 12.9 %collective-permute-start = (f32[7,32,128]{2,1,0:T(8,128)S(1)}, f32[7,32,128]{2,1,0:T(8,128)S(1)}, u32[]{:S(2)}, u32[]{:S(2)}) collective-permute-start(f32[7,32,128]{2,1,0:T(8,128)S(1)} %get-tuple-element.40.oxe), channel_id=1, source_target_pairs={{0,16},{1,17},{2,18},{3,19},{4,20},{5,21},{6,22},{7,23},{8,24},{9,... | collective-permute-start | bytes 344072 | tf_op jit(solution)/shard_map/ppermute | solution.py:614
  3.6 10.8 %collective-permute-start.1 = (f32[7,32,128]{2,1,0:T(8,128)S(1)}, f32[7,32,128]{2,1,0:T(8,128)S(1)}, u32[]{:S(2)}, u32[]{:S(2)}) collective-permute-start(f32[7,32,128]{2,1,0:T(8,128)S(1)} %get-tuple-element.41.oxo), channel_id=1, source_target_pairs={{0,1},{1,0},{2,3},{3,2},{4,5},{5,4},{6,7},{7,6},{8,9},{9,8},{10,11... | collective-permute-start | bytes 344072 | tf_op jit(solution)/shard_map/ppermute | solution.py:614
  8.5 6.0 %collective-permute-start.2 = (f32[7,16,128]{2,1,0:T(8,128)S(1)}, f32[7,16,128]{2,1,0:T(8,128)S(1)}, u32[]{:S(2)}, u32[]{:S(2)}) collective-permute-start(f32[7,16,128]{2,1,0:T(8,128)S(1)} %get-tuple-element.42.oyo), channel_id=1, source_target_pairs={{0,16},{1,2},{2,1},{3,4},{4,3},{5,6},{6,5},{7,8},{8,7},{9,10},{10,... | collective-permute-start | bytes 172040 | tf_op jit(solution)/shard_map/ppermute | solution.py:614
  9.9 4.6 %collective-permute-start.3 = (f32[7,16,128]{2,1,0:T(8,128)S(1)}, f32[7,16,128]{2,1,0:T(8,128)S(1)}, u32[]{:S(2)}, u32[]{:S(2)}) collective-permute-start(f32[7,16,128]{2,1,0:T(8,128)S(1)} %get-tuple-element.43.oye), channel_id=1, source_target_pairs={{0,1},{1,0},{2,3},{3,2},{4,5},{5,4},{6,7},{7,6},{8,9},{9,8},{10,11... | collective-permute-start | bytes 172040 | tf_op jit(solution)/shard_map/ppermute | solution.py:614
  15.4 15.0 %all-to-all-start = ((f32[16,32,128]{2,1,0:T(8,128)}), f32[16,32,128]{2,1,0:T(8,128)S(1)}, u32[]{:S(2)}, u32[]{:S(2)}) async-start(f32[16,32,128]{2,1,0:T(8,128)} %third.1), calls=%async_computation | async-start | bytes 524288 | tf_op jit(solution)/shard_map/all_to_all | solution.py:631
  30.7 9.3 %collective-permute-start.4 = (f32[4,32,128]{2,1,0:T(8,128)S(1)}, f32[4,32,128]{2,1,0:T(8,128)S(1)}, u32[]{:S(2)}, u32[]{:S(2)}) collective-permute-start(f32[4,32,128]{2,1,0:T(8,128)S(1)} %get-tuple-element.67), channel_id=1, source_target_pairs={{0,16},{1,17},{2,18},{3,19},{4,20},{5,21},{6,22},{7,23},{8,24},{9,... | collective-permute-start | bytes 196616 | tf_op jit(solution)/shard_map/ppermute | solution.py:614
  33.1 7.0 %collective-permute-start.5 = (f32[4,32,128]{2,1,0:T(8,128)S(1)}, f32[4,32,128]{2,1,0:T(8,128)S(1)}, u32[]{:S(2)}, u32[]{:S(2)}) collective-permute-start(f32[4,32,128]{2,1,0:T(8,128)S(1)} %get-tuple-element.68), channel_id=1, source_target_pairs={{0,1},{1,0},{2,3},{3,2},{4,5},{5,4},{6,7},{7,6},{8,9},{9,8},{10,11... | collective-permute-start | bytes 196616 | tf_op jit(solution)/shard_map/ppermute | solution.py:614
  34.3 5.7 %collective-permute-start.6 = (f32[4,16,128]{2,1,0:T(8,128)S(1)}, f32[4,16,128]{2,1,0:T(8,128)S(1)}, u32[]{:S(2)}, u32[]{:S(2)}) collective-permute-start(f32[4,16,128]{2,1,0:T(8,128)S(1)} %get-tuple-element.69), channel_id=1, source_target_pairs={{0,16},{1,2},{2,1},{3,4},{4,3},{5,6},{6,5},{7,8},{8,7},{9,10},{10,... | collective-permute-start | bytes 98312 | tf_op jit(solution)/shard_map/ppermute | solution.py:614
  34.3 5.7 %collective-permute-start.7 = (f32[4,16,128]{2,1,0:T(8,128)S(1)}, f32[4,16,128]{2,1,0:T(8,128)S(1)}, u32[]{:S(2)}, u32[]{:S(2)}) collective-permute-start(f32[4,16,128]{2,1,0:T(8,128)S(1)} %get-tuple-element.70), channel_id=1, source_target_pairs={{0,1},{1,0},{2,3},{3,2},{4,5},{5,4},{6,7},{7,6},{8,9},{9,8},{10,11... | collective-permute-start | bytes 98312 | tf_op jit(solution)/shard_map/ppermute | solution.py:614

commit v5 on v4

--- a/solution.py
+++ b/solution.py
@@ -467,16 +467,17 @@
         row_e, row_o, col_e, col_o = edges_at()
         _, _, wrap_x, wrap_y = edge_signs()
         near_e, near_o = cye[...], jnp.where(wrap_y, 0.0, cyo[...])
+        here = lax.broadcasted_iota(jnp.int32, (8, 128), 0)
         tile_e = col_e // 8 * 8
         tile_o = col_o // 8 * 8
         for k in range(4):
             dye[k] = near_e * hye[k]
             dyo[k] = near_o * hyo[k]
-            tye[k] = sye[k]
-            tyo[k] = syo[k]
             for i in range(1, cx - 1):
-                tye[k, i, pl.ds(col_e - tile_e, 1), :] += dye[k, i : i + 1, :]
-                tyo[k, i, pl.ds(col_o - tile_o, 1), :] += dyo[k, i : i + 1, :]
+                add_e = jnp.broadcast_to(dye[k, i : i + 1, :], (8, 128))
+                add_o = jnp.broadcast_to(dyo[k, i : i + 1, :], (8, 128))
+                tye[k, i] = sye[k, i] + jnp.where(here == col_e - tile_e, add_e, 0.0)
+                tyo[k, i] = syo[k, i] + jnp.where(here == col_o - tile_o, add_o, 0.0)
         copies = [
             pltpu.make_async_copy(
                 strip.at[:, pl.ds(1, cx - 2)],

time: 41.4 us -> 41.4 us (level)
  no operation moved by 1% of the time
where the time goes in v5:
time: 41.4 us; the launch traced here: 41 us
  starting transfers between devices  18.9 us (46%)
  Pallas kernels  13 us (31%)
  waiting for transfers between devices  9.07 us (22%)
    ppermute x8, starting transfers between devices, exchange(): lax.ppermute(e, ('gx', 'gy'), pairs)  14.1 us
    all_to_all x1, waiting for transfers between devices, shards(): lax.all_to_all(blocks, 'gx', split_axis=0, concat_axis=0, tiled=True)  5.8 us
    all_to_all x1, starting transfers between devices, shards(): lax.all_to_all(blocks, 'gx', split_axis=0, concat_axis=0, tiled=True)  4.79 us
    pallas_call x1, Pallas kernels, shards(): fourth(*pinned(adjoint, velocity, diffusivity, concentration, line, heigh...  4.42 us
    ppermute x8, waiting for transfers between devices, exchange(): lax.ppermute(e, ('gx', 'gy'), pairs)  3.27 us
    pallas_call x1, Pallas kernels, shards(): second(conc, counts, *pinned(velocity, diffusivity, heights, src, weight))  2.52 us
    pallas_call x1, Pallas kernels, shards(): out, *strips = sixth(*pinned(last), coefs, wall, arrived, hot)  2.28 us
    pallas_call x1, Pallas kernels, shards(): first(*pinned(flat, velocity, diffusivity, concentration, line))  1.61 us
  transfers between devices with their start and end apart: 9, of which 3 were waited for; matrix products, arithmetic and copies ran while one was open for 0% of the time, Pallas kernels for 22%

profile of v5, /device:TPU:10, one launch (start us, length us, event | category | flops | bytes accessed | tf_op | source)
XLA Modules:
  0.0 41.0 jit_solution(17659403889792199140)
XLA Ops:
  0.0 1.6 %first.1 = (f32[512,128]{1,0:T(8,128)S(1)}, f32[512,128]{1,0:T(8,128)S(1)}, f32[7,32,128]{2,1,0:T(8,128)S(1)}, f32[7,32,128]{2,1,0:T(8,128)S(1)}, f32[7,16,128]{2,1,0:T(8,128)S(1)}, /*index=5*/f32[7,16,128]{2,1,0:T(8,128)S(1)}) custom-call(f32[4,512,128]{2,1,0:T(8,128)} %bitcast.5, bf16[3,16,32,128]{3,2,1,0:T(8,128)(2,1)} %vel_hbm.5, ...), custom_call_target="tpu_custom_call" | custom-call | flops 4194304 | bytes 4194304 | tf_op jit(solution)/shard_map/first/pallas_call | solution.py:626
  1.6 2.0 %collective-permute-start = (f32[7,32,128]{2,1,0:T(8,128)S(1)}, f32[7,32,128]{2,1,0:T(8,128)S(1)}, u32[]{:S(2)}, u32[]{:S(2)}) collective-permute-start(f32[7,32,128]{2,1,0:T(8,128)S(1)} %get-tuple-element.40.oxe), channel_id=1, source_target_pairs={{0,16},{1,17},{2,18},{3,19},{4,20},{5,21},{6,22},{7,23},{8,24},{9,... | collective-permute-start | bytes 344072 | tf_op jit(solution)/shard_map/ppermute | solution.py:615
  3.6 4.8 %collective-permute-start.1 = (f32[7,32,128]{2,1,0:T(8,128)S(1)}, f32[7,32,128]{2,1,0:T(8,128)S(1)}, u32[]{:S(2)}, u32[]{:S(2)}) collective-permute-start(f32[7,32,128]{2,1,0:T(8,128)S(1)} %get-tuple-element.41.oxo), channel_id=1, source_target_pairs={{0,1},{1,0},{2,3},{3,2},{4,5},{5,4},{6,7},{7,6},{8,9},{9,8},{10,11... | collective-permute-start | bytes 344072 | tf_op jit(solution)/shard_map/ppermute | solution.py:615
  8.5 1.4 %collective-permute-start.2 = (f32[7,16,128]{2,1,0:T(8,128)S(1)}, f32[7,16,128]{2,1,0:T(8,128)S(1)}, u32[]{:S(2)}, u32[]{:S(2)}) collective-permute-start(f32[7,16,128]{2,1,0:T(8,128)S(1)} %get-tuple-element.42.oyo), channel_id=1, source_target_pairs={{0,16},{1,2},{2,1},{3,4},{4,3},{5,6},{6,5},{7,8},{8,7},{9,10},{10,... | collective-permute-start | bytes 172040 | tf_op jit(solution)/shard_map/ppermute | solution.py:615
  9.9 1.3 %collective-permute-start.3 = (f32[7,16,128]{2,1,0:T(8,128)S(1)}, f32[7,16,128]{2,1,0:T(8,128)S(1)}, u32[]{:S(2)}, u32[]{:S(2)}) collective-permute-start(f32[7,16,128]{2,1,0:T(8,128)S(1)} %get-tuple-element.43.oye), channel_id=1, source_target_pairs={{0,1},{1,0},{2,3},{3,2},{4,5},{5,4},{6,7},{7,6},{8,9},{9,8},{10,11... | collective-permute-start | bytes 172040 | tf_op jit(solution)/shard_map/ppermute | solution.py:615
  11.2 2.5 %second.1 = (f32[256,128]{1,0:T(8,128)S(1)}, f32[256,128]{1,0:T(8,128)S(1)}, bf16[256,128]{1,0:T(8,128)(2,1)S(1)}, f32[256,128]{1,0:T(8,128)S(1)}, f32[32,128]{1...) custom-call(f32[512,128]{1,0:T(8,128)S(1)} %get-tuple-element.46.conc_ref, ...), custom_call_target="tpu_custom_call" | custom-call | flops 8388608 | bytes 8388608 | tf_op jit(solution)/shard_map/second/pallas_call | solution.py:628
  13.7 0.8 %collective-permute-done.2.hyo = f32[7,16,128]{2,1,0:T(8,128)S(1)} collective-permute-done((f32[7,16,128]{2,1,0:T(8,128)S(1)}, f32[7,16,128]{2,1,0:T(8,128)S(1)}, u32[]{:S(2)}, u32[]{:S(2)}) %collective-permute-start.2) | collective-permute-done | bytes 57376 | tf_op jit(solution)/shard_map/ppermute | solution.py:615
  14.5 0.0 collective-permute-done.3.hye
  14.5 0.0 collective-permute-done.hxe
  14.5 0.0 collective-permute-done.1.hxo
  14.5 0.9 %third.1 = f32[16,32,128]{2,1,0:T(8,128)} custom-call(f32[7,32,128]{2,1,0:T(8,128)S(1)} %collective-permute-done.hxe, f32[7,32,128]{2,1,0:T(8,128)S(1)} %collective-permute-done.1.hxo, f32[7,16,128]{2,1,0:T(8,128)S(1)} %collective-permute-done.2.hyo, f32[7,16,128]{2,1,0:T(8,128)S(1)} %collective-permute-done.3.hye, f32[7,32,128]{2,1,0:T(8,128)S(1)} %get-tuple-element.40.oxe, ...), custom_call_target="tpu_custom_call" | custom-call | flops 2097152 | bytes 2097152 | tf_op jit(solution)/shard_map/third/pallas_call | solution.py:631
  15.4 4.8 %all-to-all-start = ((f32[16,32,128]{2,1,0:T(8,128)}), f32[16,32,128]{2,1,0:T(8,128)S(1)}, u32[]{:S(2)}, u32[]{:S(2)}) async-start(f32[16,32,128]{2,1,0:T(8,128)} %third.1), calls=%async_computation | async-start | bytes 524288 | tf_op jit(solution)/shard_map/all_to_all | solution.py:632
  20.2 4.4 %fourth.1 = (f32[4,16,32,128]{3,2,1,0:T(8,128)}, f32[7,512,128]{2,1,0:T(8,128)S(1)}, bf16[512,256]{1,0:T(8,128)(2,1)S(1)}, f32[4,32,128]{2,1,0:T(8,128)S(1)}, f3...) custom-call(f32[4,16,32,128]{3,2,1,0:T(8,128)} %adj_hbm.1, ...), custom_call_target="tpu_custom_call" | custom-call | flops 10485760 | bytes 10485760 | tf_op jit(solution)/shard_map/fourth/pallas_call | solution.py:633
  24.6 5.8 %all-to-all-done.arrived_ref = f32[16,32,128]{2,1,0:T(8,128)S(1)} async-done(((f32[16,32,128]{2,1,0:T(8,128)}), f32[16,32,128]{2,1,0:T(8,128)S(1)}, u32[]{:S(2)}, u32[]{:S(2)}) %all-to-all-start) | async-done | bytes 262176 | tf_op jit(solution)/shard_map/all_to_all | solution.py:632
  30.4 0.3 fifth.1
  30.7 2.3 %collective-permute-start.4 = (f32[4,32,128]{2,1,0:T(8,128)S(1)}, f32[4,32,128]{2,1,0:T(8,128)S(1)}, u32[]{:S(2)}, u32[]{:S(2)}) collective-permute-start(f32[4,32,128]{2,1,0:T(8,128)S(1)} %get-tuple-element.67), channel_id=1, source_target_pairs={{0,16},{1,17},{2,18},{3,19},{4,20},{5,21},{6,22},{7,23},{8,24},{9,... | collective-permute-start | bytes 196616 | tf_op jit(solution)/shard_map/ppermute | solution.py:615
  33.1 1.3 %collective-permute-start.5 = (f32[4,32,128]{2,1,0:T(8,128)S(1)}, f32[4,32,128]{2,1,0:T(8,128)S(1)}, u32[]{:S(2)}, u32[]{:S(2)}) collective-permute-start(f32[4,32,128]{2,1,0:T(8,128)S(1)} %get-tuple-element.68), channel_id=1, source_target_pairs={{0,1},{1,0},{2,3},{3,2},{4,5},{5,4},{6,7},{7,6},{8,9},{9,8},{10,11... | collective-permute-start | bytes 196616 | tf_op jit(solution)/shard_map/ppermute | solution.py:615
  34.3 0.0 collective-permute-start.6
  34.3 1.0 %collective-permute-start.7 = (f32[4,16,128]{2,1,0:T(8,128)S(1)}, f32[4,16,128]{2,1,0:T(8,128)S(1)}, u32[]{:S(2)}, u32[]{:S(2)}) collective-permute-start(f32[4,16,128]{2,1,0:T(8,128)S(1)} %get-tuple-element.70), channel_id=1, source_target_pairs={{0,1},{1,0},{2,3},{3,2},{4,5},{5,4},{6,7},{7,6},{8,9},{9,8},{10,11... | collective-permute-start | bytes 98312 | tf_op jit(solution)/shard_map/ppermute | solution.py:615
  35.3 2.3 %sixth.1 = (f32[4,16,32,128]{3,2,1,0:T(8,128)}, f32[4,32,128]{2,1,0:T(8,128)S(1)}, f32[4,32,128]{2,1,0:T(8,128)S(1)}, f32[4,16,8,128]{3,2,1,0:T(8,128)S(1)}, f32[4,16,8,128]{3,2,1,0:T(8,128)S(1)}) custom-call(f32[4,16,32,128]{3,2,1,0:T(8,128)} %get-tuple-element.44.last_hbm, ...), custom_call_target="tpu_custom_call", output_to_operand_aliasing={{0}: (0, {})} | custom-call | flops 5242880 | bytes 5242880 | tf_op jit(solution)/shard_map/sixth/pallas_call | solution.py:639
  37.6 2.5 %collective-permute-done.6.hyo = f32[4,16,128]{2,1,0:T(8,128)S(1)} collective-permute-done((f32[4,16,128]{2,1,0:T(8,128)S(1)}, f32[4,16,128]{2,1,0:T(8,128)S(1)}, u32[]{:S(2)}, u32[]{:S(2)}) %collective-permute-start.6) | collective-permute-done | bytes 32800 | tf_op jit(solution)/shard_map/ppermute | solution.py:615
  40.1 0.0 collective-permute-done.7.hye
  40.1 0.0 collective-permute-done.4.hxe
  40.1 0.0 collective-permute-done.5.hxo
  40.1 0.9 %seventh.1 = f32[4,16,32,128]{3,2,1,0:T(8,128)} custom-call(f32[4,16,32,128]{3,2,1,0:T(8,128)} %get-tuple-element.62.last_hbm, f32[4,32,128]{2,1,0:T(8,128)S(1)} %get-tuple-element.63.sxe, f32[4,32,128]{2,1,0:T(8,128)S(1)} %get-tuple-element.64.sxo, f32[4,16,8,128]{3,2,1,0:T(8,128)S(1)} %get-tuple-element.65.sye, ...), custom_call_target="tpu_custom_call", output_to_operand_aliasing={{}: (0, {})} | custom-call | flops 2097152 | bytes 2097152 | tf_op jit(solution)/shard_map/seventh/pallas_call | solution.py:640
Async XLA Ops:
  1.6 12.9 %collective-permute-start = (f32[7,32,128]{2,1,0:T(8,128)S(1)}, f32[7,32,128]{2,1,0:T(8,128)S(1)}, u32[]{:S(2)}, u32[]{:S(2)}) collective-permute-start(f32[7,32,128]{2,1,0:T(8,128)S(1)} %get-tuple-element.40.oxe), channel_id=1, source_target_pairs={{0,16},{1,17},{2,18},{3,19},{4,20},{5,21},{6,22},{7,23},{8,24},{9,... | collective-permute-start | bytes 344072 | tf_op jit(solution)/shard_map/ppermute | solution.py:615
  3.6 10.8 %collective-permute-start.1 = (f32[7,32,128]{2,1,0:T(8,128)S(1)}, f32[7,32,128]{2,1,0:T(8,128)S(1)}, u32[]{:S(2)}, u32[]{:S(2)}) collective-permute-start(f32[7,32,128]{2,1,0:T(8,128)S(1)} %get-tuple-element.41.oxo), channel_id=1, source_target_pairs={{0,1},{1,0},{2,3},{3,2},{4,5},{5,4},{6,7},{7,6},{8,9},{9,8},{10,11... | collective-permute-start | bytes 344072 | tf_op jit(solution)/shard_map/ppermute | solution.py:615
  8.5 6.0 %collective-permute-start.2 = (f32[7,16,128]{2,1,0:T(8,128)S(1)}, f32[7,16,128]{2,1,0:T(8,128)S(1)}, u32[]{:S(2)}, u32[]{:S(2)}) collective-permute-start(f32[7,16,128]{2,1,0:T(8,128)S(1)} %get-tuple-element.42.oyo), channel_id=1, source_target_pairs={{0,16},{1,2},{2,1},{3,4},{4,3},{5,6},{6,5},{7,8},{8,7},{9,10},{10,... | collective-permute-start | bytes 172040 | tf_op jit(solution)/shard_map/ppermute | solution.py:615
  9.9 4.6 %collective-permute-start.3 = (f32[7,16,128]{2,1,0:T(8,128)S(1)}, f32[7,16,128]{2,1,0:T(8,128)S(1)}, u32[]{:S(2)}, u32[]{:S(2)}) collective-permute-start(f32[7,16,128]{2,1,0:T(8,128)S(1)} %get-tuple-element.43.oye), channel_id=1, source_target_pairs={{0,1},{1,0},{2,3},{3,2},{4,5},{5,4},{6,7},{7,6},{8,9},{9,8},{10,11... | collective-permute-start | bytes 172040 | tf_op jit(solution)/shard_map/ppermute | solution.py:615
  15.4 15.0 %all-to-all-start = ((f32[16,32,128]{2,1,0:T(8,128)}), f32[16,32,128]{2,1,0:T(8,128)S(1)}, u32[]{:S(2)}, u32[]{:S(2)}) async-start(f32[16,32,128]{2,1,0:T(8,128)} %third.1), calls=%async_computation | async-start | bytes 524288 | tf_op jit(solution)/shard_map/all_to_all | solution.py:632
  30.7 9.3 %collective-permute-start.4 = (f32[4,32,128]{2,1,0:T(8,128)S(1)}, f32[4,32,128]{2,1,0:T(8,128)S(1)}, u32[]{:S(2)}, u32[]{:S(2)}) collective-permute-start(f32[4,32,128]{2,1,0:T(8,128)S(1)} %get-tuple-element.67), channel_id=1, source_target_pairs={{0,16},{1,17},{2,18},{3,19},{4,20},{5,21},{6,22},{7,23},{8,24},{9,... | collective-permute-start | bytes 196616 | tf_op jit(solution)/shard_map/ppermute | solution.py:615
  33.1 7.0 %collective-permute-start.5 = (f32[4,32,128]{2,1,0:T(8,128)S(1)}, f32[4,32,128]{2,1,0:T(8,128)S(1)}, u32[]{:S(2)}, u32[]{:S(2)}) collective-permute-start(f32[4,32,128]{2,1,0:T(8,128)S(1)} %get-tuple-element.68), channel_id=1, source_target_pairs={{0,1},{1,0},{2,3},{3,2},{4,5},{5,4},{6,7},{7,6},{8,9},{9,8},{10,11... | collective-permute-start | bytes 196616 | tf_op jit(solution)/shard_map/ppermute | solution.py:615
  34.3 5.7 %collective-permute-start.6 = (f32[4,16,128]{2,1,0:T(8,128)S(1)}, f32[4,16,128]{2,1,0:T(8,128)S(1)}, u32[]{:S(2)}, u32[]{:S(2)}) collective-permute-start(f32[4,16,128]{2,1,0:T(8,128)S(1)} %get-tuple-element.69), channel_id=1, source_target_pairs={{0,16},{1,2},{2,1},{3,4},{4,3},{5,6},{6,5},{7,8},{8,7},{9,10},{10,... | collective-permute-start | bytes 98312 | tf_op jit(solution)/shard_map/ppermute | solution.py:615
  34.3 5.7 %collective-permute-start.7 = (f32[4,16,128]{2,1,0:T(8,128)S(1)}, f32[4,16,128]{2,1,0:T(8,128)S(1)}, u32[]{:S(2)}, u32[]{:S(2)}) collective-permute-start(f32[4,16,128]{2,1,0:T(8,128)S(1)} %get-tuple-element.70), channel_id=1, source_target_pairs={{0,1},{1,0},{2,3},{3,2},{4,5},{5,4},{6,7},{7,6},{8,9},{9,8},{10,11... | collective-permute-start | bytes 98312 | tf_op jit(solution)/shard_map/ppermute | solution.py:615
